TPU v7x, 32 devices: a whole 2x2x4 slice. The times are simulated.
32 devices in a mesh: ctx: 8 (over z, y), fsdp: 4 (over x, core).
Axes of the slice: x: 2, y: 2, z: 4, core: 2. Of those that a mesh axis runs over, the one named last changes fastest.
Arguments:
- tokens: bfloat16 [4, 1024, 768], P('fsdp', 'ctx'), may hold values from -6 to 6
- first_gain: bfloat16 [768], P('fsdp'), may hold values from 0.5 to 1.5
- first_bias: bfloat16 [768], P('fsdp'), may hold values from -4 to 4
- attn_weight: bfloat16 [768, 2304], P('fsdp'), may hold values from -0.3125 to 0.3125
- query_bias: bfloat16 [768], P('fsdp'), may hold values from -4 to 4
- value_bias: bfloat16 [768], P('fsdp'), may hold values from -4 to 4
- proj_weight: bfloat16 [768, 768], P('fsdp'), may hold values from -6 to 6
- proj_bias: bfloat16 [768], P('fsdp'), may hold values from -6 to 6
- second_gain: bfloat16 [768], P('fsdp'), may hold values from 0.5 to 1.5
- second_bias: bfloat16 [768], P('fsdp'), may hold values from -4 to 4
- fc_weight: bfloat16 [768, 3072], P('fsdp'), may hold values from -0.21875 to 0.21875
- fc_bias: bfloat16 [3072], P('fsdp'), may hold values from -6 to 6
- out_weight: bfloat16 [3072, 768], P('fsdp'), may hold values from -0.3125 to 0.3125
- out_bias: bfloat16 [768], P('fsdp'), may hold values from -6 to 6
- cotangent: bfloat16 [4, 1024, 768], P('fsdp', 'ctx'), may hold values from -6 to 6
Outputs:
- block_out: bfloat16 [4, 1024, 768], P('fsdp', 'ctx')
- input_grad: bfloat16 [4, 1024, 768], P('fsdp', 'ctx')
- first_gain_grad: float32 [768], P('fsdp')
- first_bias_grad: float32 [768], P('fsdp')
- attn_weight_grad: float32 [768, 2304], P('fsdp')
- query_bias_grad: float32 [768], P('fsdp')
- value_bias_grad: float32 [768], P('fsdp')
- proj_weight_grad: float32 [768, 768], P('fsdp')
- proj_bias_grad: float32 [768], P('fsdp')
- second_gain_grad: float32 [768], P('fsdp')
- second_bias_grad: float32 [768], P('fsdp')
- fc_weight_grad: float32 [768, 3072], P('fsdp')
- fc_bias_grad: float32 [3072], P('fsdp')
- out_weight_grad: float32 [3072, 768], P('fsdp')
- out_bias_grad: float32 [768], P('fsdp')
All inputs are finite; a program needn't handle non-finite values.
Results may differ from a plain program's by a relative error of at most 0.017.
Values may be sent and summed in bfloat16 or wider, within the bound.
No kernel may reach another device: no remote copies, remote signals or barrier semaphores. Data moves between devices by JAX's collectives and lax.ppermute only.
A program may use at most 320 MiB of HBM per device.

v0:
```python
from functools import partial

import jax
import jax.numpy as jnp
from jax import lax
from jax.sharding import PartitionSpec as P

D = 768
H = 12
HD = 64
LAYERS = 12


EPSILON = 1e-05


def layer_norm(values_in, norm_gain, norm_shift):
    center = jnp.mean(values_in, axis=-1, keepdims=True)
    centered = values_in - center
    spread = jnp.mean(centered * centered, axis=-1, keepdims=True)
    return centered * lax.rsqrt(spread + EPSILON) * norm_gain + norm_shift


def left_product(first, second):
    return lax.dot_general(
        first, second, (((0,), (0,)), ((), ())), preferred_element_type=jnp.float32
    )


def right_product(first, second):
    return lax.dot_general(
        first, second, (((1,), (1,)), ((), ())), preferred_element_type=jnp.float32
    )


def score_block(query_rows, key_rows, query_offset, key_offset):
    scores = jnp.einsum(
        "sqhd,skhd->shqk", query_rows, key_rows, preferred_element_type=jnp.float32
    ) * HD ** (-0.5)
    query_index = query_offset + lax.broadcasted_iota(jnp.int32, (query_rows.shape[1], 1), 0)
    key_index = key_offset + lax.broadcasted_iota(jnp.int32, (1, key_rows.shape[1]), 1)
    return (scores, (key_index <= query_index)[None, None])


def pair_terms(
    query_rows, grad_rows, log_totals, deltas, key_rows, value_rows, query_offset, key_offset
):
    scores, visible = score_block(query_rows, key_rows, query_offset, key_offset)
    weights = jnp.where(visible, jnp.exp(scores - log_totals[..., None]), 0.0)
    grad_weights = jnp.einsum(
        "sqhd,skhd->shqk", grad_rows, value_rows, preferred_element_type=jnp.float32
    )
    grad_scores = (weights * (grad_weights - deltas[..., None])).astype(jnp.bfloat16)
    return (weights.astype(jnp.bfloat16), grad_scores)


def shards(
    tokens,
    first_gain,
    first_bias,
    attn_weight,
    query_bias,
    value_bias,
    proj_weight,
    proj_bias,
    second_gain,
    second_bias,
    fc_weight,
    fc_bias,
    out_weight,
    out_bias,
    cotangent,
):
    residual_scale = LAYERS ** (-0.5)
    score_scale = HD ** (-0.5)
    seq_count = tokens.shape[0]
    block_rows = tokens.shape[1]
    all_rows = seq_count * block_rows
    inputs = tokens.reshape(all_rows, D).astype(jnp.float32)
    ctx_index = lax.axis_index("ctx")
    my_offset = ctx_index * block_rows
    last_row = my_offset + block_rows - 1
    attn_gathered = (
        lax.all_gather(first_gain, "fsdp", axis=0, tiled=True),
        lax.all_gather(first_bias, "fsdp", axis=0, tiled=True),
        lax.all_gather(attn_weight, "fsdp", axis=0, tiled=True),
        lax.all_gather(query_bias, "fsdp", axis=0, tiled=True),
        lax.all_gather(value_bias, "fsdp", axis=0, tiled=True),
        lax.all_gather(proj_weight, "fsdp", axis=0, tiled=True),
        lax.all_gather(proj_bias, "fsdp", axis=0, tiled=True),
    )
    gain_one, shift_one, attn_matrix, query_shift, value_shift, proj_matrix, proj_shift = (
        attn_gathered
    )
    gain_one = gain_one.astype(jnp.float32)
    shift_one = shift_one.astype(jnp.float32)
    normed = layer_norm(inputs, gain_one, shift_one).astype(jnp.bfloat16)
    mixed_rows = jnp.dot(normed, attn_matrix, preferred_element_type=jnp.float32)
    query_flat = (
        (mixed_rows[:, :D] + query_shift.astype(jnp.float32))
        .astype(jnp.bfloat16)
        .reshape(seq_count, block_rows, D)
    )
    key_flat = mixed_rows[:, D : 2 * D].astype(jnp.bfloat16).reshape(seq_count, block_rows, D)
    value_flat = (
        (mixed_rows[:, 2 * D :] + value_shift.astype(jnp.float32))
        .astype(jnp.bfloat16)
        .reshape(seq_count, block_rows, D)
    )
    query_heads = query_flat.reshape(seq_count, block_rows, H, HD)
    start_state = (
        jnp.full((seq_count, H, block_rows), -1e30, jnp.float32),
        jnp.zeros((seq_count, H, block_rows), jnp.float32),
        jnp.zeros((seq_count, H, block_rows, HD), jnp.float32),
    )
    offset = jnp.int32(0)
    key_rows = lax.all_gather(key_flat, "ctx", axis=1, tiled=True)
    value_rows = lax.all_gather(value_flat, "ctx", axis=1, tiled=True)
    row_count = key_rows.shape[1]

    def update(running):
        running_max, running_sum, running_acc = running
        scores, visible = score_block(
            query_heads, key_rows.reshape(seq_count, row_count, H, HD), my_offset, offset
        )
        scores = jnp.where(visible, scores, -1e30)
        new_max = jnp.maximum(running_max, jnp.max(scores, axis=-1))
        weights = jnp.where(visible, jnp.exp(scores - new_max[..., None]), 0.0)
        running_acc = jnp.einsum(
            "shqk,skhd->shqd",
            weights.astype(jnp.bfloat16),
            value_rows.reshape(seq_count, row_count, H, HD),
            preferred_element_type=jnp.float32,
        )
        running_sum = jnp.sum(weights, axis=-1)
        return (new_max, running_sum, running_acc)

    final_max, final_sum, final_acc = lax.cond(
        offset <= last_row, update, lambda unchanged: unchanged, start_state
    )
    log_totals = final_max + jnp.log(final_sum)
    attended_heads = final_acc / final_sum[..., None]
    attended_exact = attended_heads.transpose(0, 2, 1, 3).reshape(all_rows, D)
    attended = attended_exact.astype(jnp.bfloat16)
    branch = jnp.dot(attended, proj_matrix, preferred_element_type=jnp.float32) + proj_shift.astype(
        jnp.float32
    )
    middle = inputs + residual_scale * branch
    mlp_gathered = (
        lax.all_gather(second_gain, "fsdp", axis=0, tiled=True),
        lax.all_gather(second_bias, "fsdp", axis=0, tiled=True),
        lax.all_gather(fc_weight, "fsdp", axis=0, tiled=True),
        lax.all_gather(fc_bias, "fsdp", axis=0, tiled=True),
        lax.all_gather(out_weight, "fsdp", axis=0, tiled=True),
        lax.all_gather(out_bias, "fsdp", axis=0, tiled=True),
    )
    gain_two, shift_two, fc_matrix, fc_shift, out_matrix, out_shift = mlp_gathered
    gain_two = gain_two.astype(jnp.float32)
    shift_two = shift_two.astype(jnp.float32)
    normed_two = layer_norm(middle, gain_two, shift_two).astype(jnp.bfloat16)
    hidden = jnp.dot(normed_two, fc_matrix, preferred_element_type=jnp.float32) + fc_shift.astype(
        jnp.float32
    )
    gelu_fn = partial(jax.nn.gelu, approximate=True)
    active_exact, gelu_back = jax.vjp(gelu_fn, hidden)
    active = active_exact.astype(jnp.bfloat16)
    output = jnp.dot(active, out_matrix, preferred_element_type=jnp.float32) + out_shift.astype(
        jnp.float32
    )
    block_out = (middle + residual_scale * output).astype(jnp.bfloat16)
    grad_rows = cotangent.reshape(all_rows, D).astype(jnp.float32)
    grad_output = (residual_scale * grad_rows).astype(jnp.bfloat16)
    out_weight_grad = left_product(active, grad_output)
    out_bias_grad = jnp.sum(grad_output.astype(jnp.float32), axis=0)
    grad_active = right_product(grad_output, out_matrix)
    grad_hidden = gelu_back(grad_active)[0].astype(jnp.bfloat16)
    fc_weight_grad = left_product(normed_two, grad_hidden)
    fc_bias_grad = jnp.sum(grad_hidden.astype(jnp.float32), axis=0)
    grad_normed_two = right_product(grad_hidden, fc_matrix)
    norm_two_value, norm_two_back = jax.vjp(layer_norm, middle, gain_two, shift_two)
    grad_middle, second_gain_grad, second_bias_grad = norm_two_back(grad_normed_two)
    grad_middle = grad_middle + grad_rows
    grad_branch = (residual_scale * grad_middle).astype(jnp.bfloat16)
    proj_weight_grad = left_product(attended, grad_branch)
    proj_bias_grad = jnp.sum(grad_branch.astype(jnp.float32), axis=0)
    grad_attended = right_product(grad_branch, proj_matrix).astype(jnp.bfloat16)
    grad_heads = grad_attended.reshape(seq_count, block_rows, H, HD)
    grad_seq = grad_attended.reshape(seq_count, block_rows, D)
    deltas = jnp.sum(grad_heads.astype(jnp.float32).transpose(0, 2, 1, 3) * attended_heads, axis=-1)
    zero_flat = jnp.zeros((seq_count, block_rows, D), jnp.float32)
    zero_heads = jnp.zeros((seq_count, block_rows, H, HD), jnp.float32)
    all_totals, all_deltas = (
        lax.all_gather(log_totals, "ctx", axis=2, tiled=True),
        lax.all_gather(deltas, "ctx", axis=2, tiled=True),
    )
    key_heads_own = key_flat.reshape(seq_count, block_rows, H, HD)
    value_heads_own = value_flat.reshape(seq_count, block_rows, H, HD)

    def key_side(carried, arrived, offset):
        query_rows, grad_piece = arrived
        row_count = query_rows.shape[1]

        def key_visit_block(partials):
            query_part = query_rows.reshape(seq_count, row_count, H, HD)
            grad_part = grad_piece.reshape(seq_count, row_count, H, HD)
            weights, grad_scores = pair_terms(
                query_part,
                grad_part,
                all_totals,
                all_deltas,
                key_heads_own,
                value_heads_own,
                offset,
                my_offset,
            )
            key_sum = score_scale * jnp.einsum(
                "shqk,sqhd->skhd", grad_scores, query_part, preferred_element_type=jnp.float32
            ).reshape(seq_count, block_rows, D)
            value_sum = jnp.einsum(
                "shqk,sqhd->skhd", weights, grad_part, preferred_element_type=jnp.float32
            ).reshape(seq_count, block_rows, D)
            return (key_sum, value_sum)

        return lax.cond(
            offset + row_count - 1 >= my_offset,
            key_visit_block,
            lambda unchanged: unchanged,
            carried,
        )

    key_grad, value_grad = key_side(
        (zero_flat, zero_flat),
        (
            lax.all_gather(query_flat, "ctx", axis=1, tiled=True),
            lax.all_gather(grad_seq, "ctx", axis=1, tiled=True),
        ),
        jnp.int32(0),
    )

    def query_side(carried, arrived, offset):
        key_rows, value_rows = arrived
        row_count = key_rows.shape[1]

        def query_visit_block(query_sum):
            key_part = key_rows.reshape(seq_count, row_count, H, HD)
            weights, grad_scores = pair_terms(
                query_heads,
                grad_heads,
                log_totals,
                deltas,
                key_part,
                value_rows.reshape(seq_count, row_count, H, HD),
                my_offset,
                offset,
            )
            return score_scale * jnp.einsum(
                "shqk,skhd->sqhd", grad_scores, key_part, preferred_element_type=jnp.float32
            )

        return lax.cond(offset <= last_row, query_visit_block, lambda unchanged: unchanged, carried)

    query_grad = query_side(
        zero_heads,
        (
            lax.all_gather(key_flat, "ctx", axis=1, tiled=True),
            lax.all_gather(value_flat, "ctx", axis=1, tiled=True),
        ),
        jnp.int32(0),
    )
    grad_mixed = jnp.concatenate(
        [
            query_grad.reshape(all_rows, D).astype(jnp.bfloat16),
            key_grad.reshape(all_rows, D).astype(jnp.bfloat16),
            value_grad.reshape(all_rows, D).astype(jnp.bfloat16),
        ],
        axis=1,
    )
    attn_weight_grad = left_product(normed, grad_mixed)
    query_bias_grad = jnp.sum(grad_mixed[:, :D].astype(jnp.float32), axis=0)
    value_bias_grad = jnp.sum(grad_mixed[:, 2 * D :].astype(jnp.float32), axis=0)
    grad_normed = right_product(grad_mixed, attn_matrix)
    norm_one_value, norm_one_back = jax.vjp(layer_norm, inputs, gain_one, shift_one)
    grad_inputs, first_gain_grad, first_bias_grad = norm_one_back(grad_normed)
    input_grad = (grad_inputs + grad_middle).astype(jnp.bfloat16)
    owned = (
        lax.psum_scatter(
            first_gain_grad.astype(jnp.bfloat16), "fsdp", scatter_dimension=0, tiled=True
        ).astype(jnp.float32),
        lax.psum_scatter(
            first_bias_grad.astype(jnp.bfloat16), "fsdp", scatter_dimension=0, tiled=True
        ).astype(jnp.float32),
        lax.psum_scatter(
            attn_weight_grad.astype(jnp.bfloat16), "fsdp", scatter_dimension=0, tiled=True
        ).astype(jnp.float32),
        lax.psum_scatter(
            query_bias_grad.astype(jnp.bfloat16), "fsdp", scatter_dimension=0, tiled=True
        ).astype(jnp.float32),
        lax.psum_scatter(
            value_bias_grad.astype(jnp.bfloat16), "fsdp", scatter_dimension=0, tiled=True
        ).astype(jnp.float32),
        lax.psum_scatter(
            proj_weight_grad.astype(jnp.bfloat16), "fsdp", scatter_dimension=0, tiled=True
        ).astype(jnp.float32),
        lax.psum_scatter(
            proj_bias_grad.astype(jnp.bfloat16), "fsdp", scatter_dimension=0, tiled=True
        ).astype(jnp.float32),
        lax.psum_scatter(
            second_gain_grad.astype(jnp.bfloat16), "fsdp", scatter_dimension=0, tiled=True
        ).astype(jnp.float32),
        lax.psum_scatter(
            second_bias_grad.astype(jnp.bfloat16), "fsdp", scatter_dimension=0, tiled=True
        ).astype(jnp.float32),
        lax.psum_scatter(
            fc_weight_grad.astype(jnp.bfloat16), "fsdp", scatter_dimension=0, tiled=True
        ).astype(jnp.float32),
        lax.psum_scatter(
            fc_bias_grad.astype(jnp.bfloat16), "fsdp", scatter_dimension=0, tiled=True
        ).astype(jnp.float32),
        lax.psum_scatter(
            out_weight_grad.astype(jnp.bfloat16), "fsdp", scatter_dimension=0, tiled=True
        ).astype(jnp.float32),
        lax.psum_scatter(
            out_bias_grad.astype(jnp.bfloat16), "fsdp", scatter_dimension=0, tiled=True
        ).astype(jnp.float32),
    )
    summed = lax.psum(
        (
            owned[0],
            owned[1],
            owned[2],
            owned[3],
            owned[4],
            owned[5],
            owned[6],
            owned[7],
            owned[8],
            owned[9],
            owned[10],
            owned[11],
            owned[12],
        ),
        "ctx",
    )
    return (
        block_out.reshape(seq_count, block_rows, D),
        input_grad.reshape(seq_count, block_rows, D),
        summed[0],
        summed[1],
        summed[2],
        summed[3],
        summed[4],
        summed[5],
        summed[6],
        summed[7],
        summed[8],
        summed[9],
        summed[10],
        summed[11],
        summed[12],
    )


def solution(mesh):
    placed = (
        P("fsdp", "ctx", None),
        P("fsdp"),
        P("fsdp"),
        P("fsdp", None),
        P("fsdp"),
        P("fsdp"),
        P("fsdp", None),
        P("fsdp"),
        P("fsdp"),
        P("fsdp"),
        P("fsdp", None),
        P("fsdp"),
        P("fsdp", None),
        P("fsdp"),
        P("fsdp", "ctx", None),
    )
    return jax.shard_map(
        shards,
        mesh=mesh,
        in_specs=placed,
        out_specs=(
            P("fsdp", "ctx", None),
            P("fsdp", "ctx", None),
            P("fsdp"),
            P("fsdp"),
            P("fsdp", None),
            P("fsdp"),
            P("fsdp"),
            P("fsdp", None),
            P("fsdp"),
            P("fsdp"),
            P("fsdp"),
            P("fsdp", None),
            P("fsdp"),
            P("fsdp", None),
            P("fsdp"),
        ),
        check_vma=False,
    )
```

profile of v0, /device:TPU:0, one launch (start us, length us, event | category | flops | bytes accessed | tf_op | source)
XLA Modules:
  0.0 782.9 jit_solution(8197349530382373933)
XLA Ops:
  15.8 13.4 %all-reduce.19 = (bf16[768]{0:T(1024)(128)(2,1)S(1)}, bf16[768]{0:T(1024)(128)(2,1)S(1)}, bf16[768]{0:T(1024)(128)(2,1)S(1)}, bf16[768]{0:T(1024)(128)(2,1)S(1)}...) all-reduce(bf16[768]{0:T(1024)(128)(2,1)S(1)} %dynamic-update-slice, ...), channel_id=1, replica_groups=mesh['ctx'=8,'fsdp'=4] {'fsdp'}, use_global_device_ids=true, to_apply=%add.1 | all-reduce | flops 5376 | bytes 21504
  31.4 11.8 %all-gather.15.cloned.1.call-done = bf16[768,2304]{1,0:T(8,128)(2,1)} async-done(((bf16[192,2304]{1,0:T(8,128)(2,1)}), bf16[768,2304]{1,0:T(8,128)(2,1)}) %all-gather.15.cloned.1.call-update) | async-done | bytes 3538960 | tf_op jit(solution)/shard_map/all_gather | solution.py:86
  49.5 5.2 all-gather.5
  55.7 35.5 %all-gather.25.cloned.1.call-done = bf16[1024,768]{1,0:T(8,128)(2,1)} async-done(((bf16[128,768]{1,0:T(8,128)(2,1)}), bf16[1024,768]{1,0:T(8,128)(2,1)}) %all-gather.25.cloned.1.call-update) | async-done | bytes 1572880 | tf_op jit(solution)/shard_map/all_gather | solution.py:118
  91.3 45.8 %all-gather.23.cloned.1.call-done = bf16[1024,768]{1,0:T(8,128)(2,1)} async-done(((bf16[128,768]{1,0:T(8,128)(2,1)}), bf16[1024,768]{1,0:T(8,128)(2,1)}) %all-gather.23.cloned.1.call-update) | async-done | bytes 1572880 | tf_op jit(solution)/shard_map/all_gather | solution.py:117
  137.1 13.5 %conditional.3 = (f32[1,12,128]{2,1,0:T(8,128)S(1)}, f32[1,12,128,64]{2,3,1,0:T(8,128)S(1)}, f32[1,12,128]{2,1,0:T(8,128)S(1)}) conditional(s32[]{:T(128)} %convert_element_type.215, () %tuple.32, (s32[]{:T(128)}, bf16[1,128,12,64]{1,3,2,0:T(8,128)(2,1)}, bf16[1,1024,768]{2,1,0:T(8,128)(2,1)}, bf16[1,1024,768]{2,1,0:T(8,128)(2,1)}) %tuple.106), branch_computations={%region_2.0_spmd.clone, %region_3.6_spmd.clone} | conditional | flops 423233152 | bytes 60988556 | solution.py:138
  145.6 4.9 fusion.32
  156.7 36.9 %all-gather.19.cloned.1.call-done = bf16[768,3072]{1,0:T(8,128)(2,1)} async-done(((bf16[192,3072]{1,0:T(8,128)(2,1)}), bf16[768,3072]{1,0:T(8,128)(2,1)}) %all-gather.19.cloned.1.call-update) | async-done | bytes 4718608 | tf_op jit(solution)/shard_map/all_gather | solution.py:152
  196.9 35.7 %all-gather.21.cloned.1.call-done = bf16[3072,768]{1,0:T(8,128)(2,1)} async-done(((bf16[768,768]{1,0:T(8,128)(2,1)}), bf16[3072,768]{1,0:T(8,128)(2,1)}) %all-gather.21.cloned.1.call-update) | async-done | bytes 4718608 | tf_op jit(solution)/shard_map/all_gather | solution.py:154
  232.6 5.0 fusion.93
  244.4 4.9 convolution_convert_fusion.1
  255.2 17.2 %conditional.4 = (bf16[1,128,12,64]{1,3,2,0:T(8,128)(2,1)S(1)}) conditional(s32[]{:T(128)} %convert_element_type.215, () %tuple.34, (s32[]{:T(128)}, bf16[1,128,12,64]{1,3,2,0:T(8,128)(2,1)}, bf16[1,1024,768]{2,1,0:T(8,128)(2,1)}, f32[1,12,128]{2,1,0:T(8,128)}, bf16[1,128,12,64]{1,3,2,0:T(8,128)(2,1)}, /*index=5*/bf16[1,1024,768]{2,1,0:T(8,128)(2,1)}, ...), branch_computations={%region_11.12_spmd, %region_12.13_spmd} | conditional | flops 613744768 | bytes 25269316 | solution.py:260
  257.8 5.2 fusion.8
  265.8 6.6 fusion.5
  272.4 32.5 %all-gather.4 = f32[12,1024]{1,0:T(8,128)} all-gather(f32[12,128]{1,0:T(8,128)S(1)} %fusion.68), channel_id=6, replica_groups=mesh['ctx'=8,'fsdp'=4] {'ctx'}, dimensions={1}, use_global_device_ids=true | all-gather | bytes 55296 | tf_op jit(solution)/shard_map/all_gather | solution.py:194
  304.9 33.0 %all_gather.75 = f32[1,12,1024]{2,1,0:T(8,128)} all-gather(f32[1,12,128]{2,1,0:T(8,128)} %copy-done.22), channel_id=1, replica_groups=mesh['ctx'=8,'fsdp'=4] {'ctx'}, dimensions={2}, use_global_device_ids=true | all-gather | bytes 55296 | tf_op jit(solution)/shard_map/all_gather | solution.py:193
  338.0 23.5 %conditional.5 = (bf16[1,128,768]{1,2,0:T(8,128)(2,1)S(1)}, bf16[128,768]{0,1:T(8,128)(2,1)S(1)}) conditional(s32[]{:T(128)} %convert_element_type.242, () %tuple.36, (s32[]{:T(128)}, bf16[1,1024,768]{2,1,0:T(8,128)(2,1)}, bf16[128,768]{1,0:T(8,128)(2,1)S(1)}, f32[1,12,1024]{2,1,0:T(8,128)}, bf16[1,1024,768]{2,1,0:T(8,128)(2,1)}, ...), branch_computations={%region_13.14_spmd, %region_14.15_spmd} | conditional | flops 821362816 | bytes 33965132 | solution.py:224
  340.7 5.1 fusion.94
  348.7 8.3 %fusion.21 = bf16[12,128,64]{1,2,0:T(8,128)(2,1)S(1)} fusion(bf16[1024,12,64]{0,2,1:T(8,128)(2,1)} %bitcast.164, f32[12,1024,128]{2,1,0:T(8,128)} %fusion.94, f32[12,1024]{1,0:T(8,128)S(1)} %bitcast.189, f32[12,1024]{1,0:T(8,128)} %bitcast.190, pred[1024,128]{1,0:T(8,128)(4,1)S(1)} %iota_compare_fusion.1, bf16[1024,12,64]{0,2,1:T(8,128)(2,1)} %bitcast.176, ...), kind=kOutput, calls=%fused_computation.22 | convolution fusion | flops 412286976 | bytes 10059776 | tf_op jit(solution)/shard_map/cond/branch_1_fun/shqk,sqhd->skhd/dot_general | solution.py:216
  374.1 12.4 %all-reduce.18 = (bf16[768]{0:T(1024)(128)(2,1)S(1)}, bf16[768]{0:T(1024)(128)(2,1)S(1)}, bf16[768]{0:T(1024)(128)(2,1)S(1)}, bf16[768]{0:T(1024)(128)(2,1)S(1)}...) all-reduce(bf16[768]{0:T(1024)(128)(2,1)} %dynamic-update-slice.7, ...), channel_id=1, replica_groups=mesh['ctx'=8,'fsdp'=4] {'fsdp'}, use_global_device_ids=true, to_apply=%add.7 | all-reduce | flops 9984 | bytes 39936
  392.6 10.9 %reduce-scatter.9.cloned.1.call-done = bf16[192,3072]{1,0:T(8,128)(2,1)} async-done(((bf16[768,3072]{1,0:T(8,128)(2,1)}), bf16[192,3072]{1,0:T(8,128)(2,1)}) %reduce-scatter.9.cloned.1.call-update) | async-done | bytes 1179664 | tf_op jit(solution)/shard_map/reduce_scatter | solution.py:313
  403.5 50.4 %reduce-scatter.11.cloned.1.call-done = bf16[768,768]{1,0:T(8,128)(2,1)} async-done(((bf16[3072,768]{1,0:T(8,128)(2,1)}), bf16[768,768]{1,0:T(8,128)(2,1)}) %reduce-scatter.11.cloned.1.call-update) | async-done | bytes 1179664 | tf_op jit(solution)/shard_map/reduce_scatter | solution.py:319
  453.9 43.0 %reduce-scatter.5.cloned.1.call-done = bf16[192,2304]{1,0:T(8,128)(2,1)} async-done(((bf16[768,2304]{1,0:T(8,128)(2,1)}), bf16[192,2304]{1,0:T(8,128)(2,1)}) %reduce-scatter.5.cloned.1.call-update) | async-done | bytes 884752 | tf_op jit(solution)/shard_map/reduce_scatter | solution.py:292
  497.0 279.1 %all-reduce.21 = (f32[192]{0:T(256)}, f32[192]{0:T(256)}, f32[192,2304]{1,0:T(8,128)}, f32[192]{0:T(256)}, f32[192]{0:T(256)}, /*index=5*/f32[192,768]{1,0:T(8,1...) all-reduce(f32[192]{0:T(256)S(1)} %get-tuple-element.212, ...), channel_id=1, replica_groups=mesh['ctx'=8,'fsdp'=4] {'ctx'}, use_global_device_ids=true, to_apply=%region_19.20 | all-reduce | flops 1771776 | bytes 10635264 | tf_op jit(solution)/shard_map/psum | solution.py:326
  (185 shorter events, 80.5 us)
Async XLA Ops:
  7.2 36.1 %all-gather.15.cloned.1.call-start = ((), (), s32[]{:S(2)}) async-start(), calls=%async_computation.4 | async-start | bytes 4423680 | tf_op jit(solution)/shard_map/all_gather | solution.py:86
  7.9 83.4 %all-gather.25.cloned.1.call-start = ((), (), s32[]{:S(2)}) async-start(), calls=%async_computation.13 | async-start | bytes 1769472 | tf_op jit(solution)/shard_map/all_gather | solution.py:118
  46.9 90.2 %all-gather.23.cloned.1.call-start = ((), (), s32[]{:S(2)}) async-start(), calls=%async_computation.12 | async-start | bytes 1769472 | tf_op jit(solution)/shard_map/all_gather | solution.py:117
  47.6 107.1 %all-gather.17.cloned.1.call-start = ((), (), s32[]{:S(2)}) async-start(), calls=%async_computation.5 | async-start | bytes 1474560 | tf_op jit(solution)/shard_map/all_gather | solution.py:89
  48.2 145.5 %all-gather.19.cloned.1.call-start = ((), (), s32[]{:S(2)}) async-start(), calls=%async_computation.6 | async-start | bytes 5898240 | tf_op jit(solution)/shard_map/all_gather | solution.py:152
  48.8 183.8 %all-gather.21.cloned.1.call-start = ((), (), s32[]{:S(2)}) async-start(), calls=%async_computation.7 | async-start | bytes 5898240 | tf_op jit(solution)/shard_map/all_gather | solution.py:154
  49.4 288.5 %all-gather.27.cloned.1.call-start = ((), (), s32[]{:S(2)}) async-start(), calls=%async_computation.14 | async-start | bytes 1769472 | tf_op jit(solution)/shard_map/all_gather | solution.py:234
  55.5 282.4 %all-gather.29.cloned.1.call-start = ((), (), s32[]{:S(2)}) async-start(), calls=%async_computation.15 | async-start | bytes 1769472 | tf_op jit(solution)/shard_map/all_gather | solution.py:235
  137.1 17.7 %copy-start.2 = (bf16[1,128,768]{2,1,0:T(8,128)(2,1)S(1)}, bf16[1,128,768]{2,1,0:T(8,128)(2,1)}, u32[]{:S(2)}) copy-start(bf16[1,128,768]{2,1,0:T(8,128)(2,1)} %param.21) | copy-start | bytes 589828
  150.6 43.1 %copy-start.18 = (f32[1,12,128]{2,1,0:T(8,128)}, f32[1,12,128]{2,1,0:T(8,128)S(1)}, u32[]{:S(2)}) copy-start(f32[1,12,128]{2,1,0:T(8,128)S(1)} %get-tuple-element.81) | copy-start | bytes 18436
  150.6 43.1 %copy-start.22 = (f32[1,12,128]{2,1,0:T(8,128)}, f32[1,12,128]{2,1,0:T(8,128)S(1)}, u32[]{:S(2)}) copy-start(f32[1,12,128]{2,1,0:T(8,128)S(1)} %get-tuple-element.140) | copy-start | bytes 18436
  156.5 83.4 %copy-start.24 = (f32[128]{0:T(128)}, f32[128]{0:T(128)S(1)}, u32[]{:S(2)}) copy-start(f32[128]{0:T(128)S(1)} %broadcast_multiply_fusion) | copy-start | bytes 1540
  156.7 83.2 %copy-start.27 = (f32[128]{0:T(128)}, f32[128]{0:T(128)S(1)}, u32[]{:S(2)}) copy-start(f32[128]{0:T(128)S(1)} %fusion.79) | copy-start | bytes 1540
  193.7 38.9 %copy-start.10 = (bf16[1,128,768]{2,1,0:T(8,128)(2,1)S(1)}, bf16[1,128,768]{2,1,0:T(8,128)(2,1)}, u32[]{:S(2)}) copy-start(bf16[1,128,768]{2,1,0:T(8,128)(2,1)} %param.35) | copy-start | bytes 589828
  242.8 126.1 %reduce-scatter.7.cloned.1.call-start = ((), (), s32[]{:S(2)}) async-start(), calls=%async_computation.9 | async-start | bytes 1474560 | tf_op jit(solution)/shard_map/reduce_scatter | solution.py:301
  244.4 159.2 %reduce-scatter.9.cloned.1.call-start = ((), (), s32[]{:S(2)}) async-start(), calls=%async_computation.10 | async-start | bytes 5898240 | tf_op jit(solution)/shard_map/reduce_scatter | solution.py:313
  249.3 204.6 %reduce-scatter.11.cloned.1.call-start = ((), (), s32[]{:S(2)}) async-start(), calls=%async_computation.11 | async-start | bytes 5898240 | tf_op jit(solution)/shard_map/reduce_scatter | solution.py:319
  253.4 243.6 %reduce-scatter.5.cloned.1.call-start = ((), (), s32[]{:S(2)}) async-start(), calls=%async_computation.8 | async-start | bytes 4423680 | tf_op jit(solution)/shard_map/reduce_scatter | solution.py:292
  255.2 82.8 %copy-start.6 = (bf16[128,768]{1,0:T(8,128)(2,1)S(1)}, bf16[128,768]{1,0:T(8,128)(2,1)}, u32[]{:S(2)}) copy-start(bf16[128,768]{1,0:T(8,128)(2,1)} %get-tuple-element.194) | copy-start | bytes 589828
  255.2 82.8 %copy-start.7 = (bf16[128,768]{1,0:T(8,128)(2,1)S(1)}, bf16[128,768]{1,0:T(8,128)(2,1)}, u32[]{:S(2)}) copy-start(bf16[128,768]{1,0:T(8,128)(2,1)} %slice.23) | copy-start | bytes 589828
  337.9 23.6 %copy-start.26 = (f32[128]{0:T(128)S(1)}, f32[128]{0:T(128)}, u32[]{:S(2)}) copy-start(f32[128]{0:T(128)} %copy-done.25) | copy-start | bytes 1540
  337.9 23.6 %copy-start.29 = (f32[128]{0:T(128)S(1)}, f32[128]{0:T(128)}, u32[]{:S(2)}) copy-start(f32[128]{0:T(128)} %copy-done.28) | copy-start | bytes 1540
  369.7 17.2 %copy-start.11 = (bf16[1,128,768]{2,1,0:T(8,128)(2,1)S(1)}, bf16[1,128,768]{2,1,0:T(8,128)(2,1)}, u32[]{:S(2)}) copy-start(bf16[1,128,768]{2,1,0:T(8,128)(2,1)} %param.35) | copy-start | bytes 589828
  388.5 108.5 %copy-start.15 = (bf16[192,768]{1,0:T(8,128)(2,1)S(1)}, bf16[192,768]{1,0:T(8,128)(2,1)}, u32[]{:S(2)}) copy-start(bf16[192,768]{1,0:T(8,128)(2,1)} %reduce-scatter.7.cloned.1.call-done) | copy-start | bytes 884740
  (24 other events, 110.7 us)
Sparse Core Ops, SparseCore 0:
  9.6 33.6 all-gather.14
  47.0 44.2 all-gather.24
  94.0 42.9 all-gather.22
  138.5 16.2 all-gather.16
  156.2 37.4 all-gather.18
  195.1 37.4 all-gather.20
  234.8 44.3 all-gather.26
  281.3 43.2 all-gather.28
  327.8 24.7 reduce-scatter.6
  355.1 48.3 reduce-scatter.8
  406.0 47.8 reduce-scatter.10
  456.5 40.4 reduce-scatter.4
where the time goes:
time: 784 us; the launch traced here: 783 us
  blocking collectives  375 us (48%)
  waiting for transfers between devices  277 us (35%)
  matrix products  74.9 us (10%)
  local copies, waits for them, and re-layouts  28.5 us (4%)
  between operations  16.6 us (2%)
  other arithmetic  9.79 us (1%)
    psum x1, blocking collectives, shards(): lax.psum((owned[0], owned[1], owned[2], owned[3], owned[4], owned[5], own...  279 us
    reduce_scatter x1, waiting for transfers between devices, shards(): lax.psum_scatter(out_weight_grad.astype(jnp.bfloat16), 'fsdp', scatter_di...  50.4 us
    all_gather x1, waiting for transfers between devices, shards(): key_rows = lax.all_gather(key_flat, 'ctx', axis=1, tiled=True)  45.8 us
    reduce_scatter x1, waiting for transfers between devices, shards(): lax.psum_scatter(attn_weight_grad.astype(jnp.bfloat16), 'fsdp', scatter_d...  43 us
    all_gather x1, waiting for transfers between devices, shards(): lax.all_gather(fc_weight, 'fsdp', axis=0, tiled=True)  36.9 us
    all_gather x1, waiting for transfers between devices, shards(): lax.all_gather(out_weight, 'fsdp', axis=0, tiled=True)  35.7 us
    all_gather x1, waiting for transfers between devices, shards(): value_rows = lax.all_gather(value_flat, 'ctx', axis=1, tiled=True)  35.5 us
    all_gather x1, blocking collectives, shards(): lax.all_gather(log_totals, 'ctx', axis=2, tiled=True)  33 us
  transfers between devices with their start and end apart: 12, of which 9 were waited for; matrix products, arithmetic and copies ran while one was open for 14% of the time, Pallas kernels for 0%

commit v1 on v0

v1 whole, which is shorter than its diff:
```python
from functools import partial

import jax
import jax.numpy as jnp
from jax import lax
from jax.experimental import pallas as pl
from jax.experimental.pallas import tpu as pltpu
from jax.sharding import PartitionSpec as P

HD = 64
LAYERS = 12
EPSILON = 1e-05
BF = jnp.bfloat16
F32 = jnp.float32
RESIDUAL = LAYERS ** (-0.5)
SCORE = HD ** (-0.5)
NEVER = -1e30
VMEM_BYTES = 50 * 1024 * 1024


def shape(dims, kind):
    return jax.ShapeDtypeStruct(dims, kind)


def call(body, name, outs, *args, scratch=()):
    vmem = pl.BlockSpec(memory_space=pltpu.VMEM)
    smem = pl.BlockSpec(memory_space=pltpu.SMEM)
    return pl.pallas_call(
        body,
        name=name,
        out_shape=outs,
        in_specs=[smem] + [vmem] * (len(args) - 1),
        out_specs=[vmem] * len(outs),
        scratch_shapes=list(scratch),
        compiler_params=pltpu.CompilerParams(vmem_limit_bytes=VMEM_BYTES),
    )(*args)


def rows_at(index, size):
    return pl.ds(pl.multiple_of(index * size, size), size)


def dot(first, second):
    return jnp.dot(first, second, preferred_element_type=F32)


def dot_rows(first, second):
    return lax.dot_general(first, second, (((0,), (0,)), ((), ())), preferred_element_type=F32)


def dot_columns(first, second):
    return lax.dot_general(first, second, (((1,), (1,)), ((), ())), preferred_element_type=F32)


def normalize(values):
    center = jnp.mean(values, axis=-1, keepdims=True)
    centered = values - center
    spread = jnp.mean(centered * centered, axis=-1, keepdims=True)
    scale = lax.rsqrt(spread + EPSILON)
    return centered * scale, scale


def norm_back(grad, unit, scale, gain):
    inner = grad * gain
    mean_inner = jnp.mean(inner, axis=-1, keepdims=True)
    mean_along = jnp.mean(inner * unit, axis=-1, keepdims=True)
    return scale * (inner - mean_inner - unit * mean_along)


def join_body(at, *refs):
    pieces, (whole,) = refs[:-1], refs[-1:]
    size = pieces[0].shape[0]
    for k, piece in enumerate(pieces):
        whole[rows_at(at[2] ^ k, size), :] = piece[...]


def mixed_body(parts, rows, at, gathered, bias, *refs):
    weights, (normed, matrix, vectors), outs = refs[:parts], refs[parts : parts + 3], refs[parts + 3 : -1]
    kept = refs[-1]
    width = weights[0].shape[0]
    features = parts * width
    for k, piece in enumerate(weights):
        matrix[rows_at(at[2] ^ k, width), :] = piece[...]
    small = jnp.concatenate([gathered[j, rows : rows + 8, :width] for j in range(parts)], axis=1).astype(F32)
    vectors[...] = small
    for j in range(parts):
        unit, _ = normalize(gathered[j, :rows, :].astype(F32))
        normed[j * rows : (j + 1) * rows, :] = (unit * small[0:1] + small[1:2]).astype(BF)
    kept[...] = (dot(normed[...], matrix[...]) + bias[...]).astype(BF)
    count = len(outs) // 2
    for k in range(count):
        block = rows_at(at[0] ^ k, rows)
        outs[k][...] = kept[block, :256]
        outs[count + k][...] = kept[block, 256:]


def place(at, count, blocks, rows, queries, pairs, partners, q_all, kv_all):
    for k in range(count):
        row = at[0] ^ k
        q_all[rows_at(row, rows), :] = queries[k][...]
        kv_all[rows_at(row * blocks + at[1], rows), :] = pairs[k][...]
        for j, partner in enumerate(partners):
            side = row * blocks + (at[1] ^ (j + 1))
            kv_all[rows_at(side, rows), :] = partner[k * rows : (k + 1) * rows, :]


def head_views(tile_one, tile_two, scale):
    low = lax.broadcasted_iota(jnp.int32, tile_one.shape, 1) < HD
    zero = jnp.zeros_like(tile_one)
    tile_one = tile_one * scale if scale is not None else tile_one
    tile_two = tile_two * scale if scale is not None else tile_two
    return (jnp.where(low, tile_one, zero), jnp.where(low, zero, tile_one), tile_two)


def visible_keys(at, i, blocks, rows, keys):
    query = (i * blocks + at[1]) * rows + lax.broadcasted_iota(jnp.int32, (rows, keys), 0)
    return lax.broadcasted_iota(jnp.int32, (rows, keys), 1) <= query


def attend_body(count, blocks, rows, at, *refs):
    queries, pairs = refs[:count], refs[count : 2 * count]
    partners = refs[2 * count : 2 * count + blocks - 1]
    outs = refs[2 * count + blocks - 1 :]
    pieces, (exact, totals, q_all, kv_all) = outs[:count], outs[count:]
    place(at, count, blocks, rows, queries, pairs, partners, q_all, kv_all)
    low = lax.broadcasted_iota(jnp.int32, (rows, 128), 1) < HD
    for i in range(count):
        keys = (i + 1) * blocks * rows
        mine = slice(i * rows, (i + 1) * rows)
        heads = head_views(q_all[mine, :128], q_all[mine, 128:], SCORE)
        seen = visible_keys(at, i, blocks, rows, keys)
        found = []
        for h, query in enumerate(heads):
            key_cols = slice(0, 128) if h < 2 else slice(256, 384)
            value_cols = slice(128, 256) if h < 2 else slice(256, 384)
            scores = jnp.where(seen, dot_columns(query, kv_all[:keys, key_cols]), NEVER)
            highest = jnp.max(scores, axis=-1, keepdims=True)
            weights = jnp.exp(scores - highest)
            total = jnp.sum(weights, axis=-1, keepdims=True)
            totals[mine, h : h + 1] = highest + jnp.log(total)
            weights = (weights * (1.0 / total)).astype(BF)
            found.append(dot(weights, kv_all[:keys, value_cols]))
        exact[mine, :128] = jnp.where(low, found[0], found[1])
        exact[mine, 128:] = jnp.where(low, 0.0, found[2])
    for k in range(count):
        pieces[k][...] = exact[rows_at(at[0] ^ k, rows), :].astype(BF)


def attend_back_body(count, blocks, rows, at, *refs):
    grads, (q_all, kv_all, exact, totals) = refs[:count], refs[count : count + 4]
    outs = refs[count + 4 :]
    pieces, (own, away), (g_all, dq_all, acc) = outs[:count], outs[count : count + 2], outs[count + 2 :]
    for k in range(count):
        g_all[rows_at(at[0] ^ k, rows), :] = grads[k][...]
    acc[...] = jnp.zeros_like(acc)
    low = lax.broadcasted_iota(jnp.int32, (rows, 128), 1) < HD
    for i in range(count):
        keys = (i + 1) * blocks * rows
        mine = slice(i * rows, (i + 1) * rows)
        q_heads = head_views(q_all[mine, :128], q_all[mine, 128:], SCORE)
        g_heads = head_views(g_all[mine, :128], g_all[mine, 128:], None)
        seen = visible_keys(at, i, blocks, rows, keys)
        found = []
        for h in range(3):
            key_cols = slice(0, 128) if h < 2 else slice(256, 384)
            value_cols = slice(128, 256) if h < 2 else slice(256, 384)
            kept = exact[mine, :128] if h < 2 else exact[mine, 128:]
            delta = jnp.sum(g_heads[h].astype(F32) * kept, axis=-1, keepdims=True)
            scores = dot_columns(q_heads[h], kv_all[:keys, key_cols]) - totals[mine, h : h + 1]
            weights = jnp.exp(jnp.where(seen, scores, NEVER))
            g_weights = dot_columns(g_heads[h], kv_all[:keys, value_cols])
            g_scores = (weights * (g_weights - delta)).astype(BF)
            found.append(dot(g_scores, kv_all[:keys, key_cols]))
            acc[:keys, key_cols] += dot_rows(g_scores, q_heads[h])
            acc[:keys, value_cols] += dot_rows(weights.astype(BF), g_heads[h])
        dq_all[mine, :128] = (jnp.where(low, found[0], found[1]) * SCORE).astype(BF)
        dq_all[mine, 128:] = (jnp.where(low, found[2], 0.0) * SCORE).astype(BF)
    for k in range(count):
        row = at[0] ^ k
        pieces[k][...] = dq_all[rows_at(row, rows), :]
        into = slice(k * rows, (k + 1) * rows)
        own[into, :] = acc[rows_at(row * blocks + at[1], rows), :]
        for j in range(1, blocks):
            from_rows = slice((j - 1) * count * rows + k * rows, (j - 1) * count * rows + (k + 1) * rows)
            away[from_rows, :] = acc[rows_at(row * blocks + (at[1] ^ j), rows), :].astype(BF)


def plain_heads(values):
    zero = jnp.zeros_like(values[:, :HD])
    first = jnp.concatenate([values[:, :HD], zero], 1)
    second = jnp.concatenate([zero, values[:, HD:128]], 1)
    return (first, second, values[:, 128:])


def plain_terms(at, count, blocks, rows):
    q_pos = (jnp.arange(count)[:, None] * blocks + at[1]) * rows + jnp.arange(rows)[None]
    k_pos = jnp.arange(count * blocks * rows)
    return k_pos[None] <= q_pos.reshape(-1)[:, None]


def plain_attend(count, blocks, rows, at, queries, pairs, partners):
    width = pairs[0].shape[1]
    q_all = jnp.zeros((count, rows, queries[0].shape[1]), BF)
    kv_all = jnp.zeros((count, blocks, rows, width), BF)
    for k in range(count):
        row = at[0] ^ k
        q_all = q_all.at[row].set(queries[k])
        kv_all = kv_all.at[row, at[1]].set(pairs[k])
        for j, partner in enumerate(partners):
            kv_all = kv_all.at[row, at[1] ^ (j + 1)].set(partner[k * rows : (k + 1) * rows])
    q_all, kv_all = q_all.reshape(count * rows, -1), kv_all.reshape(-1, width)
    seen = plain_terms(at, count, blocks, rows)
    found, totals = [], []
    for h, query in enumerate(plain_heads(q_all)):
        key = kv_all[:, :128] if h < 2 else kv_all[:, 256:]
        value = kv_all[:, 128:256] if h < 2 else kv_all[:, 256:]
        scores = jnp.where(seen, dot_columns(query, key) * SCORE, NEVER)
        total = jax.nn.logsumexp(scores, axis=-1, keepdims=True)
        found.append(dot(jnp.exp(scores - total).astype(BF), value))
        totals.append(total)
    exact = jnp.concatenate([found[0][:, :HD], found[1][:, HD:], jnp.zeros_like(found[2][:, :HD]), found[2][:, HD:]], 1)
    grid = exact.astype(BF).reshape(count, rows, -1)
    pieces = [grid[at[0] ^ k] for k in range(count)]
    totals = jnp.concatenate(totals + [jnp.zeros((count * rows, 125), F32)], 1)
    return (*pieces, exact, totals, q_all, kv_all)


def plain_attend_back(count, blocks, rows, at, grads, q_all, kv_all, exact, totals):
    g_all = jnp.zeros((count, rows, grads[0].shape[1]), BF)
    for k in range(count):
        g_all = g_all.at[at[0] ^ k].set(grads[k])
    g_all = g_all.reshape(count * rows, -1)
    seen = plain_terms(at, count, blocks, rows)
    dq, parts = [], []
    for h, (query, grad, kept) in enumerate(zip(plain_heads(q_all), plain_heads(g_all), plain_heads(exact))):
        key = kv_all[:, :128] if h < 2 else kv_all[:, 256:]
        value = kv_all[:, 128:256] if h < 2 else kv_all[:, 256:]
        delta = jnp.sum(grad.astype(F32) * kept, axis=-1, keepdims=True)
        scores = dot_columns(query, key) * SCORE - totals[:, h : h + 1]
        weights = jnp.exp(jnp.where(seen, scores, NEVER))
        g_scores = (weights * (dot_columns(grad, value) - delta)).astype(BF)
        dq.append(dot(g_scores, key) * SCORE)
        parts.append((dot_rows(g_scores, query) * SCORE, dot_rows(weights.astype(BF), grad)))
    dq = jnp.concatenate([dq[0][:, :HD], dq[1][:, HD:], dq[2][:, :HD], jnp.zeros_like(dq[2][:, :HD])], 1)
    dq = dq.astype(BF).reshape(count, rows, -1)
    acc = jnp.concatenate([parts[0][0] + parts[1][0], parts[0][1] + parts[1][1], parts[2][0] + parts[2][1]], 1)
    acc = acc.reshape(count, blocks, rows, -1)
    pieces = [dq[at[0] ^ k] for k in range(count)]
    own = jnp.concatenate([acc[at[0] ^ k, at[1]] for k in range(count)], 0)
    away = [acc[at[0] ^ k, at[1] ^ j].astype(BF) for j in range(1, blocks) for k in range(count)]
    return (*pieces, own, jnp.concatenate(away, 0))


def merge_body(count, rows, at, own, *refs):
    arrived, outs = refs[:-count], refs[-count:]
    for k in range(count):
        part = slice(k * rows, (k + 1) * rows)
        total = own[part, :]
        for ref in arrived:
            total = total + ref[part, :].astype(F32)
        outs[k][...] = total.astype(BF)


def gelu_terms(hidden):
    root = 0.7978845608028654
    square = hidden * hidden
    bend = jnp.tanh(root * hidden * (1.0 + 0.044715 * square))
    half = 0.5 * (1.0 + bend)
    slope = half + 0.5 * hidden * (1.0 - bend * bend) * root * (1.0 + 3.0 * 0.044715 * square)
    return hidden * half, slope


def middle_body(parts, rows, at, attended, tok, extra, vectors, fc, fc_bias, out, *refs):
    gn_mine, gn_other, mid_mine, normed, active, g_hidden, att_all, proj, mid = refs
    width = extra.shape[1] - rows
    zero = jnp.zeros((HD, proj.shape[1]), BF)
    for j in range(parts):
        weight = extra[j, rows:, :]
        proj[j * 256 : j * 256 + 128, :] = weight[:128]
        proj[j * 256 + 128 : j * 256 + 128 + HD, :] = zero
        proj[j * 256 + 128 + HD : (j + 1) * 256, :] = weight[128:width]
        for k in range(parts):
            att_all[rows_at(at[0] ^ k, rows), j * 256 : (j + 1) * 256] = attended[j, k * rows : (k + 1) * rows, :]
    branch = dot(att_all[...], proj[...]) + vectors[4:5]
    for j in range(parts):
        part = slice(j * rows, (j + 1) * rows)
        value = tok[j, :rows, :].astype(F32) + RESIDUAL * branch[part]
        mid[part, :] = value
        unit, _ = normalize(value)
        normed[part, :] = (unit * vectors[2:3] + vectors[3:4]).astype(BF)
    hidden = dot(normed[...], fc[...]) + fc_bias[...].astype(F32)
    value, slope = gelu_terms(hidden)
    active[...] = value.astype(BF)
    g_out = jnp.concatenate([(RESIDUAL * extra[j, :rows, :].astype(F32)).astype(BF) for j in range(parts)], axis=0)
    g_hidden[...] = (dot_columns(g_out, out[...]) * slope).astype(BF)
    grad = dot_columns(g_hidden[...], fc[...])
    core = at[3]
    for s in range(parts):
        part = slice(s * rows, (s + 1) * rows)
        into = slice((s // 2) * rows, (s // 2 + 1) * rows)

        @pl.when(core == s % 2)
        def _():
            gn_mine[into, :] = grad[part]
            mid_mine[into, :] = mid[part, :]

        @pl.when(core != s % 2)
        def _():
            gn_other[into, :] = grad[part]


def weights_body(parts, rows, ways, at, extra, normed, active, g_hidden, out, *refs):
    mine, other, out_grad, fc_grad, sums = refs
    g_out = jnp.concatenate([(RESIDUAL * extra[j, :rows, :].astype(F32)).astype(BF) for j in range(parts)], axis=0)
    result = dot(active[...], out[...])
    core = at[3]
    for s in range(parts):
        part = slice(s * rows, (s + 1) * rows)
        into = slice((s // 2) * rows, (s // 2 + 1) * rows)

        @pl.when(core == s % 2)
        def _():
            mine[into, :] = result[part]

        @pl.when(core != s % 2)
        def _():
            other[into, :] = result[part]

    grad = dot_rows(active[...], g_out)
    size = grad.shape[0] // ways
    for c in range(ways):
        out_grad[c, :, :] = grad[c * size : (c + 1) * size].astype(BF)
    grad = dot_rows(normed[...], g_hidden[...])
    size = grad.shape[0] // (ways * parts)
    for c in range(ways):
        for j in range(parts):
            at_row = (j * ways + c) * size
            fc_grad[c, j, :, :] = grad[at_row : at_row + size].astype(BF)
    sums[...] = jnp.zeros_like(sums)
    sums[0:1, :] = jnp.sum(g_out.astype(F32), axis=0, keepdims=True)
    sums[1:2, :] = jnp.sum(g_hidden[...].astype(F32), axis=0, keepdims=True)


def second_norm_body(rows, at, chip_sum, arrived, mid, extra, vectors, g_branch, own_middle, sums):
    grad = chip_sum[...] + arrived[...].astype(F32)
    unit, scale = normalize(mid[...])
    back = norm_back(grad, unit, scale, vectors[2:3])
    sums[...] = jnp.zeros_like(sums)
    sums[0:1, :] = jnp.sum(grad * unit, axis=0, keepdims=True)
    sums[1:2, :] = jnp.sum(grad, axis=0, keepdims=True)
    core = at[3]
    for j in range(2):
        part = slice(j * rows, (j + 1) * rows)
        g_middle = back[part] + extra[2 * j + core, :rows, :].astype(F32)
        g_branch[part, :] = (RESIDUAL * g_middle).astype(BF)

        @pl.when(at[2] == 2 * j + core)
        def _():
            own_middle[...] = g_middle


def attended_grad_body(parts, rows, at, mine, other, proj, *refs):
    outs, (kept, g_all) = refs[:parts], refs[parts:]
    core = at[3]
    for j in range(2):
        part = slice(j * rows, (j + 1) * rows)
        kept[rows_at(2 * j + core, rows), :] = mine[part, :]
        kept[rows_at(2 * j + 1 - core, rows), :] = other[part, :]
    zero = jnp.zeros((HD, proj.shape[1]), BF)
    weight = jnp.concatenate([proj[:128, :], zero, proj[128:, :]], axis=0)
    g_all[...] = dot_columns(kept[...], weight).astype(BF)
    for k in range(parts):
        outs[k][...] = g_all[rows_at(at[0] ^ k, rows), :]


def proj_grad_body(parts, rows, ways, at, attended, g_branch, proj_grad, sums):
    grad = jnp.zeros((256, g_branch.shape[1]), F32)
    for k in range(parts):
        grad = grad + dot_rows(attended[k * rows : (k + 1) * rows, :], g_branch[rows_at(at[0] ^ k, rows), :])
    grad = jnp.concatenate([grad[:128], grad[128 + HD :]], axis=0)
    size = grad.shape[0] // ways
    for c in range(ways):
        proj_grad[c, :, :] = grad[c * size : (c + 1) * size].astype(BF)
    sums[...] = jnp.zeros_like(sums)
    sums[0:1, :] = jnp.sum(g_branch[...].astype(F32), axis=0, keepdims=True)


def first_grad_body(parts, rows, ways, at, normed, matrix, *refs):
    queries, pairs = refs[:parts], refs[parts : 2 * parts]
    mine, other, grads, sums, mixed = refs[2 * parts :]
    for k in range(parts):
        block = rows_at(at[0] ^ k, rows)
        mixed[block, :256] = queries[k][...]
        mixed[block, 256:] = pairs[k][...]
    back = dot_columns(mixed[...], matrix[...])
    core = at[3]
    for s in range(parts):
        part = slice(s * rows, (s + 1) * rows)
        into = slice((s // 2) * rows, (s // 2 + 1) * rows)

        @pl.when(core == s % 2)
        def _():
            mine[into, :] = back[part]

        @pl.when(core != s % 2)
        def _():
            other[into, :] = back[part]

    grad = dot_rows(normed[...], mixed[...])
    size = grad.shape[0] // (ways * parts)
    for c in range(ways):
        for j in range(parts):
            at_row = (j * ways + c) * size
            grads[c, j, :, :] = grad[at_row : at_row + size].astype(BF)
    sums[...] = jnp.zeros_like(sums)
    sums[0:1, :] = jnp.sum(mixed[...].astype(F32), axis=0, keepdims=True)


def first_norm_body(at, own, arrived, tokens, own_middle, vectors, input_grad, sums):
    grad = own[...] + arrived[...].astype(F32)
    unit, scale = normalize(tokens[...].astype(F32))
    back = norm_back(grad, unit, scale, vectors[0:1])
    input_grad[...] = (back + own_middle[...]).astype(BF)
    sums[...] = jnp.zeros_like(sums)
    sums[0:1, :] = jnp.sum(grad * unit, axis=0, keepdims=True)
    sums[1:2, :] = jnp.sum(grad, axis=0, keepdims=True)


def shards(
    parts,
    ways,
    tokens,
    first_gain,
    first_bias,
    attn_weight,
    query_bias,
    value_bias,
    proj_weight,
    proj_bias,
    second_gain,
    second_bias,
    fc_weight,
    fc_bias,
    out_weight,
    out_bias,
    cotangent,
):
    rows, features = tokens.shape[1], tokens.shape[2]
    width = features // parts
    count = parts
    blocks = ways // count
    hidden = fc_weight.shape[1] // parts
    f = lax.axis_index("fsdp").astype(jnp.int32)
    c = lax.axis_index("ctx").astype(jnp.int32)
    a, b, core = c // blocks, c % blocks, f % 2
    at = jnp.stack([a, b, f, core])

    def over_fsdp(value, k):
        return lax.ppermute(value, "fsdp", [(i, i ^ k) for i in range(parts)])

    def over_ctx(value, k):
        return lax.ppermute(value, "ctx", [(i, i ^ k) for i in range(ways)])

    tok, cot = tokens[0], cotangent[0]

    small = jnp.stack([first_gain, first_bias, second_gain, second_bias, proj_bias, out_bias])
    small = jnp.pad(small, ((0, 2), (0, features - width)))
    tok_all = lax.all_gather(jnp.concatenate([tok, small], 0), "fsdp")
    split = attn_weight.reshape(width, 3, parts, width)
    zero = jnp.zeros((width, HD), BF)

    def head_columns(owner):
        q, k, v = (lax.dynamic_index_in_dim(split[:, i], owner, 1, keepdims=False) for i in range(3))
        return jnp.concatenate([q, zero, k[:, :128], v[:, :128], k[:, 128:], v[:, 128:]], 1)

    attn_pieces = [head_columns(f)] + [over_fsdp(head_columns(f ^ k), k) for k in range(1, parts)]
    fc_split = fc_weight.reshape(width, parts, hidden)

    def fc_columns(owner):
        return lax.dynamic_index_in_dim(fc_split, owner, 1, keepdims=False)

    fc_pieces = [fc_columns(f)] + [over_fsdp(fc_columns(f ^ k), k) for k in range(1, parts)]
    extra = lax.all_gather(jnp.concatenate([cot, proj_weight], 0), "fsdp")

    none = jnp.zeros((128,), F32)
    vb = value_bias.astype(F32)
    bias = jnp.concatenate([query_bias.astype(F32), none[:HD], none, vb[:128], none[:HD], vb[128:]])[None]
    columns = bias.shape[1]
    mixed = call(
        partial(mixed_body, parts, rows),
        "mixed",
        [shape((parts * rows, features), BF), shape((features, columns), BF), shape((8, features), F32)]
        + [shape((rows, 256), BF)] * count
        + [shape((rows, 384), BF)] * count,
        at,
        tok_all,
        bias,
        *attn_pieces,
        scratch=[pltpu.VMEM((parts * rows, columns), BF)],
    )
    normed, attn_matrix, vectors = mixed[:3]
    queries, pairs = mixed[3 : 3 + count], mixed[3 + count :]

    pairs = [pairs[0]] + [over_ctx(pairs[k], k * blocks) for k in range(1, count)]
    queries = [queries[0]] + [over_ctx(queries[k], k * blocks) for k in range(1, count)]
    joined = jnp.concatenate(pairs, 0)
    partners = [over_ctx(joined, j) for j in range(1, blocks)]
    small_blocks = blocks * count * rows <= 1024
    if small_blocks:
        kept = call(
            partial(attend_body, count, blocks, rows),
            "attend",
            [shape((rows, 256), BF)] * count
            + [
                shape((count * rows, 256), F32),
                shape((count * rows, 128), F32),
                shape((count * rows, 256), BF),
                shape((count * blocks * rows, 384), BF),
            ],
            at,
            *queries,
            *pairs,
            *partners,
        )
    else:
        kept = plain_attend(count, blocks, rows, at, queries, pairs, partners)
    att_pieces, state = kept[:count], kept[count:]
    att_pieces = [att_pieces[0]] + [over_ctx(att_pieces[k], k * blocks) for k in range(1, count)]
    attended = jnp.concatenate(att_pieces, 0)
    attended_all = lax.all_gather(attended, "fsdp")
    fc_matrix = call(join_body, "join", [shape((features, hidden), BF)], at, *fc_pieces)[0]

    half = parts * rows // 2
    gn_mine, gn_other, mid_mine, normed_two, active, g_hidden = call(
        partial(middle_body, parts, rows),
        "middle",
        [shape((half, features), F32)] * 3
        + [shape((parts * rows, features), BF), shape((parts * rows, hidden), BF), shape((parts * rows, hidden), BF)],
        at,
        attended_all,
        tok_all,
        extra,
        vectors,
        fc_matrix,
        fc_bias[None],
        out_weight,
        scratch=[
            pltpu.VMEM((parts * rows, parts * 256), BF),
            pltpu.VMEM((parts * 256, features), BF),
            pltpu.VMEM((parts * rows, features), F32),
        ],
    )
    chip_sum = gn_mine + over_fsdp(gn_other, 1)
    arrived = over_fsdp(chip_sum.astype(BF), 2)
    size = features // (ways * parts)
    mine, other, out_grad, fc_grad, sums_mlp = call(
        partial(weights_body, parts, rows, ways),
        "mlp_weights",
        [
            shape((half, features), F32),
            shape((half, features), F32),
            shape((ways, hidden // ways, features), BF),
            shape((ways, parts, size, hidden), BF),
            shape((8, features), F32),
        ],
        at,
        extra,
        normed_two,
        active,
        g_hidden,
        out_weight,
    )
    g_branch, own_middle, sums_two = call(
        partial(second_norm_body, rows),
        "second_norm",
        [shape((half, features), BF), shape((rows, features), F32), shape((8, features), F32)],
        at,
        chip_sum,
        arrived,
        mid_mine,
        extra,
        vectors,
    )
    other_branch = over_fsdp(g_branch, 1)
    grads = call(
        partial(attended_grad_body, parts, rows),
        "attended_grad",
        [shape((rows, 256), BF)] * parts + [shape((parts * rows, features), BF)],
        at,
        g_branch,
        other_branch,
        proj_weight,
        scratch=[pltpu.VMEM((parts * rows, 256), BF)],
    )
    g_pieces, g_branch_all = grads[:parts], grads[parts]
    g_pieces = [g_pieces[0]] + [over_ctx(g_pieces[k], k * blocks) for k in range(1, count)]
    proj_grad, sums_proj = call(
        partial(proj_grad_body, parts, rows, ways),
        "proj_weight_grad",
        [shape((ways, width // ways, features), BF), shape((8, features), F32)],
        at,
        attended,
        g_branch_all,
    )
    if small_blocks:
        back = call(
            partial(attend_back_body, count, blocks, rows),
            "attend_back",
            [shape((rows, 256), BF)] * count
            + [shape((count * rows, 384), F32), shape(((blocks - 1) * count * rows, 384), BF)],
            at,
            *g_pieces,
            state[2],
            state[3],
            state[0],
            state[1],
            scratch=[
                pltpu.VMEM((count * rows, 256), BF),
                pltpu.VMEM((count * rows, 256), BF),
                pltpu.VMEM((count * blocks * rows, 384), F32),
            ],
        )
    else:
        back = plain_attend_back(count, blocks, rows, at, g_pieces, state[2], state[3], state[0], state[1])
    dq, own, away = back[:count], back[count], back[count + 1]
    stack = count * rows
    from_partners = [over_ctx(away[(j - 1) * stack : j * stack], j) for j in range(1, blocks)]
    dkv = call(partial(merge_body, count, rows), "merge", [shape((rows, 384), BF)] * count, at, own, *from_partners)
    dq = [dq[0]] + [over_ctx(dq[k], k * blocks) for k in range(1, count)]
    dkv = [dkv[0]] + [over_ctx(dkv[k], k * blocks) for k in range(1, count)]
    g1_mine, g1_other, attn_grad, sums_attn = call(
        partial(first_grad_body, parts, rows, ways),
        "first_grad",
        [
            shape((half, features), F32),
            shape((half, features), F32),
            shape((ways, parts, size, columns), BF),
            shape((8, columns), F32),
        ],
        at,
        normed,
        attn_matrix,
        *dq,
        *dkv,
        scratch=[pltpu.VMEM((parts * rows, columns), BF)],
    )

    def own_rows(values, place):
        return lax.dynamic_slice_in_dim(values, place * rows, rows, 0)

    x = f // 2
    first_sum = g1_mine + over_fsdp(g1_other, 1)
    first_arrived = over_fsdp(own_rows(first_sum, 1 - x).astype(BF), 2)
    input_grad, sums_one = call(
        first_norm_body,
        "first_norm",
        [shape((rows, features), BF), shape((8, features), F32)],
        at,
        own_rows(first_sum, x),
        first_arrived,
        tok,
        own_middle,
        vectors,
    )
    out_sum = mine + over_fsdp(other, 1)
    out_arrived = over_fsdp(own_rows(out_sum, 1 - x).astype(BF), 2)
    output = own_rows(out_sum, x) + out_arrived.astype(F32) + vectors[5:6]
    block_out = (own_rows(mid_mine, x) + RESIDUAL * output).astype(BF)

    sums_one = sums_one[:2] + over_fsdp(sums_one[:2], 1)
    sums_one = sums_one + over_fsdp(sums_one, 2)
    sums_two = sums_two[:2] + over_fsdp(sums_two[:2], 1)

    def own_slice(row):
        return lax.dynamic_slice_in_dim(row, f * width, width, 0)

    sums_q = sums_attn[0, :width]
    sums_v = jnp.concatenate([sums_attn[0, 384:512], sums_attn[0, 512 + HD :]])
    vector_sums = jnp.concatenate(
        [
            own_slice(sums_one[0]),
            own_slice(sums_one[1]),
            sums_q,
            sums_v,
            own_slice(sums_proj[0]),
            own_slice(sums_two[0]),
            own_slice(sums_two[1]),
            own_slice(sums_mlp[0]),
            sums_mlp[1],
        ]
    )
    vector_sums = lax.psum(vector_sums.reshape(-1, 128), "ctx").reshape(-1)
    slices = [vector_sums[i * width : (i + 1) * width] for i in range(8)]
    fc_bias_grad = vector_sums[8 * width :]

    def reduce_ctx(value):
        return lax.psum_scatter(value, "ctx", scatter_dimension=0, tiled=False)

    def turn(value):
        return lax.all_to_all(value, "fsdp", split_axis=0, concat_axis=0, tiled=False)

    def gather_ctx(value):
        return lax.all_gather(value, "ctx")

    mlp_sum = reduce_ctx(jnp.concatenate([out_grad, fc_grad.reshape(ways, parts * size, hidden)], 1))
    out_size = hidden // ways
    fc_turned = turn(mlp_sum[out_size:].reshape(parts, size, hidden))
    mlp_all = gather_ctx(jnp.concatenate([mlp_sum[:out_size], fc_turned.reshape(parts * size, hidden)], 0))
    out_weight_grad = mlp_all[:, :out_size].reshape(hidden, features).astype(F32)
    fc_all = mlp_all[:, out_size:].reshape(ways, parts, size, hidden)
    fc_weight_grad = fc_all.transpose(0, 2, 1, 3).reshape(width, parts * hidden).astype(F32)
    proj_all = gather_ctx(reduce_ctx(proj_grad))
    proj_weight_grad = proj_all.reshape(width, features).astype(F32)
    attn_all = gather_ctx(turn(reduce_ctx(attn_grad)))
    attn_all = attn_all.transpose(0, 2, 1, 3).reshape(width, parts, columns)
    q = attn_all[:, :, :width]
    k = jnp.concatenate([attn_all[:, :, 256:384], attn_all[:, :, 512 : 512 + HD]], 2)
    v = jnp.concatenate([attn_all[:, :, 384:512], attn_all[:, :, 512 + HD :]], 2)
    attn_weight_grad = jnp.stack([q, k, v], 1).reshape(width, 3 * features).astype(F32)
    return (
        block_out[None],
        input_grad[None],
        slices[0],
        slices[1],
        attn_weight_grad,
        slices[2],
        slices[3],
        proj_weight_grad,
        slices[4],
        slices[5],
        slices[6],
        fc_weight_grad,
        fc_bias_grad,
        out_weight_grad,
        slices[7],
    )


def solution(mesh):
    rows, row, matrix = P("fsdp", "ctx", None), P("fsdp"), P("fsdp", None)
    return jax.shard_map(
        partial(shards, mesh.shape["fsdp"], mesh.shape["ctx"]),
        mesh=mesh,
        in_specs=(
            rows, row, row, matrix, row, row, matrix, row, row, row, matrix, row, matrix, row, rows,
        ),
        out_specs=(
            rows, rows, row, row, matrix, row, row, matrix, row, row, row, matrix, row, matrix, row,
        ),
        check_vma=False,
    )
```

time: 784 us -> 427 us (0.54)
  blocking collectives: 375 us -> 117 us
  waiting for transfers between devices: 277 us -> 155 us
  matrix products: 74.9 us -> 0 us
  starting transfers between devices: 0.88 us -> 46.1 us
  Pallas kernels: 0 us -> 38.6 us
  local copies, waits for them, and re-layouts: 28.5 us -> 39.3 us
    psum x1, blocking collectives: 279 us -> 35.5 us  [shards(): vector_sums = lax.psum(vector_sums.reshape(-1, 128), 'ctx').reshape(-1)]
    all_gather x8 -> x3, waiting for transfers between devices: 170 us -> 23.4 us  [the longest x1 14.7 us: shards(): extra = lax.all_gather(jnp.concatenate([cot, proj_weight], 0), 'fsdp')]
    ppermute x0 -> x36, waiting for transfers between devices: none -> 86 us  [the longest x20 44.6 us: over_ctx(): return lax.ppermute(value, 'ctx', [(i, i ^ k) for i in range(ways)])]
    dot_general x19 -> x0, matrix products: 74.9 us -> none  [the longest x4 13.5 us: left_product(): lax.dot_general(first, second, (((0,), (0,)), ((), ())), preferred_elemen...]
    reduce_scatter x4 -> x3, waiting for transfers between devices: 104 us -> 37.7 us  [reduce_ctx(): return lax.psum_scatter(value, 'ctx', scatter_dimension=0, tiled=False)]
    ppermute x0 -> x36, starting transfers between devices: none -> 39 us  [the longest x20 30.1 us: over_ctx(): return lax.ppermute(value, 'ctx', [(i, i ^ k) for i in range(ways)])]
    pallas_call x0 -> x12, Pallas kernels: none -> 38.6 us  [call(): pl.pallas_call(body, name=name, out_shape=outs, in_specs=[smem] + [vmem]...]
    unnamed x2 -> x0, blocking collectives: 25.7 us -> none
  transfers between devices with their start and end apart: 12 -> 44, of which waited for: 9 -> 26; matrix products, arithmetic and copies ran while one was open for 14% -> 6% of each run, Pallas kernels for 0% -> 4%
where the time goes in v1:
time: 427 us; the launch traced here: 422 us
  waiting for transfers between devices  155 us (36%)
  blocking collectives  117 us (27%)
  starting transfers between devices  46.1 us (11%)
  local copies, waits for them, and re-layouts  39.3 us (9%)
  Pallas kernels  38.6 us (9%)
  between operations  15.4 us (4%)
  other arithmetic  10.1 us (2%)
    all_gather x2, blocking collectives, gather_ctx(): return lax.all_gather(value, 'ctx')  66.3 us
    ppermute x20, waiting for transfers between devices, over_ctx(): return lax.ppermute(value, 'ctx', [(i, i ^ k) for i in range(ways)])  44.6 us
    ppermute x16, waiting for transfers between devices, over_fsdp(): return lax.ppermute(value, 'fsdp', [(i, i ^ k) for i in range(parts)])  41.4 us
    pallas_call x12, Pallas kernels, call(): pl.pallas_call(body, name=name, out_shape=outs, in_specs=[smem] + [vmem]...  38.6 us
    reduce_scatter x3, waiting for transfers between devices, reduce_ctx(): return lax.psum_scatter(value, 'ctx', scatter_dimension=0, tiled=False)  37.7 us
    psum x1, blocking collectives, shards(): vector_sums = lax.psum(vector_sums.reshape(-1, 128), 'ctx').reshape(-1)  35.5 us
    ppermute x20, starting transfers between devices, over_ctx(): return lax.ppermute(value, 'ctx', [(i, i ^ k) for i in range(ways)])  30.1 us
    all_gather x1, blocking collectives, shards(): tok_all = lax.all_gather(jnp.concatenate([tok, small], 0), 'fsdp')  15.4 us
  transfers between devices with their start and end apart: 44, of which 26 were waited for; matrix products, arithmetic and copies ran while one was open for 6% of the time, Pallas kernels for 4%

profile of v1, /device:TPU:0, one launch (start us, length us, event | category | flops | bytes accessed | tf_op | source)
XLA Modules:
  0.0 421.9 jit_solution(1056220156096697301)
XLA Ops:
  18.5 15.4 %all-gather = bf16[544,768]{1,0:T(8,128)(2,1)S(1)} all-gather(bf16[136,768]{1,0:T(8,128)(2,1)S(1)} %fusion.1), channel_id=2, replica_groups=mesh['ctx'=8,'fsdp'=4] {'fsdp'}, dimensions={0}, use_global_device_ids=true | all-gather | bytes 1044480 | tf_op jit(solution)/shard_map/all_gather | solution.py:468
  41.1 7.4 %collective-permute-done.7.refs_6_ = bf16[128,384]{1,0:T(8,128)(2,1)S(1)} collective-permute-done((bf16[128,384]{1,0:T(8,128)(2,1)S(1)}, bf16[128,384]{1,0:T(8,128)(2,1)S(1)}, u32[]{:S(2)}, u32[]{:S(2)}) %collective-permute-start.7) | collective-permute-done | bytes 98336 | tf_op jit(solution)/shard_map/ppermute | solution.py:462
  59.4 5.2 %attend.1 = (bf16[128,256]{1,0:T(8,128)(2,1)S(1)}, bf16[128,256]{1,0:T(8,128)(2,1)S(1)}, bf16[128,256]{1,0:T(8,128)(2,1)S(1)}, bf16[128,256]{1,0:T(8,128)(2,1)S(...) custom-call(s32[4]{0:T(128)S(1)} %pad_add_fusion.at, ...), custom_call_target="tpu_custom_call" | custom-call | tf_op jit(solution)/shard_map/attend/pallas_call | solution.py:28
  80.0 5.1 %constant_dynamic-slice_fusion.7 = (bf16[192,1,768]{2,1,0:T(2,128)(2,1)S(1)}, bf16[192,1,768]{2,1,0:T(2,128)(2,1)S(1)}, bf16[192,1,768]{2,1,0:T(2,128)(2,1)S(1)}, bf16[192,1,768]{2,1,0:T(2,128)(2,1)S(1)}) fusion(bf16[192,4,768]{2,1,0:T(4,128)(2,1)} %reshape.104, s32[]{:T(128)S(6)} %select_n.67, s32[]{:T(128)S(6)} %select_n.66, s32[]{:T(128)S(6)} %select_n.65, ...), kind=kLoop, calls=%fused_computation.45 | loop fusion | bytes 2359312 | tf_op jit(solution)/shard_map/jit(dynamic_index_in_dim)/dynamic_slice | solution.py:480
  87.4 8.9 %collective-permute-done.14.refs_2_ = bf16[192,768]{1,0:T(8,128)(2,1)S(1)} collective-permute-done((bf16[192,768]{1,0:T(8,128)(2,1)S(1)}, bf16[192,768]{1,0:T(8,128)(2,1)S(1)}, u32[]{:S(2)}, u32[]{:S(2)}) %collective-permute-start.14) | collective-permute-done | bytes 294944 | tf_op jit(solution)/shard_map/ppermute | solution.py:459
  96.3 6.0 %collective-permute-done.15.refs_3_ = bf16[192,768]{1,0:T(8,128)(2,1)S(1)} collective-permute-done((bf16[192,768]{1,0:T(8,128)(2,1)S(1)}, bf16[192,768]{1,0:T(8,128)(2,1)S(1)}, u32[]{:S(2)}, u32[]{:S(2)}) %collective-permute-start.15) | collective-permute-done | bytes 294944 | tf_op jit(solution)/shard_map/ppermute | solution.py:459
  104.0 14.7 %all-gather.11.cloned.1.call-done = bf16[1280,768]{1,0:T(8,128)(2,1)} async-done(((bf16[320,768]{1,0:T(8,128)(2,1)}), bf16[1280,768]{1,0:T(8,128)(2,1)}) %all-gather.11.cloned.1.call-update) | async-done | bytes 1966096 | tf_op jit(solution)/shard_map/all_gather | solution.py:483
  118.7 7.8 %middle.1 = (f32[256,768]{1,0:T(8,128)S(1)}, f32[256,768]{1,0:T(8,128)S(1)}, f32[256,768]{1,0:T(8,128)S(1)}, bf16[512,768]{1,0:T(8,128)(2,1)S(1)}, bf16[512,768]...) custom-call(s32[4]{0:T(128)S(1)} %pad_add_fusion.at, bf16[4,512,256]{2,1,0:T(8,128)(2,1)} %bitcast.121, ...), custom_call_target="tpu_custom_call" | custom-call | tf_op jit(solution)/shard_map/middle/pallas_call | solution.py:28
  128.6 5.9 %mlp_weights.1 = (f32[256,768]{1,0:T(8,128)S(1)}, f32[256,768]{1,0:T(8,128)}, bf16[8,96,768]{2,1,0:T(8,128)(2,1)}, bf16[8,4,24,768]{3,2,1,0:T(8,128)(2,1)}, f32[8,768]{1,0:T(8,128)S(1)}) custom-call(s32[4]{0:T(128)S(1)} %pad_add_fusion.at, bf16[4,320,768]{2,1,0:T(8,128)(2,1)} %bitcast.110, bf16[512,768]{1,0:T(8,128)(2,1)S(1)} %get-tuple-element.85.normed, ...), custom_call_target="tpu_custom_call" | custom-call | tf_op jit(solution)/shard_map/mlp_weights/pallas_call | solution.py:28
  142.3 11.0 %collective-permute-done.19.arrived = bf16[256,768]{1,0:T(8,128)(2,1)S(1)} collective-permute-done((bf16[256,768]{1,0:T(8,128)(2,1)S(1)}, bf16[256,768]{1,0:T(8,128)(2,1)S(1)}, u32[]{:S(2)}, u32[]{:S(2)}) %collective-permute-start.19) | collective-permute-done | bytes 393248 | tf_op jit(solution)/shard_map/ppermute | solution.py:459
  166.2 4.6 %collective-permute-done.21.refs_1_ = bf16[128,256]{1,0:T(8,128)(2,1)S(1)} collective-permute-done((bf16[128,256]{1,0:T(8,128)(2,1)}, bf16[128,256]{1,0:T(8,128)(2,1)S(1)}, u32[]{:S(2)}, u32[]{:S(2)}) %collective-permute-start.21) | collective-permute-done | bytes 65568 | tf_op jit(solution)/shard_map/ppermute | solution.py:462
  175.6 5.2 %attend_back.1 = (bf16[128,256]{1,0:T(8,128)(2,1)S(1)}, bf16[128,256]{1,0:T(8,128)(2,1)S(1)}, bf16[128,256]{1,0:T(8,128)(2,1)S(1)}, bf16[128,256]{1,0:T(8,128)(2...) custom-call(s32[4]{0:T(128)S(1)} %pad_add_fusion.at, bf16[128,256]{1,0:T(8,128)(2,1)S(1)} %get-tuple-element.95.refs_0_, ...), custom_call_target="tpu_custom_call" | custom-call | tf_op jit(solution)/shard_map/attend_back/pallas_call | solution.py:28
  184.9 8.1 %collective-permute-done.27.refs_0_ = bf16[512,384]{1,0:T(8,128)(2,1)S(1)} collective-permute-done((bf16[512,384]{1,0:T(8,128)(2,1)S(1)}, bf16[512,384]{1,0:T(8,128)(2,1)S(1)}, u32[]{:S(2)}, u32[]{:S(2)}) %collective-permute-start.27) | collective-permute-done | bytes 393248 | tf_op jit(solution)/shard_map/ppermute | solution.py:462
  200.5 9.3 %collective-permute-done.26.refs_3_ = bf16[128,256]{1,0:T(8,128)(2,1)S(1)} collective-permute-done((bf16[128,256]{1,0:T(8,128)(2,1)S(1)}, bf16[128,256]{1,0:T(8,128)(2,1)S(1)}, u32[]{:S(2)}, u32[]{:S(2)}) %collective-permute-start.26) | collective-permute-done | bytes 65568 | tf_op jit(solution)/shard_map/ppermute | solution.py:462
  211.3 4.3 %first_grad.1 = (f32[256,768]{1,0:T(8,128)S(1)}, f32[256,768]{1,0:T(8,128)S(1)}, bf16[8,4,24,640]{3,2,1,0:T(8,128)(2,1)}, f32[8,640]{1,0:T(8,128)S(1)}) custom-call(s32[4]{0:T(128)S(1)} %pad_add_fusion.at, bf16[512,768]{1,0:T(8,128)(2,1)S(1)} %get-tuple-element.90.normed, bf16[768,640]{1,0:T(8,128)(2,1)} %get-tuple-element.91.matrix, ...), custom_call_target="tpu_custom_call" | custom-call | tf_op jit(solution)/shard_map/first_grad/pallas_call | solution.py:28
  219.1 4.5 %collective-permute-done.17 = bf16[128,768]{1,0:T(8,128)(2,1)S(1)} collective-permute-done((bf16[128,768]{1,0:T(8,128)(2,1)S(1)}, bf16[128,768]{1,0:T(8,128)(2,1)S(1)}, u32[]{:S(2)}, u32[]{:S(2)}) %collective-permute-start.17) | collective-permute-done | bytes 196640 | tf_op jit(solution)/shard_map/ppermute | solution.py:459
  230.1 4.2 %all-to-all-done.1 = bf16[4,24,768]{2,1,0:T(8,128)(2,1)S(1)} async-done(((bf16[4,24,768]{2,1,0:T(8,128)(2,1)}), bf16[4,24,768]{2,1,0:T(8,128)(2,1)S(1)}, u32[]{:S(2)}, u32[]{:S(2)}) %all-to-all-start.1) | async-done | bytes 147488 | tf_op jit(solution)/shard_map/all_to_all | solution.py:700
  236.0 5.8 %collective-permute-done.32.arrived = bf16[128,768]{1,0:T(8,128)(2,1)S(1)} collective-permute-done((bf16[128,768]{1,0:T(8,128)(2,1)S(1)}, bf16[128,768]{1,0:T(8,128)(2,1)S(1)}, u32[]{:S(2)}, u32[]{:S(2)}) %collective-permute-start.32) | collective-permute-done | bytes 196640 | tf_op jit(solution)/shard_map/ppermute | solution.py:459
  243.4 37.7 %reduce-scatter.6.cloned.1.call-done = bf16[1,24,768]{2,1,0:T(8,128)(2,1)} async-done(((bf16[8,24,768]{2,1,0:T(8,128)(2,1)}), bf16[1,24,768]{2,1,0:T(8,128)(2,1)}) %reduce-scatter.6.cloned.1.call-update) | async-done | bytes 36880 | tf_op jit(solution)/shard_map/reduce_scatter | solution.py:697
  281.1 31.4 %all_gather.41 = bf16[8,24,768]{2,1,0:T(8,128)(2,1)S(1)} all-gather(bf16[1,24,768]{2,1,0:T(8,128)(2,1)} %reduce-scatter.6.cloned.1.call-done), channel_id=1, replica_groups=mesh['ctx'=8,'fsdp'=4] {'ctx'}, dimensions={0}, use_global_device_ids=true | all-gather | bytes 331776 | tf_op jit(solution)/shard_map/all_gather | solution.py:703
  316.4 35.5 %psum.7 = f32[18,128]{1,0:T(8,128)S(1)} all-reduce(f32[18,128]{1,0:T(8,128)S(1)} %bitcast.149), channel_id=1, replica_groups=mesh['ctx'=8,'fsdp'=4] {'ctx'}, use_global_device_ids=true, to_apply=%region_0.1 | all-reduce | flops 2304 | bytes 18432 | tf_op jit(solution)/shard_map/psum | solution.py:692
  356.5 3.9 all-to-all-done
  360.4 34.9 %all-gather.3 = bf16[32,24,640]{2,1,0:T(8,128)(2,1)S(1)} all-gather(bf16[4,24,640]{2,1,0:T(8,128)(2,1)S(1)} %all-to-all-done), channel_id=5, replica_groups=mesh['ctx'=8,'fsdp'=4] {'ctx'}, dimensions={0}, use_global_device_ids=true | all-gather | bytes 1105920 | tf_op jit(solution)/shard_map/all_gather | solution.py:703
  400.4 8.6 %all-gather.13.cloned.1.call-done = bf16[1536,768]{1,0:T(8,128)(2,1)} async-done(((bf16[192,768]{1,0:T(8,128)(2,1)}), bf16[1536,768]{1,0:T(8,128)(2,1)}) %all-gather.13.cloned.1.call-update) | async-done | bytes 2359312 | tf_op jit(solution)/shard_map/all_gather | solution.py:703
  (271 shorter events, 120.9 us)
Async XLA Ops:
  7.2 96.8 %all-gather.9.cloned.1.call-start = ((), (), s32[]{:S(2)}) async-start(), calls=%async_computation.8 | async-start | bytes 1310720 | tf_op jit(solution)/shard_map/all_gather | solution.py:530
  13.3 20.6 %collective-permute-start = (bf16[192,640]{1,0:T(8,128)(2,1)S(1)}, bf16[192,640]{1,0:T(8,128)(2,1)S(1)}, u32[]{:S(2)}, u32[]{:S(2)}) collective-permute-start(bf16[192,640]{1,0:T(8,128)(2,1)S(1)} %concatenate.45), channel_id=1, source_target_pairs={{0,1},{1,0},{2,3},{3,2},{4,5},{5,4},{6,7},{7,6},{8,9},{9,8},{10,11... | collective-permute-start | bytes 737288 | tf_op jit(solution)/shard_map/ppermute | solution.py:459
  14.1 19.8 %collective-permute-start.1 = (bf16[192,640]{1,0:T(8,128)(2,1)S(1)}, bf16[192,640]{1,0:T(8,128)(2,1)S(1)}, u32[]{:S(2)}, u32[]{:S(2)}) collective-permute-start(bf16[192,640]{1,0:T(8,128)(2,1)S(1)} %concatenate.46), channel_id=1, source_target_pairs={{0,2},{1,3},{2,0},{3,1},{4,6},{5,7},{6,4},{7,5},{8,10},{9,11},{10,... | collective-permute-start | bytes 737288 | tf_op jit(solution)/shard_map/ppermute | solution.py:459
  17.7 16.2 %collective-permute-start.2 = (bf16[192,640]{1,0:T(8,128)(2,1)}, bf16[192,640]{1,0:T(8,128)(2,1)S(1)}, u32[]{:S(2)}, u32[]{:S(2)}) collective-permute-start(bf16[192,640]{1,0:T(8,128)(2,1)} %concatenate.47), channel_id=1, source_target_pairs={{0,3},{1,2},{2,1},{3,0},{4,7},{5,6},{6,5},{7,4},{8,11},{9,10},{10,... | collective-permute-start | bytes 737288 | tf_op jit(solution)/shard_map/ppermute | solution.py:459
  37.8 10.7 %collective-permute-start.7 = (bf16[128,384]{1,0:T(8,128)(2,1)S(1)}, bf16[128,384]{1,0:T(8,128)(2,1)S(1)}, u32[]{:S(2)}, u32[]{:S(2)}) collective-permute-start(bf16[128,384]{1,0:T(8,128)(2,1)S(1)} %get-tuple-element.77), channel_id=1, source_target_pairs={{0,16},{4,20},{8,24},{12,28},{16,0},{20,4},{24,8},{28,12},{1,17},{... | collective-permute-start | bytes 294920 | tf_op jit(solution)/shard_map/ppermute | solution.py:462
  48.5 10.9 %collective-permute-start.9 = (bf16[512,384]{1,0:T(8,128)(2,1)S(1)}, bf16[512,384]{1,0:T(8,128)(2,1)S(1)}, u32[]{:S(2)}, u32[]{:S(2)}) collective-permute-start(bf16[512,384]{1,0:T(8,128)(2,1)S(1)} %pad_maximum_fusion.2), channel_id=1, source_target_pairs={{0,4},{4,0},{8,12},{12,8},{16,20},{20,16},{24,28},{28,24},{1,5},{5... | collective-permute-start | bytes 1179656 | tf_op jit(solution)/shard_map/ppermute | solution.py:462
  75.4 43.3 %all-gather.11.cloned.1.call-start = ((), (), s32[]{:S(2)}) async-start(), calls=%async_computation.9 | async-start | bytes 2457600 | tf_op jit(solution)/shard_map/all_gather | solution.py:483
  76.3 148.2 %reduce-scatter.8.cloned.1.call-start = ((), (), s32[]{:S(2)}) async-start(), calls=%async_computation.7 | async-start | bytes 2654208 | tf_op jit(solution)/shard_map/reduce_scatter | solution.py:697
  85.3 11.0 %collective-permute-start.14 = (bf16[192,768]{1,0:T(8,128)(2,1)S(1)}, bf16[192,768]{1,0:T(8,128)(2,1)S(1)}, u32[]{:S(2)}, u32[]{:S(2)}) collective-permute-start(bf16[192,768]{1,0:T(8,128)(2,1)S(1)} %bitcast.144), channel_id=1, source_target_pairs={{0,2},{1,3},{2,0},{3,1},{4,6},{5,7},{6,4},{7,5},{8,10},{9,11},{10,... | collective-permute-start | bytes 884744 | tf_op jit(solution)/shard_map/ppermute | solution.py:459
  86.9 15.4 %collective-permute-start.15 = (bf16[192,768]{1,0:T(8,128)(2,1)S(1)}, bf16[192,768]{1,0:T(8,128)(2,1)S(1)}, u32[]{:S(2)}, u32[]{:S(2)}) collective-permute-start(bf16[192,768]{1,0:T(8,128)(2,1)S(1)} %bitcast.145), channel_id=1, source_target_pairs={{0,3},{1,2},{2,1},{3,0},{4,7},{5,6},{6,5},{7,4},{8,11},{9,10},{10,... | collective-permute-start | bytes 884744 | tf_op jit(solution)/shard_map/ppermute | solution.py:459
  139.2 141.9 %reduce-scatter.6.cloned.1.call-start = ((), (), s32[]{:S(2)}) async-start(), calls=%async_computation.6 | async-start | bytes 331776 | tf_op jit(solution)/shard_map/reduce_scatter | solution.py:697
  141.9 11.3 %collective-permute-start.19 = (bf16[256,768]{1,0:T(8,128)(2,1)S(1)}, bf16[256,768]{1,0:T(8,128)(2,1)S(1)}, u32[]{:S(2)}, u32[]{:S(2)}) collective-permute-start(bf16[256,768]{1,0:T(8,128)(2,1)S(1)} %get-tuple-element.127), channel_id=1, source_target_pairs={{0,2},{1,3},{2,0},{3,1},{4,6},{5,7},{6,4},{7,5},{8,10},{9,11},{10,... | collective-permute-start | bytes 1179656 | tf_op jit(solution)/shard_map/ppermute | solution.py:459
  161.7 190.9 %reduce-scatter.4.cloned.1.call-start = ((), (), s32[]{:S(2)}) async-start(), calls=%async_computation.5 | async-start | bytes 1105920 | tf_op jit(solution)/shard_map/reduce_scatter | solution.py:697
  163.3 10.9 %collective-permute-start.22 = (bf16[128,256]{1,0:T(8,128)(2,1)}, bf16[128,256]{1,0:T(8,128)(2,1)S(1)}, u32[]{:S(2)}, u32[]{:S(2)}) collective-permute-start(bf16[128,256]{1,0:T(8,128)(2,1)} %copy-done.25), channel_id=1, source_target_pairs={{0,16},{4,20},{8,24},{12,28},{16,0},{20,4},{24,8},{28,12},{1,17},{... | collective-permute-start | bytes 196616 | tf_op jit(solution)/shard_map/ppermute | solution.py:462
  180.9 12.1 %collective-permute-start.27 = (bf16[512,384]{1,0:T(8,128)(2,1)S(1)}, bf16[512,384]{1,0:T(8,128)(2,1)S(1)}, u32[]{:S(2)}, u32[]{:S(2)}) collective-permute-start(bf16[512,384]{1,0:T(8,128)(2,1)S(1)} %get-tuple-element.108), channel_id=1, source_target_pairs={{0,4},{4,0},{8,12},{12,8},{16,20},{20,16},{24,28},{28,24},{1,5},{5... | collective-permute-start | bytes 1179656 | tf_op jit(solution)/shard_map/ppermute | solution.py:462
  182.2 16.4 %collective-permute-start.24 = (bf16[128,256]{1,0:T(8,128)(2,1)S(1)}, bf16[128,256]{1,0:T(8,128)(2,1)S(1)}, u32[]{:S(2)}, u32[]{:S(2)}) collective-permute-start(bf16[128,256]{1,0:T(8,128)(2,1)S(1)} %get-tuple-element.104), channel_id=1, source_target_pairs={{0,8},{4,12},{8,0},{12,4},{16,24},{20,28},{24,16},{28,20},{1,9},{5... | collective-permute-start | bytes 196616 | tf_op jit(solution)/shard_map/ppermute | solution.py:462
  184.3 14.3 %collective-permute-start.25 = (bf16[128,256]{1,0:T(8,128)(2,1)S(1)}, bf16[128,256]{1,0:T(8,128)(2,1)S(1)}, u32[]{:S(2)}, u32[]{:S(2)}) collective-permute-start(bf16[128,256]{1,0:T(8,128)(2,1)S(1)} %get-tuple-element.105), channel_id=1, source_target_pairs={{0,16},{4,20},{8,24},{12,28},{16,0},{20,4},{24,8},{28,12},{1,17},{... | collective-permute-start | bytes 196616 | tf_op jit(solution)/shard_map/ppermute | solution.py:462
  193.6 16.1 %collective-permute-start.28 = (bf16[128,384]{1,0:T(8,128)(2,1)S(1)}, bf16[128,384]{1,0:T(8,128)(2,1)S(1)}, u32[]{:S(2)}, u32[]{:S(2)}) collective-permute-start(bf16[128,384]{1,0:T(8,128)(2,1)S(1)} %get-tuple-element.110), channel_id=1, source_target_pairs={{0,8},{4,12},{8,0},{12,4},{16,24},{20,28},{24,16},{28,20},{1,9},{5... | collective-permute-start | bytes 294920 | tf_op jit(solution)/shard_map/ppermute | solution.py:462
  196.1 15.2 %collective-permute-start.29 = (bf16[128,384]{1,0:T(8,128)(2,1)S(1)}, bf16[128,384]{1,0:T(8,128)(2,1)S(1)}, u32[]{:S(2)}, u32[]{:S(2)}) collective-permute-start(bf16[128,384]{1,0:T(8,128)(2,1)S(1)} %get-tuple-element.111), channel_id=1, source_target_pairs={{0,16},{4,20},{8,24},{12,28},{16,0},{20,4},{24,8},{28,12},{1,17},{... | collective-permute-start | bytes 294920 | tf_op jit(solution)/shard_map/ppermute | solution.py:462
  196.6 14.7 %collective-permute-start.30 = (bf16[128,384]{1,0:T(8,128)(2,1)S(1)}, bf16[128,384]{1,0:T(8,128)(2,1)S(1)}, u32[]{:S(2)}, u32[]{:S(2)}) collective-permute-start(bf16[128,384]{1,0:T(8,128)(2,1)S(1)} %get-tuple-element.112), channel_id=1, source_target_pairs={{0,24},{4,28},{8,16},{12,20},{16,8},{20,12},{24,0},{28,4},{1,25},{... | collective-permute-start | bytes 294920 | tf_op jit(solution)/shard_map/ppermute | solution.py:462
  198.6 18.0 %collective-permute-start.16 = (f32[256,768]{1,0:T(8,128)}, f32[256,768]{1,0:T(8,128)}, u32[]{:S(2)}, u32[]{:S(2)}) collective-permute-start(f32[256,768]{1,0:T(8,128)} %get-tuple-element.89), channel_id=1, source_target_pairs={{0,1},{1,0},{2,3},{3,2},{4,5},{5,4},{6,7},{7,6},{8,9},{9,8},{10,11... | collective-permute-start | bytes 2359304 | tf_op jit(solution)/shard_map/ppermute | solution.py:459
  198.6 11.2 %collective-permute-start.26 = (bf16[128,256]{1,0:T(8,128)(2,1)S(1)}, bf16[128,256]{1,0:T(8,128)(2,1)S(1)}, u32[]{:S(2)}, u32[]{:S(2)}) collective-permute-start(bf16[128,256]{1,0:T(8,128)(2,1)S(1)} %get-tuple-element.106), channel_id=1, source_target_pairs={{0,24},{4,28},{8,16},{12,20},{16,8},{20,12},{24,0},{28,4},{1,25},{... | collective-permute-start | bytes 196616 | tf_op jit(solution)/shard_map/ppermute | solution.py:462
  229.5 179.5 %all-gather.13.cloned.1.call-start = ((), (), s32[]{:S(2)}) async-start(), calls=%async_computation.10 | async-start | bytes 2654208 | tf_op jit(solution)/shard_map/all_gather | solution.py:703
  243.4 69.0 %collective-permute-start.33 = (f32[2,768]{1,0:T(2,128)S(1)}, f32[2,768]{1,0:T(2,128)S(1)}, u32[]{:S(2)}, u32[]{:S(2)}) collective-permute-start(f32[2,768]{1,0:T(2,128)S(1)} %slice.196), channel_id=1, source_target_pairs={{0,1},{1,0},{2,3},{3,2},{4,5},{5,4},{6,7},{7,6},{8,9},{9,8},{10,11... | collective-permute-start | bytes 18440 | tf_op jit(solution)/shard_map/ppermute | solution.py:459
  (57 other events, 302.4 us)
Sparse Core Ops, SparseCore 0:
  75.5 17.2 all-gather.8
  95.0 23.7 all-gather.10
  139.3 81.1 reduce-scatter.7
  223.6 57.4 reduce-scatter.5
  284.9 62.4 reduce-scatter.3
  350.2 58.7 all-gather.12

commit v2 on v1

v2 whole, which is shorter than its diff:
```python
from functools import partial

import jax
import jax.numpy as jnp
from jax import lax
from jax.experimental import pallas as pl
from jax.experimental.pallas import tpu as pltpu
from jax.sharding import PartitionSpec as P

HD = 64
LAYERS = 12
EPSILON = 1e-05
BF = jnp.bfloat16
F32 = jnp.float32
RESIDUAL = LAYERS ** (-0.5)
SCORE = HD ** (-0.5)
NEVER = -1e30
VMEM_BYTES = 50 * 1024 * 1024


def shape(dims, kind):
    return jax.ShapeDtypeStruct(dims, kind)


def call(body, name, outs, *args, scratch=(), after=()):
    vmem = pl.BlockSpec(memory_space=pltpu.VMEM)
    smem = pl.BlockSpec(memory_space=pltpu.SMEM)
    held = pl.BlockSpec(memory_space=pl.ANY)
    count, waits = len(args), len(after)

    def run(*refs):
        body(*refs[:count], *refs[count + waits :])

    return pl.pallas_call(
        run,
        name=name,
        out_shape=outs,
        in_specs=[smem] + [vmem] * (count - 1) + [held] * waits,
        out_specs=[vmem] * len(outs),
        scratch_shapes=list(scratch),
        compiler_params=pltpu.CompilerParams(vmem_limit_bytes=VMEM_BYTES),
    )(*args, *after)


def rows_at(index, size):
    return pl.ds(pl.multiple_of(index * size, size), size)


def dot(first, second):
    return jnp.dot(first, second, preferred_element_type=F32)


def dot_rows(first, second):
    return lax.dot_general(first, second, (((0,), (0,)), ((), ())), preferred_element_type=F32)


def dot_columns(first, second):
    return lax.dot_general(first, second, (((1,), (1,)), ((), ())), preferred_element_type=F32)


def normalize(values):
    center = jnp.mean(values, axis=-1, keepdims=True)
    centered = values - center
    spread = jnp.mean(centered * centered, axis=-1, keepdims=True)
    scale = lax.rsqrt(spread + EPSILON)
    return centered * scale, scale


def norm_back(grad, unit, scale, gain):
    inner = grad * gain
    mean_inner = jnp.mean(inner, axis=-1, keepdims=True)
    mean_along = jnp.mean(inner * unit, axis=-1, keepdims=True)
    return scale * (inner - mean_inner - unit * mean_along)


def join(at, pieces, whole):
    size = pieces[0].shape[0]
    for k, piece in enumerate(pieces):
        whole[rows_at(at[2] ^ k, size), :] = piece[...]


def join_body(at, *refs):
    join(at, refs[:-1], refs[-1])


def columns_body(parts, at, attn, fc, small, *refs):
    attn_pieces, fc_pieces = refs[:parts], refs[parts:]
    features = attn.shape[1] // 3
    width = features // parts
    hidden = fc.shape[1] // parts
    unit = (
        lax.broadcasted_iota(jnp.int32, (8, HD), 0) == lax.broadcasted_iota(jnp.int32, (8, HD), 1)
    ).astype(BF)
    spare = dot_rows(small[...], unit).astype(BF)
    for owner in range(parts):

        @pl.when(at[2] == owner)
        def _():
            for k in range(parts):
                first = (owner ^ k) * width
                piece = attn_pieces[k]
                piece[:, :width] = attn[:, first : first + width]
                piece[:, width:256] = spare
                key = attn[:, features + first : features + first + width]
                value = attn[:, 2 * features + first : 2 * features + first + width]
                piece[:, 256:384] = key[:, :128]
                piece[:, 384:512] = value[:, :128]
                piece[:, 512 : 512 + HD] = key[:, 128:]
                piece[:, 512 + HD :] = value[:, 128:]
                fc_pieces[k][...] = fc[:, (owner ^ k) * hidden : ((owner ^ k) + 1) * hidden]


def block_of(at, k, rows):
    return rows_at(at[2] ^ at[0] ^ k, rows)


def mixed_body(parts, count, at, bias, *refs):
    tokens, weights = refs[:parts], refs[parts : 2 * parts]
    normed, matrix, vectors, *outs, kept = refs[2 * parts :]
    rows = tokens[0].shape[0]
    join(at, weights, matrix)
    columns = matrix.shape[1]
    width = weights[0].shape[0]
    pick = lax.broadcasted_iota(jnp.int32, (8, columns), 1) == width + lax.broadcasted_iota(
        jnp.int32, (8, columns), 0
    )
    small = dot_columns(pick.astype(BF), matrix[...])
    vectors[...] = small
    for k in range(parts):
        unit, _ = normalize(tokens[k][...].astype(F32))
        normed[k * rows : (k + 1) * rows, :] = (unit * small[0:1] + small[1:2]).astype(BF)
    lane = lax.broadcasted_iota(jnp.int32, (1, columns), 1)
    spare = (lane >= width) & (lane < 256)
    kept[...] = jnp.where(spare, 0.0, dot(normed[...], matrix[...]) + bias[...]).astype(BF)
    for k in range(count):
        block = block_of(at, k, rows)
        outs[k][...] = kept[block, :256]
        outs[count + k][...] = kept[block, 256:]


def place(at, count, blocks, rows, queries, pairs, partners, q_all, kv_all):
    for k in range(count):
        row = at[0] ^ k
        q_all[rows_at(row, rows), :] = queries[k][...]
        kv_all[rows_at(row * blocks + at[1], rows), :] = pairs[k][...]
        for j, partner in enumerate(partners):
            side = row * blocks + (at[1] ^ (j + 1))
            kv_all[rows_at(side, rows), :] = partner[k * rows : (k + 1) * rows, :]


def head_views(tile_one, tile_two, scale):
    low = lax.broadcasted_iota(jnp.int32, tile_one.shape, 1) < HD
    zero = jnp.zeros_like(tile_one)
    tile_one = tile_one * scale if scale is not None else tile_one
    tile_two = tile_two * scale if scale is not None else tile_two
    return (jnp.where(low, tile_one, zero), jnp.where(low, zero, tile_one), tile_two)


def visible_keys(at, i, blocks, rows, keys):
    query = (i * blocks + at[1]) * rows + lax.broadcasted_iota(jnp.int32, (rows, keys), 0)
    return lax.broadcasted_iota(jnp.int32, (rows, keys), 1) <= query


def attend_body(count, blocks, rows, at, *refs):
    queries, pairs = refs[:count], refs[count : 2 * count]
    partners = refs[2 * count : 2 * count + blocks - 1]
    fc_pieces = refs[2 * count + blocks - 1 : 3 * count + blocks - 1]
    outs = refs[3 * count + blocks - 1 :]
    pieces, (exact, totals, q_all, kv_all, fc) = outs[:count], outs[count:]
    join(at, fc_pieces, fc)
    place(at, count, blocks, rows, queries, pairs, partners, q_all, kv_all)
    low = lax.broadcasted_iota(jnp.int32, (rows, 128), 1) < HD
    for i in range(count):
        keys = (i + 1) * blocks * rows
        mine = slice(i * rows, (i + 1) * rows)
        heads = head_views(q_all[mine, :128], q_all[mine, 128:], SCORE)
        seen = visible_keys(at, i, blocks, rows, keys)
        found = []
        for h, query in enumerate(heads):
            key_cols = slice(0, 128) if h < 2 else slice(256, 384)
            value_cols = slice(128, 256) if h < 2 else slice(256, 384)
            scores = jnp.where(seen, dot_columns(query, kv_all[:keys, key_cols]), NEVER)
            highest = jnp.max(scores, axis=-1, keepdims=True)
            weights = jnp.exp(scores - highest)
            total = jnp.sum(weights, axis=-1, keepdims=True)
            totals[mine, h : h + 1] = highest + jnp.log(total)
            weights = (weights * (1.0 / total)).astype(BF)
            found.append(dot(weights, kv_all[:keys, value_cols]))
        exact[mine, :128] = jnp.where(low, found[0], found[1])
        exact[mine, 128:] = jnp.where(low, 0.0, found[2])
    half = rows // 2
    for k in range(count):
        block = rows_at(at[0] ^ k, rows)
        pieces[k][:rows, :] = exact[block, :128].astype(BF)
        last = exact[block, 128:]
        pair = jnp.where(low[:half], pltpu.roll(last[:half], HD, 1), last[half:])
        pieces[k][rows:, :] = pair.astype(BF)


def attend_back_body(count, blocks, rows, at, *refs):
    grads, (q_all, kv_all, exact, totals) = refs[:count], refs[count : count + 4]
    outs = refs[count + 4 :]
    pieces, (own, away), (g_all, dq_all, acc) = outs[:count], outs[count : count + 2], outs[count + 2 :]
    for k in range(count):
        g_all[rows_at(at[0] ^ k, rows), :] = grads[k][...]
    acc[...] = jnp.zeros_like(acc)
    low = lax.broadcasted_iota(jnp.int32, (rows, 128), 1) < HD
    for i in range(count):
        keys = (i + 1) * blocks * rows
        mine = slice(i * rows, (i + 1) * rows)
        q_heads = head_views(q_all[mine, :128], q_all[mine, 128:], SCORE)
        g_heads = head_views(g_all[mine, :128], g_all[mine, 128:], None)
        seen = visible_keys(at, i, blocks, rows, keys)
        found = []
        for h in range(3):
            key_cols = slice(0, 128) if h < 2 else slice(256, 384)
            value_cols = slice(128, 256) if h < 2 else slice(256, 384)
            kept = exact[mine, :128] if h < 2 else exact[mine, 128:]
            delta = jnp.sum(g_heads[h].astype(F32) * kept, axis=-1, keepdims=True)
            scores = dot_columns(q_heads[h], kv_all[:keys, key_cols]) - totals[mine, h : h + 1]
            weights = jnp.exp(jnp.where(seen, scores, NEVER))
            g_weights = dot_columns(g_heads[h], kv_all[:keys, value_cols])
            g_scores = (weights * (g_weights - delta)).astype(BF)
            found.append(dot(g_scores, kv_all[:keys, key_cols]))
            acc[:keys, key_cols] += dot_rows(g_scores, q_heads[h])
            acc[:keys, value_cols] += dot_rows(weights.astype(BF), g_heads[h])
        dq_all[mine, :128] = (jnp.where(low, found[0], found[1]) * SCORE).astype(BF)
        dq_all[mine, 128:] = (jnp.where(low, found[2], 0.0) * SCORE).astype(BF)
    for k in range(count):
        row = at[0] ^ k
        pieces[k][...] = dq_all[rows_at(row, rows), :]
        into = slice(k * rows, (k + 1) * rows)
        own[into, :] = acc[rows_at(row * blocks + at[1], rows), :]
        for j in range(1, blocks):
            from_rows = slice((j - 1) * count * rows + k * rows, (j - 1) * count * rows + (k + 1) * rows)
            away[from_rows, :] = acc[rows_at(row * blocks + (at[1] ^ j), rows), :].astype(BF)


def plain_heads(values):
    zero = jnp.zeros_like(values[:, :HD])
    first = jnp.concatenate([values[:, :HD], zero], 1)
    second = jnp.concatenate([zero, values[:, HD:128]], 1)
    return (first, second, values[:, 128:])


def plain_terms(at, count, blocks, rows):
    q_pos = (jnp.arange(count)[:, None] * blocks + at[1]) * rows + jnp.arange(rows)[None]
    k_pos = jnp.arange(count * blocks * rows)
    return k_pos[None] <= q_pos.reshape(-1)[:, None]


def plain_attend(count, blocks, rows, at, queries, pairs, partners):
    width = pairs[0].shape[1]
    q_all = jnp.zeros((count, rows, queries[0].shape[1]), BF)
    kv_all = jnp.zeros((count, blocks, rows, width), BF)
    for k in range(count):
        row = at[0] ^ k
        q_all = q_all.at[row].set(queries[k])
        kv_all = kv_all.at[row, at[1]].set(pairs[k])
        for j, partner in enumerate(partners):
            kv_all = kv_all.at[row, at[1] ^ (j + 1)].set(partner[k * rows : (k + 1) * rows])
    q_all, kv_all = q_all.reshape(count * rows, -1), kv_all.reshape(-1, width)
    seen = plain_terms(at, count, blocks, rows)
    found, totals = [], []
    for h, query in enumerate(plain_heads(q_all)):
        key = kv_all[:, :128] if h < 2 else kv_all[:, 256:]
        value = kv_all[:, 128:256] if h < 2 else kv_all[:, 256:]
        scores = jnp.where(seen, dot_columns(query, key) * SCORE, NEVER)
        total = jax.nn.logsumexp(scores, axis=-1, keepdims=True)
        found.append(dot(jnp.exp(scores - total).astype(BF), value))
        totals.append(total)
    exact = jnp.concatenate([found[0][:, :HD], found[1][:, HD:], jnp.zeros_like(found[2][:, :HD]), found[2][:, HD:]], 1)
    grid = exact.astype(BF).reshape(count, rows, -1)
    half = rows // 2
    pair = jnp.concatenate([grid[:, :half, 128 + HD :], grid[:, half:, 128 + HD :]], 2)
    grid = jnp.concatenate([grid[:, :, :128], pair], 1)
    pieces = [grid[at[0] ^ k] for k in range(count)]
    totals = jnp.concatenate(totals + [jnp.zeros((count * rows, 125), F32)], 1)
    return (*pieces, exact, totals, q_all, kv_all)


def plain_attend_back(count, blocks, rows, at, grads, q_all, kv_all, exact, totals):
    g_all = jnp.zeros((count, rows, grads[0].shape[1]), BF)
    for k in range(count):
        g_all = g_all.at[at[0] ^ k].set(grads[k])
    g_all = g_all.reshape(count * rows, -1)
    seen = plain_terms(at, count, blocks, rows)
    dq, parts = [], []
    for h, (query, grad, kept) in enumerate(zip(plain_heads(q_all), plain_heads(g_all), plain_heads(exact))):
        key = kv_all[:, :128] if h < 2 else kv_all[:, 256:]
        value = kv_all[:, 128:256] if h < 2 else kv_all[:, 256:]
        delta = jnp.sum(grad.astype(F32) * kept, axis=-1, keepdims=True)
        scores = dot_columns(query, key) * SCORE - totals[:, h : h + 1]
        weights = jnp.exp(jnp.where(seen, scores, NEVER))
        g_scores = (weights * (dot_columns(grad, value) - delta)).astype(BF)
        dq.append(dot(g_scores, key) * SCORE)
        parts.append((dot_rows(g_scores, query) * SCORE, dot_rows(weights.astype(BF), grad)))
    dq = jnp.concatenate([dq[0][:, :HD], dq[1][:, HD:], dq[2][:, :HD], jnp.zeros_like(dq[2][:, :HD])], 1)
    dq = dq.astype(BF).reshape(count, rows, -1)
    acc = jnp.concatenate([parts[0][0] + parts[1][0], parts[0][1] + parts[1][1], parts[2][0] + parts[2][1]], 1)
    acc = acc.reshape(count, blocks, rows, -1)
    pieces = [dq[at[0] ^ k] for k in range(count)]
    own = jnp.concatenate([acc[at[0] ^ k, at[1]] for k in range(count)], 0)
    away = [acc[at[0] ^ k, at[1] ^ j].astype(BF) for j in range(1, blocks) for k in range(count)]
    return (*pieces, own, jnp.concatenate(away, 0))


def merge_body(count, rows, at, own, *refs):
    arrived, outs = refs[:-count], refs[-count:]
    for k in range(count):
        part = slice(k * rows, (k + 1) * rows)
        total = own[part, :]
        for ref in arrived:
            total = total + ref[part, :].astype(F32)
        outs[k][...] = total.astype(BF)


def gelu_terms(hidden):
    root = 0.7978845608028654
    square = hidden * hidden
    bend = jnp.tanh(root * hidden * (1.0 + 0.044715 * square))
    half = 0.5 * (1.0 + bend)
    slope = half + 0.5 * hidden * (1.0 - bend * bend) * root * (1.0 + 3.0 * 0.044715 * square)
    return hidden * half, slope


def g_output(extras, rows):
    return jnp.concatenate([(RESIDUAL * ref[:rows, :].astype(F32)).astype(BF) for ref in extras], axis=0)


def split_rows(values, rows, mine, other):
    mine[:rows, :] = values[:rows]
    mine[rows:, :] = values[2 * rows : 3 * rows]
    other[:rows, :] = values[rows : 2 * rows]
    other[rows:, :] = values[3 * rows :]


def middle_body(parts, rows, at, attended, vectors, fc, fc_bias, out, *refs):
    tokens, extras = refs[:parts], refs[parts : 2 * parts]
    gn_mine, gn_other, mid_mine, normed, active, g_hidden, own, att_all, proj = refs[2 * parts :]
    zero = jnp.zeros((HD, proj.shape[1]), BF)
    half = rows // 2
    low = lax.broadcasted_iota(jnp.int32, (half, 128), 1) < HD
    for k in range(parts):
        weight = extras[k][rows:, :]
        owner = at[2] ^ k
        packed = jnp.concatenate([weight[:128], zero, weight[128:]], axis=0)
        proj[rows_at(owner, 256), :] = packed
    size = rows + half
    for j in range(parts):
        for k in range(parts):
            piece = attended[j, k * size : (k + 1) * size, :]
            pair = piece[rows:].astype(F32)
            upper = jnp.where(low, 0.0, pltpu.roll(pair, HD, 1)).astype(BF)
            lower = jnp.where(low, 0.0, pair).astype(BF)
            block = block_of(at, k, rows)
            att_all[block, j * 256 : j * 256 + 128] = piece[:rows]
            att_all[block, j * 256 + 128 : (j + 1) * 256] = jnp.concatenate([upper, lower], axis=0)
    own[...] = att_all[:, pl.ds(pl.multiple_of(at[2] * 256, 256), 256)]
    branch = dot(att_all[...], proj[...]) + vectors[4:5]
    for k in range(parts):
        part = slice(k * rows, (k + 1) * rows)
        value = tokens[k][...].astype(F32) + RESIDUAL * branch[part]
        if k % 2 == 0:
            mid_mine[(k // 2) * rows : (k // 2 + 1) * rows, :] = value
        unit, _ = normalize(value)
        normed[part, :] = (unit * vectors[2:3] + vectors[3:4]).astype(BF)
    hidden = dot(normed[...], fc[...]) + fc_bias[...].astype(F32)
    value, slope = gelu_terms(hidden)
    active[...] = value.astype(BF)
    g_hidden[...] = (dot_columns(g_output(extras, rows), out[...]) * slope).astype(BF)
    split_rows(dot_columns(g_hidden[...], fc[...]), rows, gn_mine, gn_other)


def chunk_rows(at, owner, owner_rows, blocks, count, side, k):
    size = owner_rows // (blocks * count)
    return pl.ds(pl.multiple_of(owner * owner_rows + (side * count + (at[0] ^ k)) * size, 8), size)


def weights_body(parts, rows, blocks, at, normed, active, g_hidden, out, *refs):
    extras = refs[:parts]
    mine, other, *grads, sums, out_all, fc_all = refs[parts:]
    g_out = g_output(extras, rows)
    split_rows(dot(active[...], out[...]), rows, mine, other)
    out_all[...] = dot_rows(active[...], g_out)
    fc_all[...] = dot_rows(normed[...], g_hidden[...])
    sums[...] = jnp.zeros_like(sums)
    sums[0:1, :] = jnp.sum(g_out.astype(F32), axis=0, keepdims=True)
    sums[1:2, :] = jnp.sum(g_hidden[...].astype(F32), axis=0, keepdims=True)
    if blocks != 2:
        grads[0][...] = out_all[...].astype(BF)
        grads[1][...] = fc_all[...].astype(BF)
        return
    kept, away = grads
    out_rows, fc_rows = out_all.shape[0], fc_all.shape[0] // parts
    out_size, fc_size = out_rows // (2 * parts), fc_rows // (2 * parts)
    start = 0
    for k in range(parts):
        rows_kept = chunk_rows(at, 0, out_rows, 2, parts, at[1], k)
        rows_away = chunk_rows(at, 0, out_rows, 2, parts, 1 - at[1], k)
        kept[start : start + out_size, :] = out_all[rows_kept, :]
        away[start : start + out_size, :] = out_all[rows_away, :].astype(BF)
        start += out_size
        for j in range(parts):
            rows_kept = chunk_rows(at, at[2] ^ j, fc_rows, 2, parts, at[1], k)
            rows_away = chunk_rows(at, at[2] ^ j, fc_rows, 2, parts, 1 - at[1], k)
            kept[start : start + fc_size, :] = fc_all[rows_kept, :]
            away[start : start + fc_size, :] = fc_all[rows_away, :].astype(BF)
            start += fc_size


def second_norm_body(rows, at, chip_sum, arrived, mid, own_extra, x_extra, vectors, g_branch, own_middle, sums):
    add = arrived[...].astype(F32)
    grad = chip_sum[...] + jnp.concatenate([add[rows:], add[:rows]], axis=0)
    unit, scale = normalize(mid[...])
    back = norm_back(grad, unit, scale, vectors[2:3])
    sums[...] = jnp.zeros_like(sums)
    sums[0:1, :] = jnp.sum(grad * unit, axis=0, keepdims=True)
    sums[1:2, :] = jnp.sum(grad, axis=0, keepdims=True)
    g_own = back[:rows] + own_extra[:rows, :].astype(F32)
    own_middle[...] = g_own
    g_branch[:rows, :] = (RESIDUAL * g_own).astype(BF)
    g_branch[rows:, :] = (RESIDUAL * (back[rows:] + x_extra[:rows, :].astype(F32))).astype(BF)


def attended_grad_body(parts, rows, at, mine, other, proj, *refs):
    outs, (kept, g_all) = refs[:parts], refs[parts:]
    kept[:rows, :] = mine[:rows, :]
    kept[rows : 2 * rows, :] = other[:rows, :]
    kept[2 * rows : 3 * rows, :] = mine[rows:, :]
    kept[3 * rows :, :] = other[rows:, :]
    zero = jnp.zeros((HD, proj.shape[1]), BF)
    weight = jnp.concatenate([proj[:128, :], zero, proj[128:, :]], axis=0)
    g_all[...] = dot_columns(kept[...], weight).astype(BF)
    for k in range(parts):
        outs[k][...] = g_all[block_of(at, k, rows), :]


def proj_grad_body(at, attended, g_branch, proj_grad, sums):
    grad = dot_rows(attended[...], g_branch[...])
    proj_grad[...] = jnp.concatenate([grad[:128], grad[128 + HD :]], axis=0)
    sums[...] = jnp.zeros_like(sums)
    sums[0:1, :] = jnp.sum(g_branch[...].astype(F32), axis=0, keepdims=True)


def pack_wide(values, lanes):
    third = values.shape[0] // 3
    rest = values[:, lanes:]
    low = [rest[i * third : (i + 1) * third] for i in range(3)]
    low.append(jnp.zeros((third, lanes - 384), values.dtype))
    return jnp.concatenate([values[:, :lanes], jnp.concatenate(low, axis=1)], axis=0)


def first_grad_body(parts, rows, blocks, at, normed, matrix, proj_grad, *refs):
    queries, pairs = refs[:parts], refs[parts : 2 * parts]
    mine, other, *grads, sums, mixed, attn_all = refs[2 * parts :]
    for k in range(parts):
        block = block_of(at, k, rows)
        mixed[block, :256] = queries[k][...]
        mixed[block, 256:] = pairs[k][...]
    split_rows(dot_columns(mixed[...], matrix[...]), rows, mine, other)
    attn_all[...] = dot_rows(normed[...], mixed[...])
    sums[...] = jnp.zeros_like(sums)
    sums[0:1, :] = jnp.sum(mixed[...].astype(F32), axis=0, keepdims=True)
    if blocks != 2:
        grads[0][...] = attn_all[...].astype(BF)
        grads[1][...] = proj_grad[...].astype(BF)
        return
    kept, away = grads
    lanes = attn_all.shape[1]
    owner_rows = attn_all.shape[0] // parts
    size = owner_rows // (2 * parts)
    start = 0
    for k in range(parts):
        for j in range(parts):
            kept[start : start + size, :] = attn_all[chunk_rows(at, at[2] ^ j, owner_rows, 2, parts, at[1], k), :]
            part = attn_all[chunk_rows(at, at[2] ^ j, owner_rows, 2, parts, 1 - at[1], k), :]
            away[start : start + size, :] = part.astype(BF)
            start += size
        packed = size + size // 3
        part = proj_grad[chunk_rows(at, 0, owner_rows, 2, parts, at[1], k), :]
        kept[start : start + packed, :] = pack_wide(part, lanes)
        part = proj_grad[chunk_rows(at, 0, owner_rows, 2, parts, 1 - at[1], k), :]
        away[start : start + packed, :] = pack_wide(part, lanes).astype(BF)
        start += packed


def first_norm_body(rows, at, own, arrived, tokens, own_middle, vectors, input_grad, sums):
    grad = own[:rows, :] + arrived[...].astype(F32)
    unit, scale = normalize(tokens[...].astype(F32))
    back = norm_back(grad, unit, scale, vectors[0:1])
    input_grad[...] = (back + own_middle[...]).astype(BF)
    sums[...] = jnp.zeros_like(sums)
    sums[0:1, :] = jnp.sum(grad * unit, axis=0, keepdims=True)
    sums[1:2, :] = jnp.sum(grad, axis=0, keepdims=True)


def pair_sum_body(count, at, kept, arrived, *outs):
    size = kept.shape[0] // count
    for k in range(count):
        part = slice(k * size, (k + 1) * size)
        outs[k][...] = (kept[part, :] + arrived[part, :].astype(F32)).astype(outs[k].dtype)


def total_body(count, at, *refs):
    total = refs[0][...]
    for ref in refs[1:count]:
        total = total + ref[...].astype(F32)
    start = 0
    for out in refs[count:]:
        out[...] = total[start : start + out.shape[0]].astype(BF)
        start += out.shape[0]


def mlp_final_body(parts, at, *refs):
    own, away, (out_grad, fc_grad) = refs[:parts], refs[parts], refs[parts + 1 :]
    out_rows, fc_rows = out_grad.shape[0], fc_grad.shape[0]
    hidden = fc_grad.shape[1] // parts
    out_size, fc_size = out_rows // (2 * parts), fc_rows // (2 * parts)
    size = out_size + parts * fc_size
    for side in range(2):
        block = at[1] if side == 0 else 1 - at[1]
        for k in range(parts):
            piece = own[k][...] if side == 0 else away[k * size : (k + 1) * size, :]
            piece = piece.astype(F32)
            out_grad[chunk_rows(at, 0, out_rows, 2, parts, block, k), :] = piece[:out_size]
            rows = chunk_rows(at, 0, fc_rows, 2, parts, block, k)
            for j in range(parts):
                start = out_size + j * fc_size
                lanes = pl.ds(pl.multiple_of((at[2] ^ j) * hidden, 128), hidden)
                fc_grad[rows, lanes] = piece[start : start + fc_size]


def attn_final_body(parts, at, *refs):
    own, away, (attn_grad, proj_grad, kept) = refs[:parts], refs[parts], refs[parts + 1 :]
    rows_all, features = proj_grad.shape
    width = features // parts
    lanes = kept.shape[2]
    size = rows_all // (2 * parts)
    third = size // 3
    total = parts * size + size + third
    for side in range(2):
        block = at[1] if side == 0 else 1 - at[1]
        for k in range(parts):
            piece = own[k][...] if side == 0 else away[k * total : (k + 1) * total, :]
            piece = piece.astype(F32)
            rows = chunk_rows(at, 0, rows_all, 2, parts, block, k)
            for j in range(parts):
                kept[at[2] ^ j, rows, :] = piece[j * size : (j + 1) * size]
            start = parts * size
            proj_grad[rows, :lanes] = piece[start : start + size]
            low = piece[start + size :]
            proj_grad[rows, lanes:] = jnp.concatenate([low[:, i * 128 : (i + 1) * 128] for i in range(3)], axis=0)
    for g in range(parts):
        first = g * width
        attn_grad[:, first : first + width] = kept[g, :, :width]
        first += features
        attn_grad[:, first : first + width] = jnp.concatenate([kept[g, :, 256:384], kept[g, :, 512 : 512 + HD]], axis=1)
        first += features
        attn_grad[:, first : first + width] = jnp.concatenate([kept[g, :, 384:512], kept[g, :, 512 + HD :]], axis=1)


def shards(
    parts,
    ways,
    tokens,
    first_gain,
    first_bias,
    attn_weight,
    query_bias,
    value_bias,
    proj_weight,
    proj_bias,
    second_gain,
    second_bias,
    fc_weight,
    fc_bias,
    out_weight,
    out_bias,
    cotangent,
):
    rows, features = tokens.shape[1], tokens.shape[2]
    width = features // parts
    count = parts
    blocks = ways // count
    hidden = fc_weight.shape[1] // parts
    all_rows, half_rows = parts * rows, parts * rows // 2
    f = lax.axis_index("fsdp").astype(jnp.int32)
    c = lax.axis_index("ctx").astype(jnp.int32)
    a, b = c // blocks, c % blocks
    at = jnp.stack([a, b, f])

    def over_fsdp(value, k):
        return lax.ppermute(value, "fsdp", [(i, i ^ k) for i in range(parts)])

    def over_ctx(value, k):
        return lax.ppermute(value, "ctx", [(i, i ^ k) for i in range(ways)])

    def spread(value):
        across = over_fsdp(value, 2)
        return [value, over_fsdp(value, 1), across, over_fsdp(across, 1)]

    def turn_fsdp(pieces):
        return [pieces[0]] + [over_fsdp(pieces[k], k) for k in range(1, parts)]

    def turn_ctx(pieces):
        return [pieces[0]] + [over_ctx(pieces[k], k * blocks) for k in range(1, count)]

    tok = tokens[0]
    tok_all = spread(tok)
    small = jnp.stack([first_gain, first_bias, second_gain, second_bias, proj_bias, out_bias, out_bias, out_bias])
    columns = 256 + 2 * width
    pieces = call(
        partial(columns_body, parts),
        "columns",
        [shape((width, columns), BF)] * parts + [shape((width, hidden), BF)] * parts,
        at,
        attn_weight,
        fc_weight,
        small,
    )
    attn_pieces = turn_fsdp(pieces[:parts])
    fc_pieces = turn_fsdp(pieces[parts:])
    extra = spread(jnp.concatenate([cotangent[0], proj_weight], 0))

    none = jnp.zeros((128,), F32)
    vb = value_bias.astype(F32)
    bias = jnp.concatenate([query_bias.astype(F32), none[:HD], none, vb[:128], none[:HD], vb[128:]])[None]
    mixed = call(
        partial(mixed_body, parts, count),
        "mixed",
        [shape((all_rows, features), BF), shape((features, columns), BF), shape((8, features), F32)]
        + [shape((rows, 256), BF)] * count
        + [shape((rows, 384), BF)] * count,
        at,
        bias,
        *tok_all,
        *attn_pieces,
        scratch=[pltpu.VMEM((all_rows, columns), BF)],
    )
    normed, attn_matrix, vectors = mixed[:3]

    pairs = turn_ctx(mixed[3 + count :])
    queries = turn_ctx(mixed[3 : 3 + count])
    joined = jnp.concatenate(pairs, 0)
    partners = [over_ctx(joined, j) for j in range(1, blocks)]
    small_blocks = blocks * count * rows <= 1024
    if small_blocks:
        kept = call(
            partial(attend_body, count, blocks, rows),
            "attend",
            [shape((rows + rows // 2, 128), BF)] * count
            + [
                shape((count * rows, 256), F32),
                shape((count * rows, 128), F32),
                shape((count * rows, 256), BF),
                shape((count * blocks * rows, 384), BF),
                shape((features, hidden), BF),
            ],
            at,
            *queries,
            *pairs,
            *partners,
            *fc_pieces,
        )
        kept, fc_matrix = kept[:-1], kept[-1]
    else:
        kept = plain_attend(count, blocks, rows, at, queries, pairs, partners)
        fc_matrix = call(join_body, "join", [shape((features, hidden), BF)], at, *fc_pieces)[0]
    att_pieces, state = turn_ctx(kept[:count]), kept[count:]
    attended_all = lax.all_gather(jnp.concatenate(att_pieces, 0), "fsdp")

    gn_mine, gn_other, mid_mine, normed_two, active, g_hidden, attended = call(
        partial(middle_body, parts, rows),
        "middle",
        [shape((half_rows, features), F32)] * 3
        + [shape((all_rows, features), BF), shape((all_rows, hidden), BF), shape((all_rows, hidden), BF)]
        + [shape((all_rows, 256), BF)],
        at,
        attended_all,
        vectors,
        fc_matrix,
        fc_bias[None],
        out_weight,
        *tok_all,
        *extra,
        scratch=[pltpu.VMEM((all_rows, parts * 256), BF), pltpu.VMEM((parts * 256, features), BF)],
    )
    chip_sum = gn_mine + over_fsdp(gn_other, 1)
    chip_low = chip_sum.astype(BF)
    arrived = over_fsdp(chip_low, 2)
    if blocks == 2:
        chunk = hidden // (2 * count) + features // (2 * count)
        mlp_grads = [shape((count * chunk, features), F32), shape((count * chunk, features), BF)]
    else:
        mlp_grads = [shape((hidden, features), BF), shape((features, hidden), BF)]
    mine, other, *mlp_grads, sums_mlp = call(
        partial(weights_body, parts, rows, blocks),
        "mlp_weights",
        [shape((half_rows, features), F32)] * 2 + mlp_grads + [shape((8, features), F32)],
        at,
        normed_two,
        active,
        g_hidden,
        out_weight,
        *extra,
        scratch=[pltpu.VMEM((hidden, features), F32), pltpu.VMEM((features, hidden), F32)],
        after=[chip_low],
    )
    g_branch, own_middle, sums_two = call(
        partial(second_norm_body, rows),
        "second_norm",
        [shape((half_rows, features), BF), shape((rows, features), F32), shape((8, features), F32)],
        at,
        chip_sum,
        arrived,
        mid_mine,
        extra[0],
        extra[2],
        vectors,
    )
    grads = call(
        partial(attended_grad_body, parts, rows),
        "attended_grad",
        [shape((rows, 256), BF)] * parts + [shape((all_rows, features), BF)],
        at,
        g_branch,
        over_fsdp(g_branch, 1),
        proj_weight,
        scratch=[pltpu.VMEM((all_rows, 256), BF)],
    )
    g_pieces, g_branch_all = turn_ctx(grads[:parts]), grads[parts]
    proj_grad, sums_proj = call(
        proj_grad_body,
        "proj_weight_grad",
        [shape((width, features), F32), shape((8, features), F32)],
        at,
        attended,
        g_branch_all,
    )
    if small_blocks:
        back = call(
            partial(attend_back_body, count, blocks, rows),
            "attend_back",
            [shape((rows, 256), BF)] * count
            + [shape((count * rows, 384), F32), shape(((blocks - 1) * count * rows, 384), BF)],
            at,
            *g_pieces,
            state[2],
            state[3],
            state[0],
            state[1],
            scratch=[
                pltpu.VMEM((count * rows, 256), BF),
                pltpu.VMEM((count * rows, 256), BF),
                pltpu.VMEM((count * blocks * rows, 384), F32),
            ],
        )
    else:
        back = plain_attend_back(count, blocks, rows, at, g_pieces, state[2], state[3], state[0], state[1])
    dq, own, away = back[:count], back[count], back[count + 1]
    stack = count * rows
    from_partners = [over_ctx(away[(j - 1) * stack : j * stack], j) for j in range(1, blocks)]
    dkv = call(partial(merge_body, count, rows), "merge", [shape((rows, 384), BF)] * count, at, own, *from_partners)
    dq, dkv = turn_ctx(dq), turn_ctx(dkv)
    if blocks == 2:
        size = width // (2 * count)
        chunk = parts * size + size + size // 3
        attn_grads = [shape((count * chunk, columns), F32), shape((count * chunk, columns), BF)]
    else:
        attn_grads = [shape((features, columns), BF), shape((width, features), BF)]
    g1_mine, g1_other, *attn_grads, sums_attn = call(
        partial(first_grad_body, parts, rows, blocks),
        "first_grad",
        [shape((half_rows, features), F32)] * 2 + attn_grads + [shape((8, columns), F32)],
        at,
        normed,
        attn_matrix,
        proj_grad,
        *dq,
        *dkv,
        scratch=[pltpu.VMEM((all_rows, columns), BF), pltpu.VMEM((features, columns), F32)],
    )
    first_sum = g1_mine + over_fsdp(g1_other, 1)
    input_grad, sums_one = call(
        partial(first_norm_body, rows),
        "first_norm",
        [shape((rows, features), BF), shape((8, features), F32)],
        at,
        first_sum,
        over_fsdp(first_sum[rows:].astype(BF), 2),
        tok,
        own_middle,
        vectors,
    )
    out_sum = mine + over_fsdp(other, 1)
    output = out_sum[:rows] + over_fsdp(out_sum[rows:].astype(BF), 2).astype(F32) + vectors[5:6]
    block_out = (mid_mine[:rows] + RESIDUAL * output).astype(BF)

    sums_one = sums_one[:2] + over_fsdp(sums_one[:2], 1)
    sums_one = sums_one + over_fsdp(sums_one, 2)
    sums_two = sums_two[:2] + over_fsdp(sums_two[:2], 1)

    def own_slice(row):
        return lax.dynamic_slice_in_dim(row, f * width, width, 0)

    vector_sums = jnp.concatenate(
        [
            own_slice(sums_one[0]),
            own_slice(sums_one[1]),
            sums_attn[0, :width],
            jnp.concatenate([sums_attn[0, 384:512], sums_attn[0, 512 + HD :]]),
            own_slice(sums_proj[0]),
            own_slice(sums_two[0]),
            own_slice(sums_two[1]),
            own_slice(sums_mlp[0]),
            sums_mlp[1],
        ]
    ).reshape(-1, 128)
    if blocks == 2:
        vector_sums = vector_sums + over_ctx(vector_sums, 1)
        vector_sums = sum((over_ctx(vector_sums, 2 * k) for k in range(1, count)), vector_sums)
    else:
        vector_sums = lax.psum(vector_sums, "ctx")
    vector_sums = vector_sums.reshape(-1)
    slices = [vector_sums[i * width : (i + 1) * width] for i in range(8)]
    fc_bias_grad = vector_sums[8 * width :]

    if blocks == 2:

        def summed(name, kept, away, cuts):
            size, lanes = kept.shape[0] // count, kept.shape[1]
            sent = call(
                partial(pair_sum_body, count),
                name + "_pair",
                [shape((size, lanes), F32)] + [shape((size, lanes), BF)] * (count - 1),
                at,
                kept,
                over_ctx(away, 1),
            )
            return call(
                partial(total_body, count),
                name + "_total",
                [shape((cut, lanes), BF) for cut in cuts],
                at,
                *turn_ctx(sent),
            )

        def gathered(piece):
            pieces = [piece] + [over_ctx(piece, 2 * k) for k in range(1, count)]
            return (*pieces, over_ctx(jnp.concatenate(pieces, 0), 1))

        out_size, fc_size = hidden // (2 * count), width // (2 * count)
        out_part, *fc_parts = summed("mlp", *mlp_grads, [out_size] + [fc_size] * parts)
        out_weight_grad, fc_weight_grad = call(
            partial(mlp_final_body, parts),
            "mlp_final",
            [shape((hidden, features), F32), shape((width, parts * hidden), F32)],
            at,
            *gathered(jnp.concatenate([out_part, *turn_fsdp(fc_parts)], 0)),
        )
        *attn_parts, proj_part = summed("attn", *attn_grads, [size] * parts + [size + size // 3])
        attn_weight_grad, proj_weight_grad = call(
            partial(attn_final_body, parts),
            "attn_final",
            [shape((width, 3 * features), F32), shape((width, features), F32)],
            at,
            *gathered(jnp.concatenate([*turn_fsdp(attn_parts), proj_part], 0)),
            scratch=[pltpu.VMEM((parts, width, columns), F32)],
        )
    else:

        def over_all(value):
            part = lax.psum_scatter(value, "ctx", scatter_dimension=1, tiled=True)
            return lax.all_gather(part, "ctx", axis=1, tiled=True)

        out_weight_grad = over_all(mlp_grads[0]).astype(F32)
        fc_grad = over_all(mlp_grads[1]).reshape(parts, width, hidden)
        fc_grad = lax.all_to_all(fc_grad, "fsdp", split_axis=0, concat_axis=0)
        fc_weight_grad = fc_grad.transpose(1, 0, 2).reshape(width, parts * hidden).astype(F32)
        proj_weight_grad = over_all(attn_grads[1]).astype(F32)
        attn_all = over_all(attn_grads[0]).reshape(parts, width, columns)
        attn_all = lax.all_to_all(attn_all, "fsdp", split_axis=0, concat_axis=0).transpose(1, 0, 2)
        q = attn_all[:, :, :width]
        k = jnp.concatenate([attn_all[:, :, 256:384], attn_all[:, :, 512 : 512 + HD]], 2)
        v = jnp.concatenate([attn_all[:, :, 384:512], attn_all[:, :, 512 + HD :]], 2)
        attn_weight_grad = jnp.stack([q, k, v], 1).reshape(width, 3 * features).astype(F32)
    return (
        block_out[None],
        input_grad[None],
        slices[0],
        slices[1],
        attn_weight_grad,
        slices[2],
        slices[3],
        proj_weight_grad,
        slices[4],
        slices[5],
        slices[6],
        fc_weight_grad,
        fc_bias_grad,
        out_weight_grad,
        slices[7],
    )


def solution(mesh):
    rows, row, matrix = P("fsdp", "ctx", None), P("fsdp"), P("fsdp", None)
    return jax.shard_map(
        partial(shards, mesh.shape["fsdp"], mesh.shape["ctx"]),
        mesh=mesh,
        in_specs=(
            rows, row, row, matrix, row, row, matrix, row, row, row, matrix, row, matrix, row, rows,
        ),
        out_specs=(
            rows, rows, row, row, matrix, row, row, matrix, row, row, row, matrix, row, matrix, row,
        ),
        check_vma=False,
    )
```

time: 427 us -> 300 us (0.70); the launches traced: 422 us -> 299 us
  blocking collectives: 117 us -> 9.52 us
  starting transfers between devices: 46.1 us -> 67.1 us
  between operations: 15.4 us -> 1.27 us
  local copies, waits for them, and re-layouts: 39.3 us -> 25.6 us
  waiting for transfers between devices: 155 us -> 143 us
  Pallas kernels: 38.6 us -> 50 us
  other arithmetic: 10.1 us -> 2.88 us
    all_gather x3 -> x1, blocking collectives: 81.7 us -> 9.52 us  [shards(): attended_all = lax.all_gather(jnp.concatenate(att_pieces, 0), 'fsdp')]
    ppermute x20 -> x40, waiting for transfers between devices: 44.6 us -> 105 us  [over_ctx(): return lax.ppermute(value, 'ctx', [(i, i ^ k) for i in range(ways)])]
    reduce_scatter x3 -> x0, waiting for transfers between devices: 37.7 us -> none  [reduce_ctx(): return lax.psum_scatter(value, 'ctx', scatter_dimension=0, tiled=False)]
    psum x1 -> x0, blocking collectives: 35.5 us -> none  [shards(): vector_sums = lax.psum(vector_sums.reshape(-1, 128), 'ctx').reshape(-1)]
    all_gather x3 -> x0, waiting for transfers between devices: 23.4 us -> none  [the longest x1 14.7 us: shards(): extra = lax.all_gather(jnp.concatenate([cot, proj_weight], 0), 'fsdp')]
    ppermute x20 -> x40, starting transfers between devices: 30.1 us -> 49.8 us  [over_ctx(): return lax.ppermute(value, 'ctx', [(i, i ^ k) for i in range(ways)])]
    pallas_call x12 -> x18, Pallas kernels: 38.6 us -> 50 us  [call(): pl.pallas_call(run, name=name, out_shape=outs, in_specs=[smem] + [vmem] *...]
    ppermute x16 -> x28, starting transfers between devices: 8.89 us -> 17.3 us  [over_fsdp(): return lax.ppermute(value, 'fsdp', [(i, i ^ k) for i in range(parts)])]
  transfers between devices with their start and end apart: 44 -> 68, of which waited for: 26 -> 30; matrix products, arithmetic and copies ran while one was open for 6% -> 7% of each run, Pallas kernels for 4% -> 12%
where the time goes in v2:
time: 300 us; the launch traced here: 299 us
  waiting for transfers between devices  143 us (48%)
  starting transfers between devices  67.1 us (22%)
  Pallas kernels  50 us (17%)
  local copies, waits for them, and re-layouts  25.6 us (9%)
  blocking collectives  9.52 us (3%)
    ppermute x40, waiting for transfers between devices, over_ctx(): return lax.ppermute(value, 'ctx', [(i, i ^ k) for i in range(ways)])  105 us
    pallas_call x18, Pallas kernels, call(): pl.pallas_call(run, name=name, out_shape=outs, in_specs=[smem] + [vmem] *...  50 us
    ppermute x40, starting transfers between devices, over_ctx(): return lax.ppermute(value, 'ctx', [(i, i ^ k) for i in range(ways)])  49.8 us
    ppermute x28, waiting for transfers between devices, over_fsdp(): return lax.ppermute(value, 'fsdp', [(i, i ^ k) for i in range(parts)])  38 us
    ppermute x28, starting transfers between devices, over_fsdp(): return lax.ppermute(value, 'fsdp', [(i, i ^ k) for i in range(parts)])  17.3 us
    unnamed x70, local copies, waits for them, and re-layouts  15.2 us
    all_gather x1, blocking collectives, shards(): attended_all = lax.all_gather(jnp.concatenate(att_pieces, 0), 'fsdp')  9.52 us
  transfers between devices with their start and end apart: 68, of which 30 were waited for; matrix products, arithmetic and copies ran while one was open for 7% of the time, Pallas kernels for 12%

profile of v2, /device:TPU:0, one launch (start us, length us, event | category | flops | bytes accessed | tf_op | source)
XLA Modules:
  0.0 299.2 jit_solution(9200137749820177063)
XLA Ops:
  0.7 3.0 %collective-permute-start.1 = (bf16[128,768]{1,0:T(8,128)(2,1)}, bf16[128,768]{1,0:T(8,128)(2,1)S(1)}, u32[]{:S(2)}, u32[]{:S(2)}) collective-permute-start(bf16[128,768]{1,0:T(8,128)(2,1)} %bitcast.27), channel_id=1, source_target_pairs={{0,2},{1,3},{2,0},{3,1},{4,6},{5,7},{6,4},{7,5},{8,10},{9,11},{10,... | collective-permute-start | bytes 589832 | tf_op jit(solution)/shard_map/ppermute | solution.py:594
  15.6 5.7 %collective-permute-done.4.refs_8_ = bf16[192,640]{1,0:T(8,128)(2,1)S(1)} collective-permute-done((bf16[192,640]{1,0:T(8,128)(2,1)}, bf16[192,640]{1,0:T(8,128)(2,1)S(1)}, u32[]{:S(2)}, u32[]{:S(2)}) %collective-permute-start.4) | collective-permute-done | bytes 245792 | tf_op jit(solution)/shard_map/ppermute | solution.py:594
  21.3 4.5 %collective-permute-done.5.refs_9_ = bf16[192,640]{1,0:T(8,128)(2,1)S(1)} collective-permute-done((bf16[192,640]{1,0:T(8,128)(2,1)}, bf16[192,640]{1,0:T(8,128)(2,1)S(1)}, u32[]{:S(2)}, u32[]{:S(2)}) %collective-permute-start.5) | collective-permute-done | bytes 245792 | tf_op jit(solution)/shard_map/ppermute | solution.py:594
  33.9 6.3 %collective-permute-done.10.refs_7_ = bf16[128,384]{1,0:T(8,128)(2,1)S(1)} collective-permute-done((bf16[128,384]{1,0:T(8,128)(2,1)S(1)}, bf16[128,384]{1,0:T(8,128)(2,1)S(1)}, u32[]{:S(2)}, u32[]{:S(2)}) %collective-permute-start.10) | collective-permute-done | bytes 98336 | tf_op jit(solution)/shard_map/ppermute | solution.py:597
  45.6 7.8 %collective-permute-done.14.refs_12_ = bf16[192,768]{1,0:T(8,128)(2,1)S(1)} collective-permute-done((bf16[192,768]{1,0:T(8,128)(2,1)S(1)}, bf16[192,768]{1,0:T(8,128)(2,1)S(1)}, u32[]{:S(2)}, u32[]{:S(2)}) %collective-permute-start.14) | collective-permute-done | bytes 294944 | tf_op jit(solution)/shard_map/ppermute | solution.py:594
  54.6 3.1 %collective-permute-done.15.refs_13_ = bf16[192,768]{1,0:T(8,128)(2,1)S(1)} collective-permute-done((bf16[192,768]{1,0:T(8,128)(2,1)S(1)}, bf16[192,768]{1,0:T(8,128)(2,1)S(1)}, u32[]{:S(2)}, u32[]{:S(2)}) %collective-permute-start.15) | collective-permute-done | bytes 294944 | tf_op jit(solution)/shard_map/ppermute | solution.py:594
  64.3 6.5 %attend.1 = (bf16[192,128]{1,0:T(8,128)(2,1)S(1)}, bf16[192,128]{1,0:T(8,128)(2,1)S(1)}, bf16[192,128]{1,0:T(8,128)(2,1)S(1)}, bf16[192,128]{1,0:T(8,128)(2,1)S(...) custom-call(s32[3]{0:T(128)S(1)} %pad_add_fusion.refs_0_, ...), custom_call_target="tpu_custom_call" | custom-call | tf_op jit(solution)/shard_map/attend/pallas_call | solution.py:34
  76.6 2.9 collective-permute-done.18
  79.6 9.5 %all-gather = bf16[3072,128]{1,0:T(8,128)(2,1)} all-gather(bf16[768,128]{1,0:T(8,128)(2,1)S(1)} %pad_maximum_fusion.2), channel_id=2, replica_groups=mesh['ctx'=8,'fsdp'=4] {'fsdp'}, dimensions={0}, use_global_device_ids=true | all-gather | bytes 983040 | tf_op jit(solution)/shard_map/all_gather | solution.py:671
  89.1 7.0 %middle.1 = (f32[256,768]{1,0:T(8,128)S(1)}, f32[256,768]{1,0:T(8,128)}, f32[256,768]{1,0:T(8,128)}, bf16[512,768]{1,0:T(8,128)(2,1)}, bf16[512,768]{1,0:T(8,128...) custom-call(s32[3]{0:T(128)S(1)} %pad_add_fusion.refs_0_, bf16[4,768,128]{2,1,0:T(8,128)(2,1)} %bitcast.32, ...), custom_call_target="tpu_custom_call" | custom-call | tf_op jit(solution)/shard_map/middle/pallas_call | solution.py:34
  99.8 11.1 %collective-permute-done.25.refs_2_ = bf16[256,768]{1,0:T(8,128)(2,1)S(1)} collective-permute-done((bf16[256,768]{1,0:T(8,128)(2,1)S(1)}, bf16[256,768]{1,0:T(8,128)(2,1)S(1)}, u32[]{:S(2)}, u32[]{:S(2)}) %collective-permute-start.25) | collective-permute-done | bytes 393248 | tf_op jit(solution)/shard_map/ppermute | solution.py:594
  112.8 6.1 %mlp_weights.1 = (f32[256,768]{1,0:T(8,128)S(1)}, f32[256,768]{1,0:T(8,128)S(1)}, f32[768,768]{1,0:T(8,128)}, bf16[768,768]{1,0:T(8,128)(2,1)}, f32[8,768]{1,0:T(8,128)S(1)}) custom-call(s32[3]{0:T(128)S(1)} %pad_add_fusion.refs_0_, bf16[512,768]{1,0:T(8,128)(2,1)} %get-tuple-element.127.refs_1_, bf16[512,768]{1,0:T(8,128)(2,1)} %get-tuple-element.128.refs_2_, ...), custom_call_target="tpu_custom_call" | custom-call | tf_op jit(solution)/shard_map/mlp_weights/pallas_call | solution.py:34
  136.2 5.2 %attend_back.1 = (bf16[128,256]{1,0:T(8,128)(2,1)S(1)}, bf16[128,256]{1,0:T(8,128)(2,1)S(1)}, bf16[128,256]{1,0:T(8,128)(2,1)S(1)}, bf16[128,256]{1,0:T(8,128)(2...) custom-call(s32[3]{0:T(128)S(1)} %pad_add_fusion.refs_0_, ...), custom_call_target="tpu_custom_call" | custom-call | tf_op jit(solution)/shard_map/attend_back/pallas_call | solution.py:34
  145.6 4.7 %collective-permute-done.57.refs_2_ = bf16[768,768]{1,0:T(8,128)(2,1)S(1)} collective-permute-done((bf16[768,768]{1,0:T(8,128)(2,1)}, bf16[768,768]{1,0:T(8,128)(2,1)S(1)}, u32[]{:S(2)}, u32[]{:S(2)}) %collective-permute-start.57) | collective-permute-done | bytes 1179680 | tf_op jit(solution)/shard_map/ppermute | solution.py:597
  154.2 4.0 %collective-permute-done.33.refs_2_ = bf16[512,384]{1,0:T(8,128)(2,1)S(1)} collective-permute-done((bf16[512,384]{1,0:T(8,128)(2,1)S(1)}, bf16[512,384]{1,0:T(8,128)(2,1)S(1)}, u32[]{:S(2)}, u32[]{:S(2)}) %collective-permute-start.33) | collective-permute-done | bytes 393248 | tf_op jit(solution)/shard_map/ppermute | solution.py:597
  165.4 15.0 %collective-permute-done.34.refs_9_ = bf16[128,384]{1,0:T(8,128)(2,1)S(1)} collective-permute-done((bf16[128,384]{1,0:T(8,128)(2,1)S(1)}, bf16[128,384]{1,0:T(8,128)(2,1)S(1)}, u32[]{:S(2)}, u32[]{:S(2)}) %collective-permute-start.34) | collective-permute-done | bytes 98336 | tf_op jit(solution)/shard_map/ppermute | solution.py:597
  182.8 11.9 %collective-permute-done.35.refs_10_ = bf16[128,384]{1,0:T(8,128)(2,1)S(1)} collective-permute-done((bf16[128,384]{1,0:T(8,128)(2,1)S(1)}, bf16[128,384]{1,0:T(8,128)(2,1)S(1)}, u32[]{:S(2)}, u32[]{:S(2)}) %collective-permute-start.35) | collective-permute-done | bytes 98336 | tf_op jit(solution)/shard_map/ppermute | solution.py:597
  194.7 4.1 %first_grad.1 = (f32[256,768]{1,0:T(8,128)S(1)}, f32[256,768]{1,0:T(8,128)S(1)}, f32[512,640]{1,0:T(8,128)}, bf16[512,640]{1,0:T(8,128)(2,1)S(1)}, f32[8,640]{1,0:T(8,128)S(1)}) custom-call(s32[3]{0:T(128)S(1)} %pad_add_fusion.refs_0_, bf16[512,768]{1,0:T(8,128)(2,1)} %copy-done.6, bf16[768,640]{1,0:T(8,128)(2,1)} %get-tuple-element.135.refs_2_, ...), custom_call_target="tpu_custom_call" | custom-call | tf_op jit(solution)/shard_map/first_grad/pallas_call | solution.py:34
  211.5 4.4 %collective-permute-done.64.refs_2_ = bf16[192,768]{1,0:T(8,128)(2,1)S(1)} collective-permute-done((bf16[192,768]{1,0:T(8,128)(2,1)S(1)}, bf16[192,768]{1,0:T(8,128)(2,1)S(1)}, u32[]{:S(2)}, u32[]{:S(2)}) %collective-permute-start.64) | collective-permute-done | bytes 294944 | tf_op jit(solution)/shard_map/ppermute | solution.py:597
  220.2 21.1 %collective-permute-done.65.refs_3_ = bf16[192,768]{1,0:T(8,128)(2,1)S(1)} collective-permute-done((bf16[192,768]{1,0:T(8,128)(2,1)S(1)}, bf16[192,768]{1,0:T(8,128)(2,1)S(1)}, u32[]{:S(2)}, u32[]{:S(2)}) %collective-permute-start.65) | collective-permute-done | bytes 294944 | tf_op jit(solution)/shard_map/ppermute | solution.py:597
  264.5 5.8 %collective-permute-done.42 = f32[18,128]{1,0:T(8,128)S(1)} collective-permute-done((f32[18,128]{1,0:T(8,128)S(1)}, f32[18,128]{1,0:T(8,128)S(1)}, u32[]{:S(2)}, u32[]{:S(2)}) %collective-permute-start.42) | collective-permute-done | bytes 9248 | tf_op jit(solution)/shard_map/ppermute | solution.py:597
  274.7 3.7 %collective-permute-done.54.refs_3_ = bf16[128,640]{1,0:T(8,128)(2,1)S(1)} collective-permute-done((bf16[128,640]{1,0:T(8,128)(2,1)S(1)}, bf16[128,640]{1,0:T(8,128)(2,1)S(1)}, u32[]{:S(2)}, u32[]{:S(2)}) %collective-permute-start.54) | collective-permute-done | bytes 163872 | tf_op jit(solution)/shard_map/ppermute | solution.py:597
  283.4 3.0 %mlp_final.1 = (f32[768,768]{1,0:T(8,128)}, f32[192,3072]{1,0:T(8,128)}) custom-call(s32[3]{0:T(128)S(1)} %pad_add_fusion.refs_0_, bf16[192,768]{1,0:T(8,128)(2,1)S(1)} %get-tuple-element.200.refs_1_, bf16[192,768]{1,0:T(8,128)(2,1)S(1)} %collective-permute-done.64.refs_2_, bf16[192,768]{1,0:T(8,128)(2,1)S(1)} %collective-permute-done.65.refs_3_, ...), custom_call_target="tpu_custom_call" | custom-call | tf_op jit(solution)/shard_map/mlp_final/pallas_call | solution.py:34
  286.4 10.1 %collective-permute-done.56.refs_5_ = bf16[512,640]{1,0:T(8,128)(2,1)S(1)} collective-permute-done((bf16[512,640]{1,0:T(8,128)(2,1)}, bf16[512,640]{1,0:T(8,128)(2,1)S(1)}, u32[]{:S(2)}, u32[]{:S(2)}) %collective-permute-start.56) | collective-permute-done | bytes 655392 | tf_op jit(solution)/shard_map/ppermute | solution.py:597
  (248 shorter events, 131.2 us)
Async XLA Ops:
  33.4 28.6 %collective-permute-start.20 = (bf16[320,768]{1,0:T(8,128)(2,1)S(1)}, bf16[320,768]{1,0:T(8,128)(2,1)S(1)}, u32[]{:S(2)}, u32[]{:S(2)}) collective-permute-start(bf16[320,768]{1,0:T(8,128)(2,1)S(1)} %pad_maximum_fusion.refs_10_.refs_5_.refs_4_), channel_id=1, source_target_pairs={{0,2},{1,3},{2,0},{3,1},{4,6},{5,7},{6,4},{7,5},{8,10},{9,11},{10,... | collective-permute-start | bytes 1474568 | tf_op jit(solution)/shard_map/ppermute | solution.py:594
  40.3 24.0 %collective-permute-start.12 = (bf16[512,384]{1,0:T(8,128)(2,1)S(1)}, bf16[512,384]{1,0:T(8,128)(2,1)S(1)}, u32[]{:S(2)}, u32[]{:S(2)}) collective-permute-start(bf16[512,384]{1,0:T(8,128)(2,1)S(1)} %pad_maximum_fusion.1), channel_id=1, source_target_pairs={{0,4},{4,0},{8,12},{12,8},{16,20},{20,16},{24,28},{28,24},{1,5},{5... | collective-permute-start | bytes 1179656 | tf_op jit(solution)/shard_map/ppermute | solution.py:597
  43.7 16.8 %collective-permute-start.6 = (bf16[128,256]{1,0:T(8,128)(2,1)S(1)}, bf16[128,256]{1,0:T(8,128)(2,1)S(1)}, u32[]{:S(2)}, u32[]{:S(2)}) collective-permute-start(bf16[128,256]{1,0:T(8,128)(2,1)S(1)} %get-tuple-element.109), channel_id=1, source_target_pairs={{0,8},{4,12},{8,0},{12,4},{16,24},{20,28},{24,16},{28,20},{1,9},{5... | collective-permute-start | bytes 196616 | tf_op jit(solution)/shard_map/ppermute | solution.py:597
  60.5 28.5 %collective-permute-start.19 = (bf16[320,768]{1,0:T(8,128)(2,1)S(1)}, bf16[320,768]{1,0:T(8,128)(2,1)S(1)}, u32[]{:S(2)}, u32[]{:S(2)}) collective-permute-start(bf16[320,768]{1,0:T(8,128)(2,1)S(1)} %pad_maximum_fusion.refs_10_.refs_5_.refs_4_), channel_id=1, source_target_pairs={{0,1},{1,0},{2,3},{3,2},{4,5},{5,4},{6,7},{7,6},{8,9},{9,8},{10,11... | collective-permute-start | bytes 1474568 | tf_op jit(solution)/shard_map/ppermute | solution.py:594
  62.1 27.0 %collective-permute-start.21 = (bf16[320,768]{1,0:T(8,128)(2,1)S(1)}, bf16[320,768]{1,0:T(8,128)(2,1)S(1)}, u32[]{:S(2)}, u32[]{:S(2)}) collective-permute-start(bf16[320,768]{1,0:T(8,128)(2,1)S(1)} %collective-permute-done.20.refs_12_.refs_7_.refs_5_), channel_id=1, source_target_pairs={{0,1},{1,0},{2,3},{3,2},{4,5},{5,4},{6,7},{7,6},{8,9},{9,8},{10,11... | collective-permute-start | bytes 1474568 | tf_op jit(solution)/shard_map/ppermute | solution.py:594
  121.3 29.0 %collective-permute-start.57 = (bf16[768,768]{1,0:T(8,128)(2,1)}, bf16[768,768]{1,0:T(8,128)(2,1)S(1)}, u32[]{:S(2)}, u32[]{:S(2)}) collective-permute-start(bf16[768,768]{1,0:T(8,128)(2,1)} %get-tuple-element.181), channel_id=1, source_target_pairs={{0,4},{4,0},{8,12},{12,8},{16,20},{20,16},{24,28},{28,24},{1,5},{5... | collective-permute-start | bytes 3538952 | tf_op jit(solution)/shard_map/ppermute | solution.py:597
  122.9 19.9 %collective-permute-start.23 = (f32[256,768]{1,0:T(8,128)}, f32[256,768]{1,0:T(8,128)S(1)}, u32[]{:S(2)}, u32[]{:S(2)}) collective-permute-start(f32[256,768]{1,0:T(8,128)} %copy-done.19), channel_id=1, source_target_pairs={{0,1},{1,0},{2,3},{3,2},{4,5},{5,4},{6,7},{7,6},{8,9},{9,8},{10,11... | collective-permute-start | bytes 2359304 | tf_op jit(solution)/shard_map/ppermute | solution.py:594
  125.4 16.7 %collective-permute-start.41 = (f32[2,768]{1,0:T(2,128)S(1)}, f32[2,768]{1,0:T(2,128)S(1)}, u32[]{:S(2)}, u32[]{:S(2)}) collective-permute-start(f32[2,768]{1,0:T(2,128)S(1)} %slice.105), channel_id=1, source_target_pairs={{0,1},{1,0},{2,3},{3,2},{4,5},{5,4},{6,7},{7,6},{8,9},{9,8},{10,11... | collective-permute-start | bytes 18440 | tf_op jit(solution)/shard_map/ppermute | solution.py:594
  141.5 16.7 %collective-permute-start.33 = (bf16[512,384]{1,0:T(8,128)(2,1)S(1)}, bf16[512,384]{1,0:T(8,128)(2,1)S(1)}, u32[]{:S(2)}, u32[]{:S(2)}) collective-permute-start(bf16[512,384]{1,0:T(8,128)(2,1)S(1)} %get-tuple-element.153), channel_id=1, source_target_pairs={{0,4},{4,0},{8,12},{12,8},{16,20},{20,16},{24,28},{28,24},{1,5},{5... | collective-permute-start | bytes 1179656 | tf_op jit(solution)/shard_map/ppermute | solution.py:597
  143.2 20.8 %collective-permute-start.24 = (bf16[128,768]{1,0:T(8,128)(2,1)S(1)}, bf16[128,768]{1,0:T(8,128)(2,1)S(1)}, u32[]{:S(2)}, u32[]{:S(2)}) collective-permute-start(bf16[128,768]{1,0:T(8,128)(2,1)S(1)} %slice.160), channel_id=1, source_target_pairs={{0,2},{1,3},{2,0},{3,1},{4,6},{5,7},{6,4},{7,5},{8,10},{9,11},{10,... | collective-permute-start | bytes 589832 | tf_op jit(solution)/shard_map/ppermute | solution.py:594
  158.2 42.1 %collective-permute-start.58 = (bf16[192,768]{1,0:T(8,128)(2,1)S(1)}, bf16[192,768]{1,0:T(8,128)(2,1)S(1)}, u32[]{:S(2)}, u32[]{:S(2)}) collective-permute-start(bf16[192,768]{1,0:T(8,128)(2,1)S(1)} %get-tuple-element.183), channel_id=1, source_target_pairs={{0,8},{4,12},{8,0},{12,4},{16,24},{20,28},{24,16},{28,20},{1,9},{5... | collective-permute-start | bytes 884744 | tf_op jit(solution)/shard_map/ppermute | solution.py:597
  158.8 41.5 %collective-permute-start.59 = (bf16[192,768]{1,0:T(8,128)(2,1)S(1)}, bf16[192,768]{1,0:T(8,128)(2,1)S(1)}, u32[]{:S(2)}, u32[]{:S(2)}) collective-permute-start(bf16[192,768]{1,0:T(8,128)(2,1)S(1)} %get-tuple-element.184), channel_id=1, source_target_pairs={{0,16},{4,20},{8,24},{12,28},{16,0},{20,4},{24,8},{28,12},{1,17},{... | collective-permute-start | bytes 884744 | tf_op jit(solution)/shard_map/ppermute | solution.py:597
  160.4 39.9 %collective-permute-start.60 = (bf16[192,768]{1,0:T(8,128)(2,1)S(1)}, bf16[192,768]{1,0:T(8,128)(2,1)S(1)}, u32[]{:S(2)}, u32[]{:S(2)}) collective-permute-start(bf16[192,768]{1,0:T(8,128)(2,1)S(1)} %get-tuple-element.185), channel_id=1, source_target_pairs={{0,24},{4,28},{8,16},{12,20},{16,8},{20,12},{24,0},{28,4},{1,25},{... | collective-permute-start | bytes 884744 | tf_op jit(solution)/shard_map/ppermute | solution.py:597
  163.3 17.1 %collective-permute-start.34 = (bf16[128,384]{1,0:T(8,128)(2,1)S(1)}, bf16[128,384]{1,0:T(8,128)(2,1)S(1)}, u32[]{:S(2)}, u32[]{:S(2)}) collective-permute-start(bf16[128,384]{1,0:T(8,128)(2,1)S(1)} %get-tuple-element.155), channel_id=1, source_target_pairs={{0,8},{4,12},{8,0},{12,4},{16,24},{20,28},{24,16},{28,20},{1,9},{5... | collective-permute-start | bytes 294920 | tf_op jit(solution)/shard_map/ppermute | solution.py:597
  163.9 30.7 %collective-permute-start.35 = (bf16[128,384]{1,0:T(8,128)(2,1)S(1)}, bf16[128,384]{1,0:T(8,128)(2,1)S(1)}, u32[]{:S(2)}, u32[]{:S(2)}) collective-permute-start(bf16[128,384]{1,0:T(8,128)(2,1)S(1)} %get-tuple-element.156), channel_id=1, source_target_pairs={{0,16},{4,20},{8,24},{12,28},{16,0},{20,4},{24,8},{28,12},{1,17},{... | collective-permute-start | bytes 294920 | tf_op jit(solution)/shard_map/ppermute | solution.py:597
  198.8 17.8 %collective-permute-start.46 = (bf16[512,640]{1,0:T(8,128)(2,1)S(1)}, bf16[512,640]{1,0:T(8,128)(2,1)S(1)}, u32[]{:S(2)}, u32[]{:S(2)}) collective-permute-start(bf16[512,640]{1,0:T(8,128)(2,1)S(1)} %get-tuple-element.168), channel_id=1, source_target_pairs={{0,4},{4,0},{8,12},{12,8},{16,20},{20,16},{24,28},{28,24},{1,5},{5... | collective-permute-start | bytes 1966088 | tf_op jit(solution)/shard_map/ppermute | solution.py:597
  200.3 44.8 %collective-permute-start.37 = (f32[256,768]{1,0:T(8,128)S(1)}, f32[256,768]{1,0:T(8,128)S(1)}, u32[]{:S(2)}, u32[]{:S(2)}) collective-permute-start(f32[256,768]{1,0:T(8,128)S(1)} %get-tuple-element.159), channel_id=1, source_target_pairs={{0,1},{1,0},{2,3},{3,2},{4,5},{5,4},{6,7},{7,6},{8,9},{9,8},{10,11... | collective-permute-start | bytes 2359304 | tf_op jit(solution)/shard_map/ppermute | solution.py:594
  209.1 34.8 %collective-permute-start.66 = (bf16[192,768]{1,0:T(8,128)(2,1)S(1)}, bf16[192,768]{1,0:T(8,128)(2,1)S(1)}, u32[]{:S(2)}, u32[]{:S(2)}) collective-permute-start(bf16[192,768]{1,0:T(8,128)(2,1)S(1)} %get-tuple-element.200.refs_1_), channel_id=1, source_target_pairs={{0,24},{4,28},{8,16},{12,20},{16,8},{20,12},{24,0},{28,4},{1,25},{... | collective-permute-start | bytes 884744 | tf_op jit(solution)/shard_map/ppermute | solution.py:597
  210.8 30.5 %collective-permute-start.65 = (bf16[192,768]{1,0:T(8,128)(2,1)S(1)}, bf16[192,768]{1,0:T(8,128)(2,1)S(1)}, u32[]{:S(2)}, u32[]{:S(2)}) collective-permute-start(bf16[192,768]{1,0:T(8,128)(2,1)S(1)} %get-tuple-element.200.refs_1_), channel_id=1, source_target_pairs={{0,16},{4,20},{8,24},{12,28},{16,0},{20,4},{24,8},{28,12},{1,17},{... | collective-permute-start | bytes 884744 | tf_op jit(solution)/shard_map/ppermute | solution.py:597
  217.3 29.0 %collective-permute-start.47 = (bf16[128,640]{1,0:T(8,128)(2,1)S(1)}, bf16[128,640]{1,0:T(8,128)(2,1)S(1)}, u32[]{:S(2)}, u32[]{:S(2)}) collective-permute-start(bf16[128,640]{1,0:T(8,128)(2,1)S(1)} %get-tuple-element.170), channel_id=1, source_target_pairs={{0,8},{4,12},{8,0},{12,4},{16,24},{20,28},{24,16},{28,20},{1,9},{5... | collective-permute-start | bytes 491528 | tf_op jit(solution)/shard_map/ppermute | solution.py:597
  219.8 26.8 %collective-permute-start.48 = (bf16[128,640]{1,0:T(8,128)(2,1)S(1)}, bf16[128,640]{1,0:T(8,128)(2,1)S(1)}, u32[]{:S(2)}, u32[]{:S(2)}) collective-permute-start(bf16[128,640]{1,0:T(8,128)(2,1)S(1)} %get-tuple-element.171), channel_id=1, source_target_pairs={{0,16},{4,20},{8,24},{12,28},{16,0},{20,4},{24,8},{28,12},{1,17},{... | collective-permute-start | bytes 491528 | tf_op jit(solution)/shard_map/ppermute | solution.py:597
  244.6 38.8 %collective-permute-start.67 = (bf16[768,768]{1,0:T(8,128)(2,1)}, bf16[768,768]{1,0:T(8,128)(2,1)S(1)}, u32[]{:S(2)}, u32[]{:S(2)}) collective-permute-start(bf16[768,768]{1,0:T(8,128)(2,1)} %constant_dynamic-update-slice_fusion.18), channel_id=1, source_target_pairs={{0,4},{4,0},{8,12},{12,8},{16,20},{20,16},{24,28},{28,24},{1,5},{5... | collective-permute-start | bytes 3538952 | tf_op jit(solution)/shard_map/ppermute | solution.py:597
  260.1 19.0 %collective-permute-start.55 = (bf16[128,640]{1,0:T(8,128)(2,1)S(1)}, bf16[128,640]{1,0:T(8,128)(2,1)S(1)}, u32[]{:S(2)}, u32[]{:S(2)}) collective-permute-start(bf16[128,640]{1,0:T(8,128)(2,1)S(1)} %get-tuple-element.198.refs_1_), channel_id=1, source_target_pairs={{0,24},{4,28},{8,16},{12,20},{16,8},{20,12},{24,0},{28,4},{1,25},{... | collective-permute-start | bytes 491528 | tf_op jit(solution)/shard_map/ppermute | solution.py:597
  279.8 16.8 %collective-permute-start.56 = (bf16[512,640]{1,0:T(8,128)(2,1)}, bf16[512,640]{1,0:T(8,128)(2,1)S(1)}, u32[]{:S(2)}, u32[]{:S(2)}) collective-permute-start(bf16[512,640]{1,0:T(8,128)(2,1)} %constant_dynamic-update-slice_fusion.5), channel_id=1, source_target_pairs={{0,4},{4,0},{8,12},{12,8},{16,20},{20,16},{24,28},{28,24},{1,5},{5... | collective-permute-start | bytes 1966088 | tf_op jit(solution)/shard_map/ppermute | solution.py:597
  (72 other events, 666.7 us)

commit v3 on v2

--- a/solution.py
+++ b/solution.py
@@ -22,11 +22,18 @@
     return jax.ShapeDtypeStruct(dims, kind)
 
 
+class Direct:
+    def __init__(self, array):
+        self.array = array
+
+
 def call(body, name, outs, *args, scratch=(), after=()):
     vmem = pl.BlockSpec(memory_space=pltpu.VMEM)
     smem = pl.BlockSpec(memory_space=pltpu.SMEM)
     held = pl.BlockSpec(memory_space=pl.ANY)
     count, waits = len(args), len(after)
+    specs = [pl.BlockSpec() if isinstance(arg, Direct) else vmem for arg in args[1:]]
+    args = [arg.array if isinstance(arg, Direct) else arg for arg in args]
 
     def run(*refs):
         body(*refs[:count], *refs[count + waits :])
@@ -35,7 +42,7 @@
         run,
         name=name,
         out_shape=outs,
-        in_specs=[smem] + [vmem] * (count - 1) + [held] * waits,
+        in_specs=[smem] + specs + [held] * waits,
         out_specs=[vmem] * len(outs),
         scratch_shapes=list(scratch),
         compiler_params=pltpu.CompilerParams(vmem_limit_bytes=VMEM_BYTES),
@@ -79,26 +86,26 @@
         whole[rows_at(at[2] ^ k, size), :] = piece[...]
 
 
-def join_body(at, *refs):
-    join(at, refs[:-1], refs[-1])
-
-
-def columns_body(parts, at, attn, fc, small, *refs):
-    attn_pieces, fc_pieces = refs[:parts], refs[parts:]
+def as_row(ref):
+    return ref[...].astype(F32).reshape(1, ref.shape[0])
+
+
+def attn_columns_body(parts, at, attn, *refs):
+    vectors, pieces = refs[:6], refs[6:]
     features = attn.shape[1] // 3
     width = features // parts
-    hidden = fc.shape[1] // parts
     unit = (
         lax.broadcasted_iota(jnp.int32, (8, HD), 0) == lax.broadcasted_iota(jnp.int32, (8, HD), 1)
     ).astype(BF)
-    spare = dot_rows(small[...], unit).astype(BF)
+    small = jnp.concatenate([as_row(ref) for ref in vectors] + [jnp.zeros((2, width), F32)], axis=0)
+    spare = dot_rows(small.astype(BF), unit).astype(BF)
     for owner in range(parts):
 
         @pl.when(at[2] == owner)
         def _():
             for k in range(parts):
                 first = (owner ^ k) * width
-                piece = attn_pieces[k]
+                piece = pieces[k]
                 piece[:, :width] = attn[:, first : first + width]
                 piece[:, width:256] = spare
                 key = attn[:, features + first : features + first + width]
@@ -107,14 +114,27 @@
                 piece[:, 384:512] = value[:, :128]
                 piece[:, 512 : 512 + HD] = key[:, 128:]
                 piece[:, 512 + HD :] = value[:, 128:]
-                fc_pieces[k][...] = fc[:, (owner ^ k) * hidden : ((owner ^ k) + 1) * hidden]
+
+
+def fc_columns_body(at, fc, *pieces):
+    for k, piece in enumerate(pieces):
+        hidden = piece.shape[1]
+        piece[...] = fc[:, pl.ds(pl.multiple_of((at[2] ^ k) * hidden, 128), hidden)]
+
+
+def stack_body(count, at, *refs):
+    pairs, fc_pieces, (joined, fc) = refs[:count], refs[count:-2], refs[-2:]
+    size = pairs[0].shape[0]
+    for k, pair in enumerate(pairs):
+        joined[k * size : (k + 1) * size, :] = pair[...]
+    join(at, fc_pieces, fc)
 
 
 def block_of(at, k, rows):
     return rows_at(at[2] ^ at[0] ^ k, rows)
 
 
-def mixed_body(parts, count, at, bias, *refs):
+def mixed_body(parts, count, at, query_bias, value_bias, *refs):
     tokens, weights = refs[:parts], refs[parts : 2 * parts]
     normed, matrix, vectors, *outs, kept = refs[2 * parts :]
     rows = tokens[0].shape[0]
@@ -131,7 +151,11 @@
         normed[k * rows : (k + 1) * rows, :] = (unit * small[0:1] + small[1:2]).astype(BF)
     lane = lax.broadcasted_iota(jnp.int32, (1, columns), 1)
     spare = (lane >= width) & (lane < 256)
-    kept[...] = jnp.where(spare, 0.0, dot(normed[...], matrix[...]) + bias[...]).astype(BF)
+    query, value = as_row(query_bias), as_row(value_bias)
+    none = jnp.zeros((1, 128), F32)
+    bias = [query, none[:, :HD], none, value[:, :128], none[:, :HD], value[:, 128:]]
+    bias = jnp.concatenate(bias, axis=1)
+    kept[...] = jnp.where(spare, 0.0, dot(normed[...], matrix[...]) + bias).astype(BF)
     for k in range(count):
         block = block_of(at, k, rows)
         outs[k][...] = kept[block, :256]
@@ -164,10 +188,8 @@
 def attend_body(count, blocks, rows, at, *refs):
     queries, pairs = refs[:count], refs[count : 2 * count]
     partners = refs[2 * count : 2 * count + blocks - 1]
-    fc_pieces = refs[2 * count + blocks - 1 : 3 * count + blocks - 1]
-    outs = refs[3 * count + blocks - 1 :]
-    pieces, (exact, totals, q_all, kv_all, fc) = outs[:count], outs[count:]
-    join(at, fc_pieces, fc)
+    outs = refs[2 * count + blocks - 1 :]
+    pieces, (exact, totals, q_all, kv_all) = outs[:count], outs[count:]
     place(at, count, blocks, rows, queries, pairs, partners, q_all, kv_all)
     low = lax.broadcasted_iota(jnp.int32, (rows, 128), 1) < HD
     for i in range(count):
@@ -365,48 +387,59 @@
             mid_mine[(k // 2) * rows : (k // 2 + 1) * rows, :] = value
         unit, _ = normalize(value)
         normed[part, :] = (unit * vectors[2:3] + vectors[3:4]).astype(BF)
-    hidden = dot(normed[...], fc[...]) + fc_bias[...].astype(F32)
+    hidden = dot(normed[...], fc[...]) + as_row(fc_bias)
     value, slope = gelu_terms(hidden)
     active[...] = value.astype(BF)
     g_hidden[...] = (dot_columns(g_output(extras, rows), out[...]) * slope).astype(BF)
     split_rows(dot_columns(g_hidden[...], fc[...]), rows, gn_mine, gn_other)
 
 
-def chunk_rows(at, owner, owner_rows, blocks, count, side, k):
-    size = owner_rows // (blocks * count)
-    return pl.ds(pl.multiple_of(owner * owner_rows + (side * count + (at[0] ^ k)) * size, 8), size)
-
-
-def weights_body(parts, rows, blocks, at, normed, active, g_hidden, out, *refs):
-    extras = refs[:parts]
-    mine, other, *grads, sums, out_all, fc_all = refs[parts:]
+def fill_half(half, count, bit, kept, away, chunk):
+    size = kept.shape[0] // half
+    for i in range(half):
+        into = slice(i * size, (i + 1) * size)
+        kept[into, :] = chunk(bit * half + i)
+        away[into, :] = chunk((1 - bit) * half + i).astype(BF)
+
+
+def out_weights_body(rows, step, at, active, *refs):
+    extras = refs[:-4]
+    kept, away, sums, grad = refs[-4:]
+    g_out = g_output(extras, rows)
+    grad[...] = dot_rows(active[...], g_out)
+    sums[...] = jnp.zeros_like(sums)
+    sums[0:1, :] = jnp.sum(g_out[:rows].astype(F32), axis=0, keepdims=True)
+    half = kept.shape[0]
+    bit = (at[3] // step) % 2
+    kept[...] = grad[rows_at(bit, half), :]
+    away[...] = grad[rows_at(1 - bit, half), :].astype(BF)
+
+
+def fc_weights_body(parts, rows, half, step, at, normed, active, g_hidden, out, mine, other, kept, away, sums, grad):
+    grad[...] = dot_rows(normed[...], g_hidden[...])
+    size = grad.shape[0] // (parts * 2 * half)
+
+    def chunk(i):
+        blocks = [((at[2] ^ j) * 2 * half + i) * size for j in range(parts)]
+        return jnp.concatenate([grad[pl.ds(pl.multiple_of(start, 8), size), :] for start in blocks], axis=0)
+
+    fill_half(half, parts, (at[3] // step) % 2, kept, away, chunk)
+    split_rows(dot(active[...], out[...]), rows, mine, other)
+    sums[...] = jnp.zeros_like(sums)
+    sums[0:1, :] = jnp.sum(g_hidden[...].astype(F32), axis=0, keepdims=True)
+
+
+def plain_weights_body(rows, at, normed, active, g_hidden, out, *refs):
+    extras = refs[:-6]
+    mine, other, out_grad, fc_grad, out_sums, fc_sums = refs[-6:]
     g_out = g_output(extras, rows)
     split_rows(dot(active[...], out[...]), rows, mine, other)
-    out_all[...] = dot_rows(active[...], g_out)
-    fc_all[...] = dot_rows(normed[...], g_hidden[...])
-    sums[...] = jnp.zeros_like(sums)
-    sums[0:1, :] = jnp.sum(g_out.astype(F32), axis=0, keepdims=True)
-    sums[1:2, :] = jnp.sum(g_hidden[...].astype(F32), axis=0, keepdims=True)
-    if blocks != 2:
-        grads[0][...] = out_all[...].astype(BF)
-        grads[1][...] = fc_all[...].astype(BF)
-        return
-    kept, away = grads
-    out_rows, fc_rows = out_all.shape[0], fc_all.shape[0] // parts
-    out_size, fc_size = out_rows // (2 * parts), fc_rows // (2 * parts)
-    start = 0
-    for k in range(parts):
-        rows_kept = chunk_rows(at, 0, out_rows, 2, parts, at[1], k)
-        rows_away = chunk_rows(at, 0, out_rows, 2, parts, 1 - at[1], k)
-        kept[start : start + out_size, :] = out_all[rows_kept, :]
-        away[start : start + out_size, :] = out_all[rows_away, :].astype(BF)
-        start += out_size
-        for j in range(parts):
-            rows_kept = chunk_rows(at, at[2] ^ j, fc_rows, 2, parts, at[1], k)
-            rows_away = chunk_rows(at, at[2] ^ j, fc_rows, 2, parts, 1 - at[1], k)
-            kept[start : start + fc_size, :] = fc_all[rows_kept, :]
-            away[start : start + fc_size, :] = fc_all[rows_away, :].astype(BF)
-            start += fc_size
+    out_grad[...] = dot_rows(active[...], g_out).astype(BF)
+    fc_grad[...] = dot_rows(normed[...], g_hidden[...]).astype(BF)
+    out_sums[...] = jnp.zeros_like(out_sums)
+    out_sums[0:1, :] = jnp.sum(g_out[:rows].astype(F32), axis=0, keepdims=True)
+    fc_sums[...] = jnp.zeros_like(fc_sums)
+    fc_sums[0:1, :] = jnp.sum(g_hidden[...].astype(F32), axis=0, keepdims=True)
 
 
 def second_norm_body(rows, at, chip_sum, arrived, mid, own_extra, x_extra, vectors, g_branch, own_middle, sums):
@@ -415,8 +448,8 @@
     unit, scale = normalize(mid[...])
     back = norm_back(grad, unit, scale, vectors[2:3])
     sums[...] = jnp.zeros_like(sums)
-    sums[0:1, :] = jnp.sum(grad * unit, axis=0, keepdims=True)
-    sums[1:2, :] = jnp.sum(grad, axis=0, keepdims=True)
+    sums[0:1, :] = jnp.sum(grad[:rows] * unit[:rows], axis=0, keepdims=True)
+    sums[1:2, :] = jnp.sum(grad[:rows], axis=0, keepdims=True)
     g_own = back[:rows] + own_extra[:rows, :].astype(F32)
     own_middle[...] = g_own
     g_branch[:rows, :] = (RESIDUAL * g_own).astype(BF)
@@ -436,11 +469,11 @@
         outs[k][...] = g_all[block_of(at, k, rows), :]
 
 
-def proj_grad_body(at, attended, g_branch, proj_grad, sums):
+def proj_grad_body(rows, at, attended, g_branch, proj_grad, sums):
     grad = dot_rows(attended[...], g_branch[...])
     proj_grad[...] = jnp.concatenate([grad[:128], grad[128 + HD :]], axis=0)
     sums[...] = jnp.zeros_like(sums)
-    sums[0:1, :] = jnp.sum(g_branch[...].astype(F32), axis=0, keepdims=True)
+    sums[0:1, :] = jnp.sum(g_branch[:rows, :].astype(F32), axis=0, keepdims=True)
 
 
 def pack_wide(values, lanes):
@@ -451,7 +484,7 @@
     return jnp.concatenate([values[:, :lanes], jnp.concatenate(low, axis=1)], axis=0)
 
 
-def first_grad_body(parts, rows, blocks, at, normed, matrix, proj_grad, *refs):
+def first_grad_body(parts, rows, half, step, at, normed, matrix, proj_grad, *refs):
     queries, pairs = refs[:parts], refs[parts : 2 * parts]
     mine, other, *grads, sums, mixed, attn_all = refs[2 * parts :]
     for k in range(parts):
@@ -462,95 +495,140 @@
     attn_all[...] = dot_rows(normed[...], mixed[...])
     sums[...] = jnp.zeros_like(sums)
     sums[0:1, :] = jnp.sum(mixed[...].astype(F32), axis=0, keepdims=True)
-    if blocks != 2:
+    if not half:
         grads[0][...] = attn_all[...].astype(BF)
         grads[1][...] = proj_grad[...].astype(BF)
         return
-    kept, away = grads
     lanes = attn_all.shape[1]
-    owner_rows = attn_all.shape[0] // parts
-    size = owner_rows // (2 * parts)
-    start = 0
-    for k in range(parts):
-        for j in range(parts):
-            kept[start : start + size, :] = attn_all[chunk_rows(at, at[2] ^ j, owner_rows, 2, parts, at[1], k), :]
-            part = attn_all[chunk_rows(at, at[2] ^ j, owner_rows, 2, parts, 1 - at[1], k), :]
-            away[start : start + size, :] = part.astype(BF)
-            start += size
-        packed = size + size // 3
-        part = proj_grad[chunk_rows(at, 0, owner_rows, 2, parts, at[1], k), :]
-        kept[start : start + packed, :] = pack_wide(part, lanes)
-        part = proj_grad[chunk_rows(at, 0, owner_rows, 2, parts, 1 - at[1], k), :]
-        away[start : start + packed, :] = pack_wide(part, lanes).astype(BF)
-        start += packed
-
-
-def first_norm_body(rows, at, own, arrived, tokens, own_middle, vectors, input_grad, sums):
+    size = attn_all.shape[0] // (parts * 2 * half)
+
+    def chunk(i):
+        blocks = [((at[2] ^ j) * 2 * half + i) * size for j in range(parts)]
+        found = [attn_all[pl.ds(pl.multiple_of(start, 8), size), :] for start in blocks]
+        found.append(pack_wide(proj_grad[pl.ds(pl.multiple_of(i * size, 8), size), :], lanes))
+        return jnp.concatenate(found, axis=0)
+
+    fill_half(half, parts, (at[3] // step) % 2, *grads, chunk)
+
+
+def first_norm_body(rows, at, own, arrived, tokens, own_middle, vectors, two, proj, out_sums, fc_sums, attn, input_grad, whole, local):
     grad = own[:rows, :] + arrived[...].astype(F32)
     unit, scale = normalize(tokens[...].astype(F32))
     back = norm_back(grad, unit, scale, vectors[0:1])
     input_grad[...] = (back + own_middle[...]).astype(BF)
-    sums[...] = jnp.zeros_like(sums)
-    sums[0:1, :] = jnp.sum(grad * unit, axis=0, keepdims=True)
-    sums[1:2, :] = jnp.sum(grad, axis=0, keepdims=True)
-
-
-def pair_sum_body(count, at, kept, arrived, *outs):
-    size = kept.shape[0] // count
-    for k in range(count):
-        part = slice(k * size, (k + 1) * size)
-        outs[k][...] = (kept[part, :] + arrived[part, :].astype(F32)).astype(outs[k].dtype)
-
-
-def total_body(count, at, *refs):
+    whole[0:1, :] = jnp.sum(grad * unit, axis=0, keepdims=True)
+    whole[1:2, :] = jnp.sum(grad, axis=0, keepdims=True)
+    whole[2:4, :] = two[0:2, :]
+    whole[4:5, :] = proj[0:1, :]
+    whole[5:6, :] = out_sums[0:1, :]
+    whole[6:8, :] = jnp.zeros_like(whole[6:8, :])
+    local[0:1, :] = fc_sums[0:1, :]
+    local[1:2, :] = jnp.zeros_like(local[1:2, :])
+    local[1:2, :256] = attn[0:1, :256]
+    local[1:2, 256:384] = attn[0:1, 384:512]
+    local[1:2, 384:512] = attn[0:1, 512:]
+    local[2:, :] = jnp.zeros_like(local[2:, :])
+
+
+def vector_pack_body(parts, at, mine, across, local, out):
+    total = mine[...] + across[...]
+    width = total.shape[1] // parts
+    out[...] = jnp.zeros_like(out)
+    for owner in range(parts):
+
+        @pl.when(at[2] == owner)
+        def _():
+            out[0:6, :width] = total[0:6, owner * width : (owner + 1) * width]
+
+    out[6:8, :] = local[0:2, :]
+
+
+def vector_final_body(at, *refs):
+    count = len(refs) - 9
     total = refs[0][...]
     for ref in refs[1:count]:
-        total = total + ref[...].astype(F32)
+        total = total + ref[...]
+    outs = refs[count:]
+    width = outs[0].shape[0]
+    for row in range(6):
+        outs[row][...] = total[row : row + 1, :width].reshape(width)
+    outs[6][...] = total[7:8, :width].reshape(width)
+    value = jnp.concatenate([total[7:8, 256:384], total[7:8, 384 + HD : 512]], axis=1)
+    outs[7][...] = value.reshape(width)
+    outs[8][...] = total[6:7, :].reshape(total.shape[1])
+
+
+def halve_body(step, at, held, arrived, kept, away, total):
+    total[...] = held[...] + arrived[...].astype(F32)
+    half = kept.shape[0]
+    bit = (at[3] // step) % 2
+    kept[...] = total[rows_at(bit, half), :]
+    away[...] = total[rows_at(1 - bit, half), :].astype(BF)
+
+
+def last_sum_body(at, held, arrived, *outs):
+    total = held[...] + arrived[...].astype(F32)
     start = 0
-    for out in refs[count:]:
+    for out in outs:
         out[...] = total[start : start + out.shape[0]].astype(BF)
         start += out.shape[0]
 
 
-def mlp_final_body(parts, at, *refs):
-    own, away, (out_grad, fc_grad) = refs[:parts], refs[parts], refs[parts + 1 :]
-    out_rows, fc_rows = out_grad.shape[0], fc_grad.shape[0]
-    hidden = fc_grad.shape[1] // parts
-    out_size, fc_size = out_rows // (2 * parts), fc_rows // (2 * parts)
-    size = out_size + parts * fc_size
-    for side in range(2):
-        block = at[1] if side == 0 else 1 - at[1]
-        for k in range(parts):
-            piece = own[k][...] if side == 0 else away[k * size : (k + 1) * size, :]
-            piece = piece.astype(F32)
-            out_grad[chunk_rows(at, 0, out_rows, 2, parts, block, k), :] = piece[:out_size]
-            rows = chunk_rows(at, 0, fc_rows, 2, parts, block, k)
-            for j in range(parts):
-                start = out_size + j * fc_size
-                lanes = pl.ds(pl.multiple_of((at[2] ^ j) * hidden, 128), hidden)
-                fc_grad[rows, lanes] = piece[start : start + fc_size]
-
-
-def attn_final_body(parts, at, *refs):
-    own, away, (attn_grad, proj_grad, kept) = refs[:parts], refs[parts], refs[parts + 1 :]
-    rows_all, features = proj_grad.shape
+def stack_rows_body(at, *refs):
+    out = refs[-1]
+    start = 0
+    for ref in refs[:-1]:
+        out[start : start + ref.shape[0], :] = ref[...]
+        start += ref.shape[0]
+
+
+def chunk_number(at, mask, steps):
+    number = 0
+    for step in steps:
+        number = number * 2 + ((at[3] ^ mask) // step) % 2
+    return number
+
+
+def chunks_of(at, steps, refs):
+    masks = [0]
+    found = [(0, refs[0], 0)]
+    for step, ref in zip(reversed(steps), refs[1:]):
+        found += [(mask ^ step, ref, i) for i, mask in enumerate(masks)]
+        masks = masks + [mask ^ step for mask in masks]
+    size = refs[0].shape[0]
+    for mask, ref, i in found:
+        yield chunk_number(at, mask, steps), ref[i * size : (i + 1) * size, :].astype(F32)
+
+
+def out_final_body(steps, at, *refs):
+    for place, piece in chunks_of(at, steps, refs[:-1]):
+        refs[-1][rows_at(place, piece.shape[0]), :] = piece
+
+
+def fc_final_body(parts, steps, at, *refs):
+    out = refs[-1]
+    hidden = out.shape[1] // parts
+    for place, piece in chunks_of(at, steps, refs[:-1]):
+        size = piece.shape[0] // parts
+        for j in range(parts):
+            lanes = pl.ds(pl.multiple_of((at[2] ^ j) * hidden, 128), hidden)
+            out[rows_at(place, size), lanes] = piece[j * size : (j + 1) * size]
+
+
+def attn_final_body(parts, steps, at, *refs):
+    attn_grad, proj_grad, kept = refs[-3:]
+    features = proj_grad.shape[1]
     width = features // parts
     lanes = kept.shape[2]
-    size = rows_all // (2 * parts)
-    third = size // 3
-    total = parts * size + size + third
-    for side in range(2):
-        block = at[1] if side == 0 else 1 - at[1]
-        for k in range(parts):
-            piece = own[k][...] if side == 0 else away[k * total : (k + 1) * total, :]
-            piece = piece.astype(F32)
-            rows = chunk_rows(at, 0, rows_all, 2, parts, block, k)
-            for j in range(parts):
-                kept[at[2] ^ j, rows, :] = piece[j * size : (j + 1) * size]
-            start = parts * size
-            proj_grad[rows, :lanes] = piece[start : start + size]
-            low = piece[start + size :]
-            proj_grad[rows, lanes:] = jnp.concatenate([low[:, i * 128 : (i + 1) * 128] for i in range(3)], axis=0)
+    for place, piece in chunks_of(at, steps, refs[:-3]):
+        size = proj_grad.shape[0] // 2 ** len(steps)
+        rows = rows_at(place, size)
+        for j in range(parts):
+            kept[at[2] ^ j, rows, :] = piece[j * size : (j + 1) * size]
+        start = parts * size
+        proj_grad[rows, :lanes] = piece[start : start + size]
+        low = piece[start + size :]
+        proj_grad[rows, lanes:] = jnp.concatenate([low[:, i * 128 : (i + 1) * 128] for i in range(3)], axis=0)
     for g in range(parts):
         first = g * width
         attn_grad[:, first : first + width] = kept[g, :, :width]
@@ -588,7 +666,10 @@
     f = lax.axis_index("fsdp").astype(jnp.int32)
     c = lax.axis_index("ctx").astype(jnp.int32)
     a, b = c // blocks, c % blocks
-    at = jnp.stack([a, b, f])
+    at = jnp.stack([a, b, f, c])
+    halved = ways == 8
+    out_steps, fc_steps, attn_steps = (1, 2, 4), (2, 1, 4), (1, 2, 4)
+    chunks = 4
 
     def over_fsdp(value, k):
         return lax.ppermute(value, "fsdp", [(i, i ^ k) for i in range(parts)])
@@ -606,26 +687,49 @@
     def turn_ctx(pieces):
         return [pieces[0]] + [over_ctx(pieces[k], k * blocks) for k in range(1, count)]
 
+    def halve(name, kept, arrived, step, after=()):
+        size, lanes = kept.shape[0] // 2, kept.shape[1]
+        return call(
+            partial(halve_body, step),
+            name,
+            [shape((size, lanes), F32), shape((size, lanes), BF)],
+            at,
+            kept,
+            arrived,
+            scratch=[pltpu.VMEM((2 * size, lanes), F32)],
+            after=after,
+        )
+
+    def last_sum(name, kept, arrived, cuts, after=()):
+        outs = [shape((cut, kept.shape[1]), BF) for cut in cuts]
+        return call(last_sum_body, name, outs, at, kept, arrived, after=after)
+
+    def stacked(name, pieces, after=()):
+        total = sum(piece.shape[0] for piece in pieces)
+        outs = [shape((total, pieces[0].shape[1]), BF)]
+        return call(stack_rows_body, name, outs, at, *pieces, after=after)[0]
+
     tok = tokens[0]
     tok_all = spread(tok)
-    small = jnp.stack([first_gain, first_bias, second_gain, second_bias, proj_bias, out_bias, out_bias, out_bias])
     columns = 256 + 2 * width
-    pieces = call(
-        partial(columns_body, parts),
-        "columns",
-        [shape((width, columns), BF)] * parts + [shape((width, hidden), BF)] * parts,
-        at,
-        attn_weight,
-        fc_weight,
-        small,
-    )
-    attn_pieces = turn_fsdp(pieces[:parts])
-    fc_pieces = turn_fsdp(pieces[parts:])
-    extra = spread(jnp.concatenate([cotangent[0], proj_weight], 0))
-
-    none = jnp.zeros((128,), F32)
-    vb = value_bias.astype(F32)
-    bias = jnp.concatenate([query_bias.astype(F32), none[:HD], none, vb[:128], none[:HD], vb[128:]])[None]
+    attn_pieces = call(
+        partial(attn_columns_body, parts),
+        "attn_columns",
+        [shape((width, columns), BF)] * parts,
+        at,
+        *map(Direct, (attn_weight, first_gain, first_bias, second_gain, second_bias, proj_bias, out_bias)),
+    )
+    attn_pieces = turn_fsdp(attn_pieces)
+    fc_pieces = call(
+        fc_columns_body,
+        "fc_columns",
+        [shape((width, hidden), BF)] * parts,
+        at,
+        Direct(fc_weight),
+        after=attn_pieces[1:],
+    )
+    fc_pieces = turn_fsdp(fc_pieces)
+
     mixed = call(
         partial(mixed_body, parts, count),
         "mixed",
@@ -633,16 +737,34 @@
         + [shape((rows, 256), BF)] * count
         + [shape((rows, 384), BF)] * count,
         at,
-        bias,
+        query_bias,
+        value_bias,
         *tok_all,
         *attn_pieces,
         scratch=[pltpu.VMEM((all_rows, columns), BF)],
     )
     normed, attn_matrix, vectors = mixed[:3]
+    extra = call(
+        stack_rows_body,
+        "stack_extra",
+        [shape((rows + width, features), BF)],
+        at,
+        Direct(cotangent[0]),
+        Direct(proj_weight),
+        after=[vectors],
+    )[0]
+    extra = spread(extra)
 
     pairs = turn_ctx(mixed[3 + count :])
     queries = turn_ctx(mixed[3 : 3 + count])
-    joined = jnp.concatenate(pairs, 0)
+    joined, fc_matrix = call(
+        partial(stack_body, count),
+        "stack_pairs",
+        [shape((count * rows, pairs[0].shape[1]), BF), shape((features, hidden), BF)],
+        at,
+        *pairs,
+        *fc_pieces,
+    )
     partners = [over_ctx(joined, j) for j in range(1, blocks)]
     small_blocks = blocks * count * rows <= 1024
     if small_blocks:
@@ -655,18 +777,15 @@
                 shape((count * rows, 128), F32),
                 shape((count * rows, 256), BF),
                 shape((count * blocks * rows, 384), BF),
-                shape((features, hidden), BF),
             ],
             at,
             *queries,
             *pairs,
             *partners,
-            *fc_pieces,
+            after=extra,
         )
-        kept, fc_matrix = kept[:-1], kept[-1]
     else:
         kept = plain_attend(count, blocks, rows, at, queries, pairs, partners)
-        fc_matrix = call(join_body, "join", [shape((features, hidden), BF)], at, *fc_pieces)[0]
     att_pieces, state = turn_ctx(kept[:count]), kept[count:]
     attended_all = lax.all_gather(jnp.concatenate(att_pieces, 0), "fsdp")
 
@@ -680,7 +799,7 @@
         attended_all,
         vectors,
         fc_matrix,
-        fc_bias[None],
+        fc_bias,
         out_weight,
         *tok_all,
         *extra,
@@ -689,24 +808,48 @@
     chip_sum = gn_mine + over_fsdp(gn_other, 1)
     chip_low = chip_sum.astype(BF)
     arrived = over_fsdp(chip_low, 2)
-    if blocks == 2:
-        chunk = hidden // (2 * count) + features // (2 * count)
-        mlp_grads = [shape((count * chunk, features), F32), shape((count * chunk, features), BF)]
+    mlp_sums = [shape((8, features), F32), shape((8, hidden), F32)]
+    if halved:
+        out_kept, out_away, out_sums = call(
+            partial(out_weights_body, rows, out_steps[0]),
+            "out_weights",
+            [shape((hidden // 2, features), F32), shape((hidden // 2, features), BF), mlp_sums[0]],
+            at,
+            active,
+            *extra,
+            scratch=[pltpu.VMEM((hidden, features), F32)],
+            after=[chip_low],
+        )
+        mine, other, fc_kept, fc_away, fc_sums = call(
+            partial(fc_weights_body, parts, rows, chunks, fc_steps[0]),
+            "fc_weights",
+            [shape((half_rows, features), F32)] * 2
+            + [shape((features // 2, hidden), F32), shape((features // 2, hidden), BF), mlp_sums[1]],
+            at,
+            normed_two,
+            active,
+            g_hidden,
+            out_weight,
+            scratch=[pltpu.VMEM((features, hidden), F32)],
+            after=[out_away],
+        )
     else:
-        mlp_grads = [shape((hidden, features), BF), shape((features, hidden), BF)]
-    mine, other, *mlp_grads, sums_mlp = call(
-        partial(weights_body, parts, rows, blocks),
-        "mlp_weights",
-        [shape((half_rows, features), F32)] * 2 + mlp_grads + [shape((8, features), F32)],
-        at,
-        normed_two,
-        active,
-        g_hidden,
-        out_weight,
-        *extra,
-        scratch=[pltpu.VMEM((hidden, features), F32), pltpu.VMEM((features, hidden), F32)],
-        after=[chip_low],
-    )
+        mine, other, out_grad, fc_grad, out_sums, fc_sums = call(
+            partial(plain_weights_body, rows),
+            "mlp_weights",
+            [shape((half_rows, features), F32)] * 2
+            + [shape((hidden, features), BF), shape((features, hidden), BF)]
+            + mlp_sums,
+            at,
+            normed_two,
+            active,
+            g_hidden,
+            out_weight,
+            *extra,
+        )
+    if halved:
+        out_in = over_ctx(out_away, out_steps[0])
+        fc_in = over_ctx(fc_away, fc_steps[0])
     g_branch, own_middle, sums_two = call(
         partial(second_norm_body, rows),
         "second_norm",
@@ -718,6 +861,7 @@
         extra[0],
         extra[2],
         vectors,
+        after=[fc_sums],
     )
     grads = call(
         partial(attended_grad_body, parts, rows),
@@ -731,13 +875,16 @@
     )
     g_pieces, g_branch_all = turn_ctx(grads[:parts]), grads[parts]
     proj_grad, sums_proj = call(
-        proj_grad_body,
+        partial(proj_grad_body, rows),
         "proj_weight_grad",
         [shape((width, features), F32), shape((8, features), F32)],
         at,
         attended,
         g_branch_all,
     )
+    if halved:
+        out_kept, out_away = halve("out_halve_one", out_kept, out_in, out_steps[1])
+        out_in = over_ctx(out_away, out_steps[1])
     if small_blocks:
         back = call(
             partial(attend_back_body, count, blocks, rows),
@@ -755,22 +902,39 @@
                 pltpu.VMEM((count * rows, 256), BF),
                 pltpu.VMEM((count * blocks * rows, 384), F32),
             ],
+            after=[out_away] if halved else [],
         )
     else:
         back = plain_attend_back(count, blocks, rows, at, g_pieces, state[2], state[3], state[0], state[1])
     dq, own, away = back[:count], back[count], back[count + 1]
     stack = count * rows
     from_partners = [over_ctx(away[(j - 1) * stack : j * stack], j) for j in range(1, blocks)]
-    dkv = call(partial(merge_body, count, rows), "merge", [shape((rows, 384), BF)] * count, at, own, *from_partners)
+    if halved:
+        fc_kept, fc_away = halve("fc_halve_one", fc_kept, fc_in, fc_steps[1])
+        fc_in = over_ctx(fc_away, fc_steps[1])
+    dkv = call(
+        partial(merge_body, count, rows),
+        "merge",
+        [shape((rows, 384), BF)] * count,
+        at,
+        own,
+        *from_partners,
+        after=[fc_away] if halved else [],
+    )
     dq, dkv = turn_ctx(dq), turn_ctx(dkv)
-    if blocks == 2:
-        size = width // (2 * count)
-        chunk = parts * size + size + size // 3
-        attn_grads = [shape((count * chunk, columns), F32), shape((count * chunk, columns), BF)]
+    if halved:
+        out_kept, out_away = halve("out_halve_two", out_kept, out_in, out_steps[2])
+        out_in = over_ctx(out_away, out_steps[2])
+        fc_kept, fc_away = halve("fc_halve_two", fc_kept, fc_in, fc_steps[2])
+        fc_in = over_ctx(fc_away, fc_steps[2])
+        size = width // (2 * chunks)
+        packed = size + size // 3
+        chunk = parts * size + packed
+        attn_grads = [shape((chunks * chunk, columns), F32), shape((chunks * chunk, columns), BF)]
     else:
         attn_grads = [shape((features, columns), BF), shape((width, features), BF)]
     g1_mine, g1_other, *attn_grads, sums_attn = call(
-        partial(first_grad_body, parts, rows, blocks),
+        partial(first_grad_body, parts, rows, chunks if halved else 0, attn_steps[0]),
         "first_grad",
         [shape((half_rows, features), F32)] * 2 + attn_grads + [shape((8, columns), F32)],
         at,
@@ -780,92 +944,100 @@
         *dq,
         *dkv,
         scratch=[pltpu.VMEM((all_rows, columns), BF), pltpu.VMEM((features, columns), F32)],
+        after=[out_away, fc_away] if halved else [],
     )
     first_sum = g1_mine + over_fsdp(g1_other, 1)
-    input_grad, sums_one = call(
+    input_grad, vectors_whole, vectors_local = call(
         partial(first_norm_body, rows),
         "first_norm",
-        [shape((rows, features), BF), shape((8, features), F32)],
+        [shape((rows, features), BF), shape((8, features), F32), shape((8, hidden), F32)],
         at,
         first_sum,
         over_fsdp(first_sum[rows:].astype(BF), 2),
         tok,
         own_middle,
         vectors,
+        sums_two,
+        sums_proj,
+        out_sums,
+        fc_sums,
+        sums_attn,
     )
     out_sum = mine + over_fsdp(other, 1)
     output = out_sum[:rows] + over_fsdp(out_sum[rows:].astype(BF), 2).astype(F32) + vectors[5:6]
     block_out = (mid_mine[:rows] + RESIDUAL * output).astype(BF)
 
-    sums_one = sums_one[:2] + over_fsdp(sums_one[:2], 1)
-    sums_one = sums_one + over_fsdp(sums_one, 2)
-    sums_two = sums_two[:2] + over_fsdp(sums_two[:2], 1)
-
-    def own_slice(row):
-        return lax.dynamic_slice_in_dim(row, f * width, width, 0)
-
-    vector_sums = jnp.concatenate(
-        [
-            own_slice(sums_one[0]),
-            own_slice(sums_one[1]),
-            sums_attn[0, :width],
-            jnp.concatenate([sums_attn[0, 384:512], sums_attn[0, 512 + HD :]]),
-            own_slice(sums_proj[0]),
-            own_slice(sums_two[0]),
-            own_slice(sums_two[1]),
-            own_slice(sums_mlp[0]),
-            sums_mlp[1],
-        ]
-    ).reshape(-1, 128)
+    vectors_whole = vectors_whole + over_fsdp(vectors_whole, 1)
+    vector_sums = call(
+        partial(vector_pack_body, parts),
+        "vector_pack",
+        [shape((8, hidden), F32)],
+        at,
+        vectors_whole,
+        over_fsdp(vectors_whole, 2),
+        vectors_local,
+    )[0]
     if blocks == 2:
         vector_sums = vector_sums + over_ctx(vector_sums, 1)
-        vector_sums = sum((over_ctx(vector_sums, 2 * k) for k in range(1, count)), vector_sums)
+        vector_sums = [vector_sums] + [over_ctx(vector_sums, 2 * k) for k in range(1, count)]
     else:
-        vector_sums = lax.psum(vector_sums, "ctx")
-    vector_sums = vector_sums.reshape(-1)
-    slices = [vector_sums[i * width : (i + 1) * width] for i in range(8)]
-    fc_bias_grad = vector_sums[8 * width :]
-
-    if blocks == 2:
-
-        def summed(name, kept, away, cuts):
-            size, lanes = kept.shape[0] // count, kept.shape[1]
-            sent = call(
-                partial(pair_sum_body, count),
-                name + "_pair",
-                [shape((size, lanes), F32)] + [shape((size, lanes), BF)] * (count - 1),
-                at,
-                kept,
-                over_ctx(away, 1),
-            )
-            return call(
-                partial(total_body, count),
-                name + "_total",
-                [shape((cut, lanes), BF) for cut in cuts],
-                at,
-                *turn_ctx(sent),
-            )
-
-        def gathered(piece):
-            pieces = [piece] + [over_ctx(piece, 2 * k) for k in range(1, count)]
-            return (*pieces, over_ctx(jnp.concatenate(pieces, 0), 1))
-
-        out_size, fc_size = hidden // (2 * count), width // (2 * count)
-        out_part, *fc_parts = summed("mlp", *mlp_grads, [out_size] + [fc_size] * parts)
-        out_weight_grad, fc_weight_grad = call(
-            partial(mlp_final_body, parts),
-            "mlp_final",
-            [shape((hidden, features), F32), shape((width, parts * hidden), F32)],
+        vector_sums = [lax.psum(vector_sums, "ctx")]
+    vector_grads = call(
+        vector_final_body,
+        "vector_final",
+        [shape((width,), F32)] * 8 + [shape((hidden,), F32)],
+        at,
+        *vector_sums,
+    )
+    first_gain_grad, first_bias_grad, second_gain_grad, second_bias_grad = vector_grads[:4]
+    proj_bias_grad, out_bias_grad, query_bias_grad, value_bias_grad, fc_bias_grad = vector_grads[4:]
+
+    if halved:
+        kept, away = attn_grads
+        attn_in = over_ctx(away, attn_steps[0])
+        out_part = last_sum("out_sum", out_kept, out_in, [hidden // (2 * chunks)])[0]
+        fc_parts = last_sum("fc_sum", fc_kept, fc_in, [size] * parts)
+        out_pieces = [out_part, over_ctx(out_part, out_steps[2])]
+        fc_part = stacked("fc_turned", turn_fsdp(fc_parts))
+        fc_pieces = [fc_part, over_ctx(fc_part, fc_steps[2])]
+        kept, away = halve("attn_halve_one", kept, attn_in, attn_steps[1], after=[out_part, fc_parts[0], vectors_whole])
+        attn_in = over_ctx(away, attn_steps[1])
+        out_pieces.append(over_ctx(stacked("out_two", out_pieces), out_steps[1]))
+        fc_message = stacked("fc_two", fc_pieces)
+        fc_pieces.append(over_ctx(fc_message, fc_steps[1]))
+        kept, away = halve("attn_halve_two", kept, attn_in, attn_steps[2], after=[fc_message, vector_sums[0]])
+        attn_in = over_ctx(away, attn_steps[2])
+        out_message = stacked("out_four", out_pieces)
+        out_pieces.append(over_ctx(out_message, out_steps[0]))
+        fc_message = stacked("fc_four", fc_pieces)
+        fc_pieces.append(over_ctx(fc_message, fc_steps[0]))
+        *attn_parts, proj_part = last_sum(
+            "attn_sum", kept, attn_in, [size] * parts + [packed], after=[out_message, fc_message]
+        )
+        attn_part = stacked("attn_turned", [*turn_fsdp(attn_parts), proj_part])
+        attn_pieces = [attn_part, over_ctx(attn_part, attn_steps[2])]
+        attn_pieces.append(over_ctx(stacked("attn_two", attn_pieces), attn_steps[1]))
+        out_weight_grad = call(
+            partial(out_final_body, out_steps),
+            "out_final",
+            [shape((hidden, features), F32)],
             at,
-            *gathered(jnp.concatenate([out_part, *turn_fsdp(fc_parts)], 0)),
-        )
-        *attn_parts, proj_part = summed("attn", *attn_grads, [size] * parts + [size + size // 3])
+            *out_pieces,
+        )[0]
+        fc_weight_grad = call(
+            partial(fc_final_body, parts, fc_steps),
+            "fc_final",
+            [shape((width, parts * hidden), F32)],
+            at,
+            *fc_pieces,
+        )[0]
+        attn_pieces.append(over_ctx(stacked("attn_four", attn_pieces), attn_steps[0]))
         attn_weight_grad, proj_weight_grad = call(
-            partial(attn_final_body, parts),
+            partial(attn_final_body, parts, attn_steps),
             "attn_final",
             [shape((width, 3 * features), F32), shape((width, features), F32)],
             at,
-            *gathered(jnp.concatenate([*turn_fsdp(attn_parts), proj_part], 0)),
+            *attn_pieces,
             scratch=[pltpu.VMEM((parts, width, columns), F32)],
         )
     else:
@@ -874,8 +1046,8 @@
             part = lax.psum_scatter(value, "ctx", scatter_dimension=1, tiled=True)
             return lax.all_gather(part, "ctx", axis=1, tiled=True)
 
-        out_weight_grad = over_all(mlp_grads[0]).astype(F32)
-        fc_grad = over_all(mlp_grads[1]).reshape(parts, width, hidden)
+        out_weight_grad = over_all(out_grad).astype(F32)
+        fc_grad = over_all(fc_grad).reshape(parts, width, hidden)
         fc_grad = lax.all_to_all(fc_grad, "fsdp", split_axis=0, concat_axis=0)
         fc_weight_grad = fc_grad.transpose(1, 0, 2).reshape(width, parts * hidden).astype(F32)
         proj_weight_grad = over_all(attn_grads[1]).astype(F32)
@@ -888,19 +1060,19 @@
     return (
         block_out[None],
         input_grad[None],
-        slices[0],
-        slices[1],
+        first_gain_grad,
+        first_bias_grad,
         attn_weight_grad,
-        slices[2],
-        slices[3],
+        query_bias_grad,
+        value_bias_grad,
         proj_weight_grad,
-        slices[4],
-        slices[5],
-        slices[6],
+        proj_bias_grad,
+        second_gain_grad,
+        second_bias_grad,
         fc_weight_grad,
         fc_bias_grad,
         out_weight_grad,
-        slices[7],
+        out_bias_grad,
     )
 
 

time: 300 us -> 279 us (0.930)
  local copies, waits for them, and re-layouts: 25.6 us -> 8.46 us
  waiting for transfers between devices: 143 us -> 128 us
  Pallas kernels: 50 us -> 59 us
  starting transfers between devices: 67.1 us -> 72.3 us
    ppermute x40 -> x42, waiting for transfers between devices: 105 us -> 91.6 us  [over_ctx(): return lax.ppermute(value, 'ctx', [(i, i ^ k) for i in range(ways)])]
    pallas_call x18 -> x38, Pallas kernels: 50 us -> 59 us  [call(): pl.pallas_call(run, name=name, out_shape=outs, in_specs=[smem] + specs +...]
    unnamed x70 -> x50, local copies, waits for them, and re-layouts: 15.2 us -> 8.4 us
    ppermute x40 -> x42, starting transfers between devices: 49.8 us -> 54.7 us  [over_ctx(): return lax.ppermute(value, 'ctx', [(i, i ^ k) for i in range(ways)])]
    another operation x8 -> x0, local copies, waits for them, and re-layouts: 3.98 us -> none  [the longest x7 3.98 us: shards(): jnp.stack([first_gain, first_bias, second_gain, second_bias, proj_bias, o...]
    ppermute x28 -> x27, waiting for transfers between devices: 38 us -> 36.4 us  [over_fsdp(): return lax.ppermute(value, 'fsdp', [(i, i ^ k) for i in range(parts)])]
    ppermute x28 -> x27, starting transfers between devices: 17.3 us -> 17.6 us  [over_fsdp(): return lax.ppermute(value, 'fsdp', [(i, i ^ k) for i in range(parts)])]
  transfers between devices with their start and end apart: 68 -> 69, of which waited for: 30 -> 35; matrix products, arithmetic and copies ran while one was open for 7% -> 0% of each run, Pallas kernels for 12% -> 13%
where the time goes in v3:
time: 279 us; the launch traced here: 278 us
  waiting for transfers between devices  128 us (46%)
  starting transfers between devices  72.3 us (26%)
  Pallas kernels  59 us (21%)
  local copies, waits for them, and re-layouts  8.46 us (3%)
  blocking collectives  8.26 us (3%)
    ppermute x42, waiting for transfers between devices, over_ctx(): return lax.ppermute(value, 'ctx', [(i, i ^ k) for i in range(ways)])  91.6 us
    pallas_call x38, Pallas kernels, call(): pl.pallas_call(run, name=name, out_shape=outs, in_specs=[smem] + specs +...  59 us
    ppermute x42, starting transfers between devices, over_ctx(): return lax.ppermute(value, 'ctx', [(i, i ^ k) for i in range(ways)])  54.7 us
    ppermute x27, waiting for transfers between devices, over_fsdp(): return lax.ppermute(value, 'fsdp', [(i, i ^ k) for i in range(parts)])  36.4 us
    ppermute x27, starting transfers between devices, over_fsdp(): return lax.ppermute(value, 'fsdp', [(i, i ^ k) for i in range(parts)])  17.6 us
    unnamed x50, local copies, waits for them, and re-layouts  8.4 us
    all_gather x1, blocking collectives, shards(): attended_all = lax.all_gather(jnp.concatenate(att_pieces, 0), 'fsdp')  8.26 us
  transfers between devices with their start and end apart: 69, of which 35 were waited for; matrix products, arithmetic and copies ran while one was open for 0% of the time, Pallas kernels for 13%

profile of v3, /device:TPU:0, one launch (start us, length us, event | category | flops | bytes accessed | tf_op | source)
XLA Modules:
  0.0 278.4 jit_solution(10669053162772016899)
XLA Ops:
  0.6 3.0 %collective-permute-start.1 = (bf16[128,768]{1,0:T(8,128)(2,1)}, bf16[128,768]{1,0:T(8,128)(2,1)S(1)}, u32[]{:S(2)}, u32[]{:S(2)}) collective-permute-start(bf16[128,768]{1,0:T(8,128)(2,1)} %bitcast.10), channel_id=1, source_target_pairs={{0,2},{1,3},{2,0},{3,1},{4,6},{5,7},{6,4},{7,5},{8,10},{9,11},{10,... | collective-permute-start | bytes 589832 | tf_op jit(solution)/shard_map/ppermute | solution.py:675
  13.5 5.3 %collective-permute-done.4.refs_9_.refs_3_ = bf16[192,640]{1,0:T(8,128)(2,1)S(1)} collective-permute-done((bf16[192,640]{1,0:T(8,128)(2,1)S(1)}, bf16[192,640]{1,0:T(8,128)(2,1)S(1)}, u32[]{:S(2)}, u32[]{:S(2)}) %collective-permute-start.4) | collective-permute-done | bytes 245792 | tf_op jit(solution)/shard_map/ppermute | solution.py:675
  18.8 4.4 %collective-permute-done.5.refs_10_.refs_4_ = bf16[192,640]{1,0:T(8,128)(2,1)S(1)} collective-permute-done((bf16[192,640]{1,0:T(8,128)(2,1)S(1)}, bf16[192,640]{1,0:T(8,128)(2,1)S(1)}, u32[]{:S(2)}, u32[]{:S(2)}) %collective-permute-start.5) | collective-permute-done | bytes 245792 | tf_op jit(solution)/shard_map/ppermute | solution.py:675
  35.8 4.9 %collective-permute-done.10.refs_3_.refs_7_ = bf16[128,384]{1,0:T(8,128)(2,1)S(1)} collective-permute-done((bf16[128,384]{1,0:T(8,128)(2,1)S(1)}, bf16[128,384]{1,0:T(8,128)(2,1)S(1)}, u32[]{:S(2)}, u32[]{:S(2)}) %collective-permute-start.10) | collective-permute-done | bytes 98336 | tf_op jit(solution)/shard_map/ppermute | solution.py:678
  43.7 3.5 %collective-permute-done.11.refs_4_.refs_8_ = bf16[128,384]{1,0:T(8,128)(2,1)S(1)} collective-permute-done((bf16[128,384]{1,0:T(8,128)(2,1)S(1)}, bf16[128,384]{1,0:T(8,128)(2,1)S(1)}, u32[]{:S(2)}, u32[]{:S(2)}) %collective-permute-start.11) | collective-permute-done | bytes 98336 | tf_op jit(solution)/shard_map/ppermute | solution.py:678
  48.3 5.0 %collective-permute-done.14.refs_8_ = bf16[192,768]{1,0:T(8,128)(2,1)S(1)} collective-permute-done((bf16[192,768]{1,0:T(8,128)(2,1)S(1)}, bf16[192,768]{1,0:T(8,128)(2,1)S(1)}, u32[]{:S(2)}, u32[]{:S(2)}) %collective-permute-start.14) | collective-permute-done | bytes 294944 | tf_op jit(solution)/shard_map/ppermute | solution.py:675
  60.8 4.3 %collective-permute-start.8 = (bf16[128,256]{1,0:T(8,128)(2,1)S(1)}, bf16[128,256]{1,0:T(8,128)(2,1)S(1)}, u32[]{:S(2)}, u32[]{:S(2)}) collective-permute-start(bf16[128,256]{1,0:T(8,128)(2,1)S(1)} %get-tuple-element.126), channel_id=1, source_target_pairs={{0,24},{4,28},{8,16},{12,20},{16,8},{20,12},{24,0},{28,4},{1,25},{... | collective-permute-start | bytes 196616 | tf_op jit(solution)/shard_map/ppermute | solution.py:678
  67.4 6.3 %attend.1 = (bf16[192,128]{1,0:T(8,128)(2,1)S(1)}, bf16[192,128]{1,0:T(8,128)(2,1)S(1)}, bf16[192,128]{1,0:T(8,128)(2,1)S(1)}, bf16[192,128]{1,0:T(8,128)(2,1)S(...) custom-call(s32[4]{0:T(128)S(1)} %pad_add_fusion.refs_0_, ...), custom_call_target="tpu_custom_call" | custom-call | tf_op jit(solution)/shard_map/attend/pallas_call | solution.py:41
  73.7 3.8 %collective-permute-start.21 = (bf16[192,128]{1,0:T(8,128)(2,1)S(1)}, bf16[192,128]{1,0:T(8,128)(2,1)S(1)}, u32[]{:S(2)}, u32[]{:S(2)}) collective-permute-start(bf16[192,128]{1,0:T(8,128)(2,1)S(1)} %get-tuple-element.140), channel_id=1, source_target_pairs={{0,24},{4,28},{8,16},{12,20},{16,8},{20,12},{24,0},{28,4},{1,25},{... | collective-permute-start | bytes 147464 | tf_op jit(solution)/shard_map/ppermute | solution.py:678
  82.5 8.3 %all-gather = bf16[3072,128]{1,0:T(8,128)(2,1)} all-gather(bf16[768,128]{1,0:T(8,128)(2,1)S(1)} %pad_maximum_fusion), channel_id=2, replica_groups=mesh['ctx'=8,'fsdp'=4] {'fsdp'}, dimensions={0}, use_global_device_ids=true | all-gather | bytes 983040 | tf_op jit(solution)/shard_map/all_gather | solution.py:790
  90.7 7.0 %middle.1 = (f32[256,768]{1,0:T(8,128)S(1)}, f32[256,768]{1,0:T(8,128)}, f32[256,768]{1,0:T(8,128)}, bf16[512,768]{1,0:T(8,128)(2,1)}, bf16[512,768]{1,0:T(8,128...) custom-call(s32[4]{0:T(128)S(1)} %pad_add_fusion.refs_0_, bf16[4,768,128]{2,1,0:T(8,128)(2,1)} %bitcast.16, ...), custom_call_target="tpu_custom_call" | custom-call | tf_op jit(solution)/shard_map/middle/pallas_call | solution.py:41
  105.2 4.0 %fc_weights.1 = (f32[256,768]{1,0:T(8,128)S(1)}, f32[256,768]{1,0:T(8,128)S(1)}, f32[384,768]{1,0:T(8,128)}, bf16[384,768]{1,0:T(8,128)(2,1)S(1)}, f32[8,768]{1,0:T(8,128)S(1)}) custom-call(s32[4]{0:T(128)S(1)} %pad_add_fusion.refs_0_, bf16[512,768]{1,0:T(8,128)(2,1)S(1)} %copy-done.11, bf16[512,768]{1,0:T(8,128)(2,1)} %get-tuple-element.144.refs_1_.refs_2_, ...), custom_call_target="tpu_custom_call" | custom-call | tf_op jit(solution)/shard_map/fc_weights/pallas_call | solution.py:41
  121.0 10.6 %collective-permute-done.27.refs_2_ = bf16[128,256]{1,0:T(8,128)(2,1)S(1)} collective-permute-done((bf16[128,256]{1,0:T(8,128)(2,1)S(1)}, bf16[128,256]{1,0:T(8,128)(2,1)S(1)}, u32[]{:S(2)}, u32[]{:S(2)}) %collective-permute-start.27) | collective-permute-done | bytes 65568 | tf_op jit(solution)/shard_map/ppermute | solution.py:678
  134.5 5.5 %attend_back.1 = (bf16[128,256]{1,0:T(8,128)(2,1)S(1)}, bf16[128,256]{1,0:T(8,128)(2,1)S(1)}, bf16[128,256]{1,0:T(8,128)(2,1)S(1)}, bf16[128,256]{1,0:T(8,128)(2...) custom-call(s32[4]{0:T(128)S(1)} %pad_add_fusion.refs_0_, ...), custom_call_target="tpu_custom_call" | custom-call | tf_op jit(solution)/shard_map/attend_back/pallas_call | solution.py:41
  144.9 7.1 %collective-permute-done.34.refs_2_ = bf16[512,384]{1,0:T(8,128)(2,1)S(1)} collective-permute-done((bf16[512,384]{1,0:T(8,128)(2,1)S(1)}, bf16[512,384]{1,0:T(8,128)(2,1)S(1)}, u32[]{:S(2)}, u32[]{:S(2)}) %collective-permute-start.34) | collective-permute-done | bytes 393248 | tf_op jit(solution)/shard_map/ppermute | solution.py:678
  153.9 3.2 %collective-permute-start.38 = (bf16[128,384]{1,0:T(8,128)(2,1)S(1)}, bf16[128,384]{1,0:T(8,128)(2,1)S(1)}, u32[]{:S(2)}, u32[]{:S(2)}) collective-permute-start(bf16[128,384]{1,0:T(8,128)(2,1)S(1)} %get-tuple-element.180), channel_id=1, source_target_pairs={{0,24},{4,28},{8,16},{12,20},{16,8},{20,12},{24,0},{28,4},{1,25},{... | collective-permute-start | bytes 294920 | tf_op jit(solution)/shard_map/ppermute | solution.py:678
  160.9 6.2 %collective-permute-done.32.refs_6_ = bf16[128,256]{1,0:T(8,128)(2,1)S(1)} collective-permute-done((bf16[128,256]{1,0:T(8,128)(2,1)S(1)}, bf16[128,256]{1,0:T(8,128)(2,1)S(1)}, u32[]{:S(2)}, u32[]{:S(2)}) %collective-permute-start.32) | collective-permute-done | bytes 65568 | tf_op jit(solution)/shard_map/ppermute | solution.py:678
  167.1 4.1 %first_grad.1 = (f32[256,768]{1,0:T(8,128)S(1)}, f32[256,768]{1,0:T(8,128)S(1)}, f32[512,640]{1,0:T(8,128)}, bf16[512,640]{1,0:T(8,128)(2,1)S(1)}, f32[8,640]{1,0:T(8,128)S(1)}) custom-call(s32[4]{0:T(128)S(1)} %pad_add_fusion.refs_0_, bf16[512,768]{1,0:T(8,128)(2,1)} %copy-done.12, bf16[768,640]{1,0:T(8,128)(2,1)} %get-tuple-element.152.refs_2_, ...), custom_call_target="tpu_custom_call" | custom-call | tf_op jit(solution)/shard_map/first_grad/pallas_call | solution.py:41
  182.3 6.5 %collective-permute-done.50.refs_2_ = bf16[96,768]{1,0:T(8,128)(2,1)S(1)} collective-permute-done((bf16[96,768]{1,0:T(8,128)(2,1)S(1)}, bf16[96,768]{1,0:T(8,128)(2,1)S(1)}, u32[]{:S(2)}, u32[]{:S(2)}) %collective-permute-start.50) | collective-permute-done | bytes 147488 | tf_op jit(solution)/shard_map/ppermute | solution.py:678
  199.8 8.9 %collective-permute-done.58.refs_2_ = bf16[96,768]{1,0:T(8,128)(2,1)S(1)} collective-permute-done((bf16[96,768]{1,0:T(8,128)(2,1)S(1)}, bf16[96,768]{1,0:T(8,128)(2,1)S(1)}, u32[]{:S(2)}, u32[]{:S(2)}) %collective-permute-start.58) | collective-permute-done | bytes 147488 | tf_op jit(solution)/shard_map/ppermute | solution.py:678
  213.0 3.3 %collective-permute-done.44.refs_2_ = f32[8,768]{1,0:T(8,128)S(1)} collective-permute-done((f32[8,768]{1,0:T(8,128)S(1)}, f32[8,768]{1,0:T(8,128)S(1)}, u32[]{:S(2)}, u32[]{:S(2)}) %collective-permute-start.44) | collective-permute-done | bytes 24608 | tf_op jit(solution)/shard_map/ppermute | solution.py:675
  222.9 7.2 %collective-permute-done.57.refs_2_ = bf16[128,640]{1,0:T(8,128)(2,1)S(1)} collective-permute-done((bf16[128,640]{1,0:T(8,128)(2,1)S(1)}, bf16[128,640]{1,0:T(8,128)(2,1)S(1)}, u32[]{:S(2)}, u32[]{:S(2)}) %collective-permute-start.57) | collective-permute-done | bytes 163872 | tf_op jit(solution)/shard_map/ppermute | solution.py:678
  235.9 9.6 %collective-permute-done.64.refs_2_ = bf16[128,640]{1,0:T(8,128)(2,1)S(1)} collective-permute-done((bf16[128,640]{1,0:T(8,128)(2,1)S(1)}, bf16[128,640]{1,0:T(8,128)(2,1)S(1)}, u32[]{:S(2)}, u32[]{:S(2)}) %collective-permute-start.64) | collective-permute-done | bytes 163872 | tf_op jit(solution)/shard_map/ppermute | solution.py:678
  246.9 8.9 %collective-permute-done.65.refs_3_ = bf16[256,640]{1,0:T(8,128)(2,1)S(1)} collective-permute-done((bf16[256,640]{1,0:T(8,128)(2,1)S(1)}, bf16[256,640]{1,0:T(8,128)(2,1)S(1)}, u32[]{:S(2)}, u32[]{:S(2)}) %collective-permute-start.65) | collective-permute-done | bytes 327712 | tf_op jit(solution)/shard_map/ppermute | solution.py:678
  (214 shorter events, 136.3 us)
Async XLA Ops:
  27.9 19.2 %collective-permute-start.17 = (bf16[320,768]{1,0:T(8,128)(2,1)S(1)}, bf16[320,768]{1,0:T(8,128)(2,1)S(1)}, u32[]{:S(2)}, u32[]{:S(2)}) collective-permute-start(bf16[320,768]{1,0:T(8,128)(2,1)S(1)} %stack_extra.1.refs_10_.refs_2_.refs_4_), channel_id=1, source_target_pairs={{0,2},{1,3},{2,0},{3,1},{4,6},{5,7},{6,4},{7,5},{8,10},{9,11},{10,... | collective-permute-start | bytes 1474568 | tf_op jit(solution)/shard_map/ppermute | solution.py:675
  30.7 16.9 %collective-permute-start.12 = (bf16[192,768]{1,0:T(8,128)(2,1)S(1)}, bf16[192,768]{1,0:T(8,128)(2,1)S(1)}, u32[]{:S(2)}, u32[]{:S(2)}) collective-permute-start(bf16[192,768]{1,0:T(8,128)(2,1)S(1)} %get-tuple-element.132), channel_id=1, source_target_pairs={{0,1},{1,0},{2,3},{3,2},{4,5},{5,4},{6,7},{7,6},{8,9},{9,8},{10,11... | collective-permute-start | bytes 884744 | tf_op jit(solution)/shard_map/ppermute | solution.py:675
  30.8 17.6 %collective-permute-start.13 = (bf16[192,768]{1,0:T(8,128)(2,1)S(1)}, bf16[192,768]{1,0:T(8,128)(2,1)S(1)}, u32[]{:S(2)}, u32[]{:S(2)}) collective-permute-start(bf16[192,768]{1,0:T(8,128)(2,1)S(1)} %get-tuple-element.133), channel_id=1, source_target_pairs={{0,2},{1,3},{2,0},{3,1},{4,6},{5,7},{6,4},{7,5},{8,10},{9,11},{10,... | collective-permute-start | bytes 884744 | tf_op jit(solution)/shard_map/ppermute | solution.py:675
  32.4 21.0 %collective-permute-start.14 = (bf16[192,768]{1,0:T(8,128)(2,1)S(1)}, bf16[192,768]{1,0:T(8,128)(2,1)S(1)}, u32[]{:S(2)}, u32[]{:S(2)}) collective-permute-start(bf16[192,768]{1,0:T(8,128)(2,1)S(1)} %get-tuple-element.134), channel_id=1, source_target_pairs={{0,3},{1,2},{2,1},{3,0},{4,7},{5,6},{6,5},{7,4},{8,11},{9,10},{10,... | collective-permute-start | bytes 884744 | tf_op jit(solution)/shard_map/ppermute | solution.py:675
  47.1 20.3 %collective-permute-start.16 = (bf16[320,768]{1,0:T(8,128)(2,1)S(1)}, bf16[320,768]{1,0:T(8,128)(2,1)S(1)}, u32[]{:S(2)}, u32[]{:S(2)}) collective-permute-start(bf16[320,768]{1,0:T(8,128)(2,1)S(1)} %stack_extra.1.refs_10_.refs_2_.refs_4_), channel_id=1, source_target_pairs={{0,1},{1,0},{2,3},{3,2},{4,5},{5,4},{6,7},{7,6},{8,9},{9,8},{10,11... | collective-permute-start | bytes 1474568 | tf_op jit(solution)/shard_map/ppermute | solution.py:675
  47.1 20.3 %collective-permute-start.18 = (bf16[320,768]{1,0:T(8,128)(2,1)S(1)}, bf16[320,768]{1,0:T(8,128)(2,1)S(1)}, u32[]{:S(2)}, u32[]{:S(2)}) collective-permute-start(bf16[320,768]{1,0:T(8,128)(2,1)S(1)} %collective-permute-done.17.refs_12_.refs_4_.refs_5_), channel_id=1, source_target_pairs={{0,1},{1,0},{2,3},{3,2},{4,5},{5,4},{6,7},{7,6},{8,9},{9,8},{10,11... | collective-permute-start | bytes 1474568 | tf_op jit(solution)/shard_map/ppermute | solution.py:675
  104.6 15.5 %collective-permute-start.30 = (bf16[384,768]{1,0:T(8,128)(2,1)S(1)}, bf16[384,768]{1,0:T(8,128)(2,1)S(1)}, u32[]{:S(2)}, u32[]{:S(2)}) collective-permute-start(bf16[384,768]{1,0:T(8,128)(2,1)S(1)} %get-tuple-element.148.refs_5_), channel_id=1, source_target_pairs={{0,4},{4,0},{8,12},{12,8},{16,20},{20,16},{24,28},{28,24},{1,5},{5... | collective-permute-start | bytes 1769480 | tf_op jit(solution)/shard_map/ppermute | solution.py:678
  113.1 27.5 %collective-permute-start.35 = (bf16[384,768]{1,0:T(8,128)(2,1)S(1)}, bf16[384,768]{1,0:T(8,128)(2,1)S(1)}, u32[]{:S(2)}, u32[]{:S(2)}) collective-permute-start(bf16[384,768]{1,0:T(8,128)(2,1)S(1)} %get-tuple-element.175), channel_id=1, source_target_pairs={{0,8},{4,12},{8,0},{12,4},{16,24},{20,28},{24,16},{28,20},{1,9},{5... | collective-permute-start | bytes 1769480 | tf_op jit(solution)/shard_map/ppermute | solution.py:678
  115.7 15.9 %collective-permute-start.27 = (bf16[128,256]{1,0:T(8,128)(2,1)S(1)}, bf16[128,256]{1,0:T(8,128)(2,1)S(1)}, u32[]{:S(2)}, u32[]{:S(2)}) collective-permute-start(bf16[128,256]{1,0:T(8,128)(2,1)S(1)} %get-tuple-element.159), channel_id=1, source_target_pairs={{0,8},{4,12},{8,0},{12,4},{16,24},{20,28},{24,16},{28,20},{1,9},{5... | collective-permute-start | bytes 196616 | tf_op jit(solution)/shard_map/ppermute | solution.py:678
  116.2 15.4 %collective-permute-start.28 = (bf16[128,256]{1,0:T(8,128)(2,1)S(1)}, bf16[128,256]{1,0:T(8,128)(2,1)S(1)}, u32[]{:S(2)}, u32[]{:S(2)}) collective-permute-start(bf16[128,256]{1,0:T(8,128)(2,1)S(1)} %get-tuple-element.160), channel_id=1, source_target_pairs={{0,16},{4,20},{8,24},{12,28},{16,0},{20,4},{24,8},{28,12},{1,17},{... | collective-permute-start | bytes 196616 | tf_op jit(solution)/shard_map/ppermute | solution.py:678
  118.2 16.2 %collective-permute-start.29 = (bf16[128,256]{1,0:T(8,128)(2,1)S(1)}, bf16[128,256]{1,0:T(8,128)(2,1)S(1)}, u32[]{:S(2)}, u32[]{:S(2)}) collective-permute-start(bf16[128,256]{1,0:T(8,128)(2,1)S(1)} %get-tuple-element.161), channel_id=1, source_target_pairs={{0,24},{4,28},{8,16},{12,20},{16,8},{20,12},{24,0},{28,4},{1,25},{... | collective-permute-start | bytes 196616 | tf_op jit(solution)/shard_map/ppermute | solution.py:678
  141.3 15.8 %collective-permute-start.40 = (bf16[192,768]{1,0:T(8,128)(2,1)S(1)}, bf16[192,768]{1,0:T(8,128)(2,1)S(1)}, u32[]{:S(2)}, u32[]{:S(2)}) collective-permute-start(bf16[192,768]{1,0:T(8,128)(2,1)S(1)} %get-tuple-element.176.refs_3_), channel_id=1, source_target_pairs={{0,4},{4,0},{8,12},{12,8},{16,20},{20,16},{24,28},{28,24},{1,5},{5... | collective-permute-start | bytes 884744 | tf_op jit(solution)/shard_map/ppermute | solution.py:678
  142.9 14.2 %collective-permute-start.31 = (bf16[128,256]{1,0:T(8,128)(2,1)S(1)}, bf16[128,256]{1,0:T(8,128)(2,1)S(1)}, u32[]{:S(2)}, u32[]{:S(2)}) collective-permute-start(bf16[128,256]{1,0:T(8,128)(2,1)S(1)} %get-tuple-element.169), channel_id=1, source_target_pairs={{0,8},{4,12},{8,0},{12,4},{16,24},{20,28},{24,16},{28,20},{1,9},{5... | collective-permute-start | bytes 196616 | tf_op jit(solution)/shard_map/ppermute | solution.py:678
  152.7 14.5 %collective-permute-start.36 = (bf16[128,384]{1,0:T(8,128)(2,1)S(1)}, bf16[128,384]{1,0:T(8,128)(2,1)S(1)}, u32[]{:S(2)}, u32[]{:S(2)}) collective-permute-start(bf16[128,384]{1,0:T(8,128)(2,1)S(1)} %get-tuple-element.178), channel_id=1, source_target_pairs={{0,8},{4,12},{8,0},{12,4},{16,24},{20,28},{24,16},{28,20},{1,9},{5... | collective-permute-start | bytes 294920 | tf_op jit(solution)/shard_map/ppermute | solution.py:678
  152.7 14.4 %collective-permute-start.37 = (bf16[128,384]{1,0:T(8,128)(2,1)S(1)}, bf16[128,384]{1,0:T(8,128)(2,1)S(1)}, u32[]{:S(2)}, u32[]{:S(2)}) collective-permute-start(bf16[128,384]{1,0:T(8,128)(2,1)S(1)} %get-tuple-element.179), channel_id=1, source_target_pairs={{0,16},{4,20},{8,24},{12,28},{16,0},{20,4},{24,8},{28,12},{1,17},{... | collective-permute-start | bytes 294920 | tf_op jit(solution)/shard_map/ppermute | solution.py:678
  171.2 20.6 %collective-permute-start.49 = (bf16[512,640]{1,0:T(8,128)(2,1)S(1)}, bf16[512,640]{1,0:T(8,128)(2,1)S(1)}, u32[]{:S(2)}, u32[]{:S(2)}) collective-permute-start(bf16[512,640]{1,0:T(8,128)(2,1)S(1)} %get-tuple-element.198), channel_id=1, source_target_pairs={{0,4},{4,0},{8,12},{12,8},{16,20},{20,16},{24,28},{28,24},{1,5},{5... | collective-permute-start | bytes 1966088 | tf_op jit(solution)/shard_map/ppermute | solution.py:678
  176.6 14.6 %collective-permute-start.51 = (bf16[96,768]{1,0:T(8,128)(2,1)S(1)}, bf16[96,768]{1,0:T(8,128)(2,1)S(1)}, u32[]{:S(2)}, u32[]{:S(2)}) collective-permute-start(bf16[96,768]{1,0:T(8,128)(2,1)S(1)} %get-tuple-element.184.refs_13_), channel_id=1, source_target_pairs={{0,16},{4,20},{8,24},{12,28},{16,0},{20,4},{24,8},{28,12},{1,17},{... | collective-permute-start | bytes 442376 | tf_op jit(solution)/shard_map/ppermute | solution.py:678
  192.6 28.2 %collective-permute-start.52 = (bf16[256,640]{1,0:T(8,128)(2,1)S(1)}, bf16[256,640]{1,0:T(8,128)(2,1)S(1)}, u32[]{:S(2)}, u32[]{:S(2)}) collective-permute-start(bf16[256,640]{1,0:T(8,128)(2,1)S(1)} %get-tuple-element.203), channel_id=1, source_target_pairs={{0,8},{4,12},{8,0},{12,4},{16,24},{20,28},{24,16},{28,20},{1,9},{5... | collective-permute-start | bytes 983048 | tf_op jit(solution)/shard_map/ppermute | solution.py:678
  194.7 14.0 %collective-permute-start.58 = (bf16[96,768]{1,0:T(8,128)(2,1)S(1)}, bf16[96,768]{1,0:T(8,128)(2,1)S(1)}, u32[]{:S(2)}, u32[]{:S(2)}) collective-permute-start(bf16[96,768]{1,0:T(8,128)(2,1)S(1)} %out_sum.1.refs_3_.refs_1_), channel_id=1, source_target_pairs={{0,16},{4,20},{8,24},{12,28},{16,0},{20,4},{24,8},{28,12},{1,17},{... | collective-permute-start | bytes 442376 | tf_op jit(solution)/shard_map/ppermute | solution.py:678
  221.6 35.8 %collective-permute-start.23 = (f32[256,768]{1,0:T(8,128)S(1)}, f32[256,768]{1,0:T(8,128)S(1)}, u32[]{:S(2)}, u32[]{:S(2)}) collective-permute-start(f32[256,768]{1,0:T(8,128)S(1)} %get-tuple-element.150), channel_id=1, source_target_pairs={{0,1},{1,0},{2,3},{3,2},{4,5},{5,4},{6,7},{7,6},{8,9},{9,8},{10,11... | collective-permute-start | bytes 2359304 | tf_op jit(solution)/shard_map/ppermute | solution.py:675
  246.2 19.4 %collective-permute-start.68 = (bf16[384,768]{1,0:T(8,128)(2,1)S(1)}, bf16[384,768]{1,0:T(8,128)(2,1)S(1)}, u32[]{:S(2)}, u32[]{:S(2)}) collective-permute-start(bf16[384,768]{1,0:T(8,128)(2,1)S(1)} %out_four.1.refs_3_), channel_id=1, source_target_pairs={{0,4},{4,0},{8,12},{12,8},{16,20},{20,16},{24,28},{28,24},{1,5},{5... | collective-permute-start | bytes 1769480 | tf_op jit(solution)/shard_map/ppermute | solution.py:678
  256.4 19.3 %collective-permute-start.66 = (bf16[512,640]{1,0:T(8,128)(2,1)S(1)}, bf16[512,640]{1,0:T(8,128)(2,1)S(1)}, u32[]{:S(2)}, u32[]{:S(2)}) collective-permute-start(bf16[512,640]{1,0:T(8,128)(2,1)S(1)} %attn_four.1), channel_id=1, source_target_pairs={{0,4},{4,0},{8,12},{12,8},{16,20},{20,16},{24,28},{28,24},{1,5},{5... | collective-permute-start | bytes 1966088 | tf_op jit(solution)/shard_map/ppermute | solution.py:678
  257.1 15.2 %collective-permute-start.67 = (bf16[384,768]{1,0:T(8,128)(2,1)S(1)}, bf16[384,768]{1,0:T(8,128)(2,1)S(1)}, u32[]{:S(2)}, u32[]{:S(2)}) collective-permute-start(bf16[384,768]{1,0:T(8,128)(2,1)S(1)} %fc_four.1.refs_4_), channel_id=1, source_target_pairs={{0,8},{4,12},{8,0},{12,4},{16,24},{20,28},{24,16},{28,20},{1,9},{5... | collective-permute-start | bytes 1769480 | tf_op jit(solution)/shard_map/ppermute | solution.py:678
  258.7 15.8 %collective-permute-start.46 = (f32[8,768]{1,0:T(8,128)S(1)}, f32[8,768]{1,0:T(8,128)S(1)}, u32[]{:S(2)}, u32[]{:S(2)}) collective-permute-start(f32[8,768]{1,0:T(8,128)S(1)} %add.46.refs_1_.refs_4_), channel_id=1, source_target_pairs={{0,8},{4,12},{8,0},{12,4},{16,24},{20,28},{24,16},{28,20},{1,9},{5... | collective-permute-start | bytes 73736 | tf_op jit(solution)/shard_map/ppermute | solution.py:678
  (70 other events, 508.2 us)

commit v4 on v3

v4 whole, which is shorter than its diff:
```python
from functools import partial

import jax
import jax.numpy as jnp
from jax import lax
from jax.experimental import pallas as pl
from jax.experimental.pallas import tpu as pltpu
from jax.sharding import PartitionSpec as P

HD = 64
LAYERS = 12
EPSILON = 1e-05
BF = jnp.bfloat16
F32 = jnp.float32
RESIDUAL = LAYERS ** (-0.5)
SCORE = HD ** (-0.5)
NEVER = -1e30
OUT_STEPS, FC_STEPS = (1, 2, 4), (2, 1, 4)
MERGE_PERMUTES = False


def shape(dims, kind):
    return jax.ShapeDtypeStruct(dims, kind)


def call(body, name, outs, *args, scratch=(), after=(), us=1.0, mib=16):
    vmem = pl.BlockSpec(memory_space=pltpu.VMEM)
    smem = pl.BlockSpec(memory_space=pltpu.SMEM)
    held = pl.BlockSpec(memory_space=pl.ANY)
    count, waits = len(args), len(after)

    def run(*refs):
        body(*refs[:count], *refs[count + waits :])

    return pl.pallas_call(
        run,
        name=name,
        out_shape=outs,
        in_specs=[smem] + [vmem] * (count - 1) + [held] * waits,
        out_specs=[vmem] * len(outs),
        scratch_shapes=list(scratch),
        cost_estimate=pl.CostEstimate(flops=int(us * 1e3), transcendentals=0, bytes_accessed=int(us * 1e3)),
        compiler_params=pltpu.CompilerParams(vmem_limit_bytes=mib * 1024 * 1024),
    )(*args, *after)


def rows_at(index, size):
    return pl.ds(pl.multiple_of(index * size, size), size)


def dot(first, second):
    return jnp.dot(first, second, preferred_element_type=F32)


def dot_rows(first, second):
    return lax.dot_general(first, second, (((0,), (0,)), ((), ())), preferred_element_type=F32)


def dot_columns(first, second):
    return lax.dot_general(first, second, (((1,), (1,)), ((), ())), preferred_element_type=F32)


def normalize(values):
    center = jnp.mean(values, axis=-1, keepdims=True)
    centered = values - center
    spread = jnp.mean(centered * centered, axis=-1, keepdims=True)
    scale = lax.rsqrt(spread + EPSILON)
    return centered * scale, scale


def norm_back(grad, unit, scale, gain):
    inner = grad * gain
    mean_inner = jnp.mean(inner, axis=-1, keepdims=True)
    mean_along = jnp.mean(inner * unit, axis=-1, keepdims=True)
    return scale * (inner - mean_inner - unit * mean_along)


def join(at, pieces, whole):
    size = pieces[0].shape[0]
    for k, piece in enumerate(pieces):
        whole[rows_at(at[2] ^ k, size), :] = piece[...]


def as_row(ref):
    return ref[...].astype(F32).reshape(1, ref.shape[0])


def attn_columns_body(parts, at, attn, *pieces):
    features = attn.shape[1] // 3
    width = features // parts
    for owner in range(parts):

        @pl.when(at[2] == owner)
        def _():
            for k in range(parts):
                first = (owner ^ k) * width
                piece = pieces[k]
                piece[:, :width] = attn[:, first : first + width]
                piece[:, width:256] = jnp.zeros((width, 256 - width), BF)
                key = attn[:, features + first : features + first + width]
                value = attn[:, 2 * features + first : 2 * features + first + width]
                piece[:, 256:384] = key[:, :128]
                piece[:, 384:512] = value[:, :128]
                piece[:, 512 : 512 + HD] = key[:, 128:]
                piece[:, 512 + HD :] = value[:, 128:]


def token_message_body(at, tokens, *refs):
    vectors, out = refs[:-1], refs[-1]
    rows, width = tokens.shape[0], vectors[0].shape[0]
    out[:rows, :] = tokens[...]
    small = jnp.concatenate([as_row(ref) for ref in vectors] + [jnp.zeros((8 - len(vectors), width), F32)], axis=0)
    rest = jnp.zeros((8, tokens.shape[1] - width), F32)
    out[rows:, :] = jnp.concatenate([small, rest], axis=1).astype(BF)


def fc_columns_body(at, fc, *pieces):
    for k, piece in enumerate(pieces):
        hidden = piece.shape[1]
        piece[...] = fc[:, pl.ds(pl.multiple_of((at[2] ^ k) * hidden, 128), hidden)]


def join_body(at, *refs):
    join(at, refs[:-1], refs[-1])


def block_of(at, k, rows):
    return rows_at(at[2] ^ at[0] ^ k, rows)


def mixed_body(parts, count, at, query_bias, value_bias, *refs):
    tokens, weights = refs[:parts], refs[parts : 2 * parts]
    normed, matrix, vectors, *outs, kept = refs[2 * parts :]
    rows = tokens[0].shape[0] - 8
    join(at, weights, matrix)
    columns = matrix.shape[1]
    width = weights[0].shape[0]
    for owner in range(parts):

        @pl.when(at[2] == owner)
        def _():
            for k in range(parts):
                lanes = slice((owner ^ k) * width, ((owner ^ k) + 1) * width)
                vectors[:, lanes] = tokens[k][rows:, :width].astype(F32)

    small = vectors[...]
    for k in range(parts):
        unit, _ = normalize(tokens[k][:rows, :].astype(F32))
        normed[k * rows : (k + 1) * rows, :] = (unit * small[0:1] + small[1:2]).astype(BF)
    query, value = as_row(query_bias), as_row(value_bias)
    none = jnp.zeros((1, 128), F32)
    bias = [query, none[:, :HD], none, value[:, :128], none[:, :HD], value[:, 128:]]
    bias = jnp.concatenate(bias, axis=1)
    kept[...] = (dot(normed[...], matrix[...]) + bias).astype(BF)
    half = rows // 2
    third = normed.shape[1] // 6
    first = (at[2] % 2) * 3 * third
    for k in range(count):
        block = block_of(at, k, rows)
        outs[k][:rows, :] = kept[block, :256]
        part = normed[block, pl.ds(pl.multiple_of(first, 128), 3 * third)]
        outs[k][rows : 2 * rows, :] = part[:, : 2 * third]
        outs[k][2 * rows :, :third] = part[:half, 2 * third :]
        outs[k][2 * rows :, third:] = part[half:, 2 * third :]
        outs[count + k][...] = kept[block, 256:]


def normed_stack_body(rows, at, *refs):
    half = rows // 2
    out = refs[-1]
    third = out.shape[1] // 3
    for k, ref in enumerate(refs[:-1]):
        part = slice(k * rows, (k + 1) * rows)
        out[part, : 2 * third] = ref[rows : 2 * rows, :]
        out[k * rows : k * rows + half, 2 * third :] = ref[2 * rows :, :third]
        out[k * rows + half : (k + 1) * rows, 2 * third :] = ref[2 * rows :, third:]


def normed_place_body(count, blocks, rows, at, *refs):
    sides, (every, own) = refs[:-2], refs[-2:]
    lanes = sides[0].shape[1]
    core = at[2] % 2
    for side in range(2):
        part = pl.ds(pl.multiple_of((core if side == 0 else 1 - core) * lanes, 128), lanes)
        for j in range(blocks):
            ref = sides[side * blocks + j]
            for k in range(count):
                row = at[0] ^ k
                piece = ref[k * rows : (k + 1) * rows, :]
                every[rows_at(row * blocks + (at[1] ^ j), rows), part] = piece
                if j == 0:
                    own[rows_at(row, rows), part] = piece


def place(at, count, blocks, rows, queries, pairs, partners, q_all, kv_all):
    for k in range(count):
        row = at[0] ^ k
        q_all[rows_at(row, rows), :] = queries[k][:rows, :]
        kv_all[rows_at(row * blocks + at[1], rows), :] = pairs[k][...]
        for j, partner in enumerate(partners):
            side = row * blocks + (at[1] ^ (j + 1))
            kv_all[rows_at(side, rows), :] = partner[k * rows : (k + 1) * rows, :]


def head_views(tile_one, tile_two, scale):
    low = lax.broadcasted_iota(jnp.int32, tile_one.shape, 1) < HD
    zero = jnp.zeros_like(tile_one)
    tile_one = tile_one * scale if scale is not None else tile_one
    tile_two = tile_two * scale if scale is not None else tile_two
    return (jnp.where(low, tile_one, zero), jnp.where(low, zero, tile_one), tile_two)


def visible_keys(at, i, blocks, rows, keys):
    query = (i * blocks + at[1]) * rows + lax.broadcasted_iota(jnp.int32, (rows, keys), 0)
    return lax.broadcasted_iota(jnp.int32, (rows, keys), 1) <= query


def attend_body(count, blocks, rows, at, *refs):
    queries, pairs = refs[:count], refs[count : 2 * count]
    partners = refs[2 * count : 2 * count + blocks - 1]
    outs = refs[2 * count + blocks - 1 :]
    pieces, (exact, totals, q_all, kv_all) = outs[:count], outs[count:]
    place(at, count, blocks, rows, queries, pairs, partners, q_all, kv_all)
    low = lax.broadcasted_iota(jnp.int32, (rows, 128), 1) < HD
    for i in range(count):
        keys = (i + 1) * blocks * rows
        mine = slice(i * rows, (i + 1) * rows)
        heads = head_views(q_all[mine, :128], q_all[mine, 128:], SCORE)
        seen = visible_keys(at, i, blocks, rows, keys)
        found = []
        for h, query in enumerate(heads):
            key_cols = slice(0, 128) if h < 2 else slice(256, 384)
            value_cols = slice(128, 256) if h < 2 else slice(256, 384)
            scores = jnp.where(seen, dot_columns(query, kv_all[:keys, key_cols]), NEVER)
            highest = jnp.max(scores, axis=-1, keepdims=True)
            weights = jnp.exp(scores - highest)
            total = jnp.sum(weights, axis=-1, keepdims=True)
            totals[mine, h : h + 1] = highest + jnp.log(total)
            weights = (weights * (1.0 / total)).astype(BF)
            found.append(dot(weights, kv_all[:keys, value_cols]))
        exact[mine, :128] = jnp.where(low, found[0], found[1])
        exact[mine, 128:] = jnp.where(low, 0.0, found[2])
    half = rows // 2
    for k in range(count):
        block = rows_at(at[0] ^ k, rows)
        pieces[k][:rows, :] = exact[block, :128].astype(BF)
        last = exact[block, 128:]
        pair = jnp.where(low[:half], pltpu.roll(last[:half], HD, 1), last[half:])
        pieces[k][rows:, :] = pair.astype(BF)


def attend_back_body(count, blocks, rows, at, *refs):
    grads, (q_all, kv_all, exact, totals) = refs[:count], refs[count : count + 4]
    outs = refs[count + 4 :]
    own, away, dq_all, summed, g_all, acc = outs
    for k in range(count):
        g_all[rows_at(at[0] ^ k, rows), :] = grads[k][...]
    acc[...] = jnp.zeros_like(acc)
    low = lax.broadcasted_iota(jnp.int32, (rows, 128), 1) < HD
    for i in range(count):
        keys = (i + 1) * blocks * rows
        mine = slice(i * rows, (i + 1) * rows)
        q_heads = head_views(q_all[mine, :128], q_all[mine, 128:], SCORE)
        g_heads = head_views(g_all[mine, :128], g_all[mine, 128:], None)
        seen = visible_keys(at, i, blocks, rows, keys)
        found = []
        for h in range(3):
            key_cols = slice(0, 128) if h < 2 else slice(256, 384)
            value_cols = slice(128, 256) if h < 2 else slice(256, 384)
            kept = exact[mine, :128] if h < 2 else exact[mine, 128:]
            delta = jnp.sum(g_heads[h].astype(F32) * kept, axis=-1, keepdims=True)
            scores = dot_columns(q_heads[h], kv_all[:keys, key_cols]) - totals[mine, h : h + 1]
            weights = jnp.exp(jnp.where(seen, scores, NEVER))
            g_weights = dot_columns(g_heads[h], kv_all[:keys, value_cols])
            g_scores = (weights * (g_weights - delta)).astype(BF)
            found.append(dot(g_scores, kv_all[:keys, key_cols]))
            acc[:keys, key_cols] += dot_rows(g_scores, q_heads[h])
            acc[:keys, value_cols] += dot_rows(weights.astype(BF), g_heads[h])
        dq_all[mine, :128] = (jnp.where(low, found[0], found[1]) * SCORE).astype(BF)
        dq_all[mine, 128:] = (jnp.where(low, found[2], 0.0) * SCORE).astype(BF)
    summed[...] = acc[...].astype(BF)
    for i in range(count):
        into = slice(i * rows, (i + 1) * rows)
        own[into, :] = acc[rows_at(i * blocks + at[1], rows), :]
        for j in range(1, blocks):
            from_rows = slice(((j - 1) * count + i) * rows, ((j - 1) * count + i + 1) * rows)
            away[from_rows, :] = acc[rows_at(i * blocks + (at[1] ^ j), rows), :].astype(BF)


def plain_heads(values):
    zero = jnp.zeros_like(values[:, :HD])
    first = jnp.concatenate([values[:, :HD], zero], 1)
    second = jnp.concatenate([zero, values[:, HD:128]], 1)
    return (first, second, values[:, 128:])


def plain_terms(at, count, blocks, rows):
    q_pos = (jnp.arange(count)[:, None] * blocks + at[1]) * rows + jnp.arange(rows)[None]
    k_pos = jnp.arange(count * blocks * rows)
    return k_pos[None] <= q_pos.reshape(-1)[:, None]


def plain_attend(count, blocks, rows, at, queries, pairs, partners):
    width = pairs[0].shape[1]
    q_all = jnp.zeros((count, rows, queries[0].shape[1]), BF)
    kv_all = jnp.zeros((count, blocks, rows, width), BF)
    for k in range(count):
        row = at[0] ^ k
        q_all = q_all.at[row].set(queries[k][:rows])
        kv_all = kv_all.at[row, at[1]].set(pairs[k])
        for j, partner in enumerate(partners):
            kv_all = kv_all.at[row, at[1] ^ (j + 1)].set(partner[k * rows : (k + 1) * rows])
    q_all, kv_all = q_all.reshape(count * rows, -1), kv_all.reshape(-1, width)
    seen = plain_terms(at, count, blocks, rows)
    found, totals = [], []
    for h, query in enumerate(plain_heads(q_all)):
        key = kv_all[:, :128] if h < 2 else kv_all[:, 256:]
        value = kv_all[:, 128:256] if h < 2 else kv_all[:, 256:]
        scores = jnp.where(seen, dot_columns(query, key) * SCORE, NEVER)
        total = jax.nn.logsumexp(scores, axis=-1, keepdims=True)
        found.append(dot(jnp.exp(scores - total).astype(BF), value))
        totals.append(total)
    exact = jnp.concatenate([found[0][:, :HD], found[1][:, HD:], jnp.zeros_like(found[2][:, :HD]), found[2][:, HD:]], 1)
    grid = exact.astype(BF).reshape(count, rows, -1)
    half = rows // 2
    pair = jnp.concatenate([grid[:, :half, 128 + HD :], grid[:, half:, 128 + HD :]], 2)
    grid = jnp.concatenate([grid[:, :, :128], pair], 1)
    pieces = [grid[at[0] ^ k] for k in range(count)]
    totals = jnp.concatenate(totals + [jnp.zeros((count * rows, 125), F32)], 1)
    return (*pieces, exact, totals, q_all, kv_all)


def plain_attend_back(count, blocks, rows, at, grads, q_all, kv_all, exact, totals):
    g_all = jnp.zeros((count, rows, grads[0].shape[1]), BF)
    for k in range(count):
        g_all = g_all.at[at[0] ^ k].set(grads[k])
    g_all = g_all.reshape(count * rows, -1)
    seen = plain_terms(at, count, blocks, rows)
    dq, parts = [], []
    for h, (query, grad, kept) in enumerate(zip(plain_heads(q_all), plain_heads(g_all), plain_heads(exact))):
        key = kv_all[:, :128] if h < 2 else kv_all[:, 256:]
        value = kv_all[:, 128:256] if h < 2 else kv_all[:, 256:]
        delta = jnp.sum(grad.astype(F32) * kept, axis=-1, keepdims=True)
        scores = dot_columns(query, key) * SCORE - totals[:, h : h + 1]
        weights = jnp.exp(jnp.where(seen, scores, NEVER))
        g_scores = (weights * (dot_columns(grad, value) - delta)).astype(BF)
        dq.append(dot(g_scores, key) * SCORE)
        parts.append((dot_rows(g_scores, query) * SCORE, dot_rows(weights.astype(BF), grad)))
    dq = jnp.concatenate([dq[0][:, :HD], dq[1][:, HD:], dq[2][:, :HD], jnp.zeros_like(dq[2][:, :HD])], 1)
    dq = dq.astype(BF).reshape(count, rows, -1)
    acc = jnp.concatenate([parts[0][0] + parts[1][0], parts[0][1] + parts[1][1], parts[2][0] + parts[2][1]], 1)
    acc = acc.reshape(count, blocks, rows, -1)
    dq_all, summed = dq.reshape(count * rows, -1), acc.reshape(-1, acc.shape[-1]).astype(BF)
    own = jnp.concatenate([acc[i, at[1]] for i in range(count)], 0)
    away = [acc[i, at[1] ^ j].astype(BF) for j in range(1, blocks) for i in range(count)]
    return (own, jnp.concatenate(away, 0), dq_all, summed)


def merge_body(at, dq, own, *refs):
    arrived, out = refs[:-1], refs[-1]
    total = own[...]
    for ref in arrived:
        total = total + ref[...].astype(F32)
    out[:, :256] = dq[...]
    out[:, 256:] = total.astype(BF)


def gelu_terms(hidden):
    root = 0.7978845608028654
    square = hidden * hidden
    bend = jnp.tanh(root * hidden * (1.0 + 0.044715 * square))
    half = 0.5 * (1.0 + bend)
    slope = half + 0.5 * hidden * (1.0 - bend * bend) * root * (1.0 + 3.0 * 0.044715 * square)
    return hidden * half, slope


def g_output(extras, rows):
    return jnp.concatenate([(RESIDUAL * ref[:rows, :].astype(F32)).astype(BF) for ref in extras], axis=0)


def split_rows(values, rows, mine, other):
    mine[:rows, :] = values[:rows]
    mine[rows:, :] = values[2 * rows : 3 * rows]
    other[:rows, :] = values[rows : 2 * rows]
    other[rows:, :] = values[3 * rows :]


def middle_body(parts, rows, at, attended, vectors, fc, fc_bias, out, *refs):
    tokens, extras = refs[:parts], refs[parts : 2 * parts]
    gn_mine, gn_other, mid_mine, normed, active, g_hidden, own, att_all, proj = refs[2 * parts :]
    zero = jnp.zeros((HD, proj.shape[1]), BF)
    half = rows // 2
    low = lax.broadcasted_iota(jnp.int32, (half, 128), 1) < HD
    for k in range(parts):
        weight = extras[k][rows:, :]
        owner = at[2] ^ k
        packed = jnp.concatenate([weight[:128], zero, weight[128:]], axis=0)
        proj[rows_at(owner, 256), :] = packed
    size = rows + half
    for j in range(parts):
        for k in range(parts):
            piece = attended[j, k * size : (k + 1) * size, :]
            pair = piece[rows:].astype(F32)
            upper = jnp.where(low, 0.0, pltpu.roll(pair, HD, 1)).astype(BF)
            lower = jnp.where(low, 0.0, pair).astype(BF)
            block = block_of(at, k, rows)
            att_all[block, j * 256 : j * 256 + 128] = piece[:rows]
            att_all[block, j * 256 + 128 : (j + 1) * 256] = jnp.concatenate([upper, lower], axis=0)
    own[...] = att_all[:, pl.ds(pl.multiple_of(at[2] * 256, 256), 256)]
    branch = dot(att_all[...], proj[...]) + vectors[4:5]
    for k in range(parts):
        part = slice(k * rows, (k + 1) * rows)
        value = tokens[k][:rows, :].astype(F32) + RESIDUAL * branch[part]
        if k % 2 == 0:
            mid_mine[(k // 2) * rows : (k // 2 + 1) * rows, :] = value
        unit, _ = normalize(value)
        normed[part, :] = (unit * vectors[2:3] + vectors[3:4]).astype(BF)
    hidden = dot(normed[...], fc[...]) + as_row(fc_bias)
    value, slope = gelu_terms(hidden)
    active[...] = value.astype(BF)
    g_hidden[...] = (dot_columns(g_output(extras, rows), out[...]) * slope).astype(BF)
    split_rows(dot_columns(g_hidden[...], fc[...]), rows, gn_mine, gn_other)


def fill_half(half, bit, kept, away, chunk):
    size = kept.shape[0] // half
    for i in range(half):
        into = slice(i * size, (i + 1) * size)
        kept[into, :] = chunk(bit * half + i)
        away[into, :] = chunk((1 - bit) * half + i).astype(BF)


def proj_grad(attended, g_branch):
    grad = dot_rows(attended[...], g_branch[...])
    return jnp.concatenate([grad[:128], grad[128 + HD :]], axis=0)


def proj_grad_body(rows, at, attended, g_branch, sums_in, grad, sums):
    grad[...] = proj_grad(attended, g_branch)
    sums[...] = sums_in[...]
    sums[4:5, :] = jnp.sum(g_branch[:rows, :].astype(F32), axis=0, keepdims=True)


def pack_wide(values, lanes):
    third = values.shape[0] // 3
    rest = values[:, lanes:]
    low = [rest[i * third : (i + 1) * third] for i in range(3)]
    low.append(jnp.zeros((third, lanes - 384), values.dtype))
    return jnp.concatenate([values[:, :lanes], jnp.concatenate(low, axis=1)], axis=0)


def out_partial_body(rows, at, active, out, mine, other):
    split_rows(dot(active[...], out[...]), rows, mine, other)


def out_weights_body(rows, step, at, active, sums_in, *refs):
    extras = refs[:-4]
    kept, away, sums, grad = refs[-4:]
    g_out = g_output(extras, rows)
    grad[...] = dot_rows(active[...], g_out)
    half = kept.shape[0]
    bit = (at[3] // step) % 2
    kept[...] = grad[rows_at(bit, half), :]
    away[...] = grad[rows_at(1 - bit, half), :].astype(BF)
    sums[...] = sums_in[...]
    sums[5:6, :] = jnp.sum(g_out[:rows].astype(F32), axis=0, keepdims=True)


def fc_weights_body(parts, half, step, at, normed, g_hidden, sums_in, kept, away, sums, grad):
    grad[...] = dot_rows(normed[...], g_hidden[...])
    size = grad.shape[0] // (parts * 2 * half)

    def chunk(i):
        blocks = [((at[2] ^ j) * 2 * half + i) * size for j in range(parts)]
        return jnp.concatenate([grad[pl.ds(pl.multiple_of(start, 8), size), :] for start in blocks], axis=0)

    fill_half(half, (at[3] // step) % 2, kept, away, chunk)
    sums[...] = sums_in[...]
    sums[6:7, :] = jnp.sum(g_hidden[...].astype(F32), axis=0, keepdims=True)


def plain_weights_body(rows, at, active, normed, g_hidden, sums_in, *refs):
    extras = refs[:-3]
    out_grad, fc_grad, sums = refs[-3:]
    g_out = g_output(extras, rows)
    out_grad[...] = dot_rows(active[...], g_out).astype(BF)
    fc_grad[...] = dot_rows(normed[...], g_hidden[...]).astype(BF)
    sums[...] = sums_in[...]
    sums[5:6, :] = jnp.sum(g_out[:rows].astype(F32), axis=0, keepdims=True)
    sums[6:7, :] = jnp.sum(g_hidden[...].astype(F32), axis=0, keepdims=True)


def second_norm_body(rows, at, chip_sum, arrived, mid, own_extra, x_extra, vectors, sums_in, g_branch, own_middle, sums):
    add = arrived[...].astype(F32)
    grad = chip_sum[...] + jnp.concatenate([add[rows:], add[:rows]], axis=0)
    unit, scale = normalize(mid[...])
    back = norm_back(grad, unit, scale, vectors[2:3])
    sums[...] = sums_in[...]
    sums[2:3, :] = jnp.sum(grad[:rows] * unit[:rows], axis=0, keepdims=True)
    sums[3:4, :] = jnp.sum(grad[:rows], axis=0, keepdims=True)
    g_own = back[:rows] + own_extra[:rows, :].astype(F32)
    own_middle[...] = g_own
    g_branch[:rows, :] = (RESIDUAL * g_own).astype(BF)
    g_branch[rows:, :] = (RESIDUAL * (back[rows:] + x_extra[:rows, :].astype(F32))).astype(BF)


def attended_grad_body(parts, rows, at, mine, other, proj, *refs):
    outs, (kept, g_all) = refs[:parts], refs[parts:]
    kept[:rows, :] = mine[:rows, :]
    kept[rows : 2 * rows, :] = other[:rows, :]
    kept[2 * rows : 3 * rows, :] = mine[rows:, :]
    kept[3 * rows :, :] = other[rows:, :]
    zero = jnp.zeros((HD, proj.shape[1]), BF)
    weight = jnp.concatenate([proj[:128, :], zero, proj[128:, :]], axis=0)
    g_all[...] = dot_columns(kept[...], weight).astype(BF)
    for k in range(parts):
        outs[k][...] = g_all[block_of(at, k, rows), :]


def merge_pieces_body(rows, at, dq, own, arrived, *outs):
    for k, out in enumerate(outs):
        part = rows_at(at[0] ^ k, rows)
        out[:, :256] = dq[part, :]
        out[:, 256:] = (own[part, :] + arrived[part, :].astype(F32)).astype(BF)


def first_grad_body(parts, rows, at, matrix, *refs):
    pieces, (mine, other, mixed) = refs[:-3], refs[-3:]
    for i in range(parts):
        if len(pieces) == 1:
            mixed[rows_at(at[2] ^ i, rows), :] = pieces[0][i * rows : (i + 1) * rows, :]
        else:
            mixed[block_of(at, i, rows), :] = pieces[i][...]
    split_rows(dot_columns(mixed[...], matrix[...]), rows, mine, other)


def attn_halves_body(parts, count, at, own, every, dq, dkv, proj, kept, away, sums, grad):
    grad[:, :256] = dot_rows(own[...], dq[...])
    grad[:, 256:] = dot_rows(every[...], dkv[...])
    owner_rows = grad.shape[0] // parts
    size = owner_rows // (2 * count)
    packed = size + size // 3
    start = 0
    for k in range(count):
        place = at[1] * count + (at[0] ^ k)
        other = (1 - at[1]) * count + (at[0] ^ k)
        for j in range(parts):
            base = (at[2] ^ j) * 2 * count
            kept[start : start + size, :] = grad[rows_at(base + place, size), :]
            away[start : start + size, :] = grad[rows_at(base + other, size), :].astype(BF)
            start += size
        kept[start : start + packed, :] = pack_wide(proj[rows_at(place, size), :], grad.shape[1])
        away[start : start + packed, :] = pack_wide(proj[rows_at(other, size), :], grad.shape[1]).astype(BF)
        start += packed
    sums[...] = jnp.zeros_like(sums)
    sums[0:1, :256] = jnp.sum(dq[...].astype(F32), axis=0, keepdims=True)
    sums[0:1, 256:] = jnp.sum(dkv[...].astype(F32), axis=0, keepdims=True)


def attn_pair_body(at, kept, arrived, *outs):
    size = outs[0].shape[0]
    for k, out in enumerate(outs):
        part = slice(k * size, (k + 1) * size)
        out[...] = (kept[part, :] + arrived[part, :].astype(F32)).astype(out.dtype)


def attn_fold_body(count, at, *refs):
    total = refs[0][...]
    for ref in refs[1:count]:
        total = total + ref[...].astype(F32)
    start = 0
    for out in refs[count:]:
        out[...] = total[start : start + out.shape[0]].astype(BF)
        start += out.shape[0]


def attn_place_body(parts, count, at, *refs):
    own, away, (out, proj, kept) = refs[:count], refs[count], refs[count + 1 :]
    features = proj.shape[1]
    width, lanes = features // parts, kept.shape[2]
    size = width // (2 * count)
    total = own[0].shape[0]
    for side in range(2):
        block = at[1] if side == 0 else 1 - at[1]
        for k in range(count):
            piece = own[k][...] if side == 0 else away[k * total : (k + 1) * total, :]
            piece = piece.astype(F32)
            rows = rows_at(block * count + (at[0] ^ k), size)
            for j in range(parts):
                kept[at[2] ^ j, rows, :] = piece[j * size : (j + 1) * size]
            start = parts * size
            proj[rows, :lanes] = piece[start : start + size]
            low = piece[start + size :]
            proj[rows, lanes:] = jnp.concatenate([low[:, i * 128 : (i + 1) * 128] for i in range(3)], axis=0)
    for g in range(parts):
        first = g * width
        out[:, first : first + width] = kept[g, :, :width]
        first += features
        out[:, first : first + width] = jnp.concatenate([kept[g, :, 256:384], kept[g, :, 512 : 512 + HD]], axis=1)
        first += features
        out[:, first : first + width] = jnp.concatenate([kept[g, :, 384:512], kept[g, :, 512 + HD :]], axis=1)


def attn_weights_body(parts, ways, at, own, every, dq, dkv, grads, sums):
    query = dot_rows(own[...], dq[...])
    pair = dot_rows(every[...], dkv[...])
    size = query.shape[0] // (parts * ways)
    for c in range(ways):
        for j in range(parts):
            at_row = (j * ways + c) * size
            grads[c * parts + j, :, :256] = query[at_row : at_row + size].astype(BF)
            grads[c * parts + j, :, 256:] = pair[at_row : at_row + size].astype(BF)
    sums[...] = jnp.zeros_like(sums)
    sums[0:1, :256] = jnp.sum(dq[...].astype(F32), axis=0, keepdims=True)
    sums[0:1, 256:] = jnp.sum(dkv[...].astype(F32), axis=0, keepdims=True)


def attn_sum_body(parts, ways, at, arrived, out):
    for j in range(parts):
        total = arrived[j].astype(F32)
        for c in range(1, ways):
            total = total + arrived[c * parts + j].astype(F32)
        total = total.astype(BF)
        for c in range(ways):
            out[c, j, :, :] = total


def attn_final_body(parts, ways, at, arrived, out):
    size = arrived.shape[2]
    width = size * ways
    features = out.shape[1] // 3
    for c in range(ways):
        rows = slice(c * size, (c + 1) * size)
        for g in range(parts):
            piece = arrived[c, g].astype(F32)
            first = g * width
            out[rows, first : first + width] = piece[:, :width]
            first += features
            out[rows, first : first + width] = jnp.concatenate([piece[:, 256:384], piece[:, 512 : 512 + HD]], axis=1)
            first += features
            out[rows, first : first + width] = jnp.concatenate([piece[:, 384:512], piece[:, 512 + HD :]], axis=1)


def first_norm_body(rows, at, own, core, arrived, tokens, own_middle, vectors, sums, attn, input_grad, shares):
    grad = own[:rows, :] + core[:rows, :] + arrived[...].astype(F32)
    unit, scale = normalize(tokens[...].astype(F32))
    back = norm_back(grad, unit, scale, vectors[0:1])
    input_grad[...] = (back + own_middle[...]).astype(BF)
    first = [jnp.sum(grad * unit, axis=0, keepdims=True), jnp.sum(grad, axis=0, keepdims=True)]
    whole = jnp.concatenate(first + [sums[2:6, :], jnp.zeros((2, grad.shape[1]), F32)], axis=0)
    parts = whole.shape[1] // HD // 3
    width = whole.shape[1] // parts
    part = sums.shape[1] // 4
    value = jnp.concatenate([attn[0:1, 384:512], attn[0:1, 512 + HD :]], axis=1)
    local = [sums[6:7, i * part : (i + 1) * part] for i in range(4)] + [attn[0:1, :width], value]
    local = jnp.concatenate(local + [jnp.zeros((2, width), F32)], axis=0)
    blank = jnp.zeros((8, 256 - width), F32)
    for j in range(parts):
        piece = jnp.concatenate([whole[:, j * width : (j + 1) * width], blank, local, blank], axis=1)
        for c in range(shares.shape[0] // parts):
            shares[c * parts + j, :, :] = piece


def vector_final_body(ways, parts, at, arrived, *outs):
    width, hidden = outs[0].shape[0], outs[8].shape[0]
    total, local = jnp.zeros((8, arrived.shape[2]), F32), jnp.zeros((8, arrived.shape[2]), F32)
    for i in range(ways * parts):
        total = total + arrived[i]
    for c in range(ways):
        local = local + arrived[c * parts + at[2]]
    for row in range(6):
        outs[row][...] = total[row : row + 1, :width].reshape(width)
    part = hidden // 4
    outs[8][...] = jnp.concatenate([local[i : i + 1, 256 : 256 + part] for i in range(4)], axis=1).reshape(hidden)
    outs[6][...] = local[4:5, 256 : 256 + width].reshape(width)
    outs[7][...] = local[5:6, 256 : 256 + width].reshape(width)


def halve_body(step, at, held, arrived, kept, away, total):
    total[...] = held[...] + arrived[...].astype(F32)
    half = kept.shape[0]
    bit = (at[3] // step) % 2
    kept[...] = total[pl.ds(pl.multiple_of(bit * half, 8), half), :]
    away[...] = total[pl.ds(pl.multiple_of((1 - bit) * half, 8), half), :].astype(BF)


def last_sum_body(at, held, arrived, *outs):
    total = held[...] + arrived[...].astype(F32)
    start = 0
    for out in outs:
        out[...] = total[start : start + out.shape[0]].astype(BF)
        start += out.shape[0]


def stack_rows_body(at, *refs):
    out = refs[-1]
    start = 0
    for ref in refs[:-1]:
        out[start : start + ref.shape[0], :] = ref[...]
        start += ref.shape[0]


def chunk_number(at, mask, steps):
    number = 0
    for step in steps:
        number = number * 2 + ((at[3] ^ mask) // step) % 2
    return number


def chunks_of(at, steps, refs):
    masks = [0]
    found = [(0, refs[0], 0)]
    for step, ref in zip(reversed(steps), refs[1:]):
        found += [(mask ^ step, ref, i) for i, mask in enumerate(masks)]
        masks = masks + [mask ^ step for mask in masks]
    size = refs[0].shape[0]
    for mask, ref, i in found:
        yield chunk_number(at, mask, steps), ref[i * size : (i + 1) * size, :].astype(F32)


def out_final_body(steps, at, *refs):
    for place, piece in chunks_of(at, steps, refs[:-1]):
        refs[-1][rows_at(place, piece.shape[0]), :] = piece


def fc_final_body(parts, steps, at, *refs):
    out = refs[-1]
    hidden = out.shape[1] // parts
    for place, piece in chunks_of(at, steps, refs[:-1]):
        size = piece.shape[0] // parts
        for j in range(parts):
            lanes = pl.ds(pl.multiple_of((at[2] ^ j) * hidden, 128), hidden)
            out[rows_at(place, size), lanes] = piece[j * size : (j + 1) * size]


class Values:
    pass


def shards(
    parts,
    ways,
    tokens,
    first_gain,
    first_bias,
    attn_weight,
    query_bias,
    value_bias,
    proj_weight,
    proj_bias,
    second_gain,
    second_bias,
    fc_weight,
    fc_bias,
    out_weight,
    out_bias,
    cotangent,
):
    rows, features = tokens.shape[1], tokens.shape[2]
    width = features // parts
    count = parts
    blocks = ways // count
    hidden = fc_weight.shape[1] // parts
    columns = 256 + 2 * width
    all_rows, half_rows = parts * rows, parts * rows // 2
    f = lax.axis_index("fsdp").astype(jnp.int32)
    c = lax.axis_index("ctx").astype(jnp.int32)
    at = jnp.stack([c // blocks, c % blocks, f, c])
    halved = ways == 8
    chunks, size = 4, width // 8
    packed = size + size // 3
    small_blocks = blocks * count * rows <= 1024
    last = []
    v = Values()

    def run(body, outs, *args, mib=16, scratch=()):
        task = v.task
        held = [] if task in v.free else last
        hooked = jax.tree.leaves(v.hooks[task]()) if task in v.hooks else []
        made = call(
            body,
            task.__name__,
            outs,
            at,
            *args,
            scratch=scratch,
            after=[*held, *hooked],
            us=v.costs.get(task, 1.0),
            mib=mib,
        )
        if task not in v.free:
            last[:] = [made[-1]]
        return made

    def over_fsdp(value, k):
        return lax.ppermute(value, "fsdp", [(i, i ^ k) for i in range(parts)])

    def over_ctx(value, k):
        return lax.ppermute(value, "ctx", [(i, i ^ k) for i in range(ways)])

    def spread(value):
        across = over_fsdp(value, 2)
        return [value, over_fsdp(value, 1), across, over_fsdp(across, 1)]

    def turn_fsdp(pieces):
        return [pieces[0]] + [over_fsdp(pieces[k], k) for k in range(1, parts)]

    def turn_ctx(pieces):
        return [pieces[0]] + [over_ctx(pieces[k], k * blocks) for k in range(1, count)]

    def halve(kept, arrived, step):
        half, lanes = kept.shape[0] // 2, kept.shape[1]
        outs = [shape((half, lanes), F32), shape((half, lanes), BF)]
        return run(partial(halve_body, step), outs, kept, arrived, scratch=[pltpu.VMEM((2 * half, lanes), F32)])

    def last_sum(kept, arrived, cuts):
        return run(last_sum_body, [shape((cut, kept.shape[1]), BF) for cut in cuts], kept, arrived)

    def stacked(pieces):
        total = sum(piece.shape[0] for piece in pieces)
        return run(stack_rows_body, [shape((total, pieces[0].shape[1]), BF)], *pieces)[0]

    v.sums = jnp.zeros((8, features), F32)

    def attn_columns():
        outs = [shape((width, columns), BF)] * parts
        v.attn_pieces = turn_fsdp(run(partial(attn_columns_body, parts), outs, attn_weight))
        v.attn_core = [v.attn_pieces[1]]

    def token_message():
        args = (tokens[0], first_gain, first_bias, second_gain, second_bias, proj_bias, out_bias)
        v.tokens = spread(run(token_message_body, [shape((rows + 8, features), BF)], *args)[0])

    def fc_columns():
        outs = [shape((width, hidden), BF)] * parts
        v.fc_columns = turn_fsdp(run(fc_columns_body, outs, fc_weight))
        v.fc_core = [v.fc_columns[1]]

    def mixed():
        made = run(
            partial(mixed_body, parts, count),
            [shape((all_rows, features), BF), shape((features, columns), BF), shape((8, features), F32)]
            + [shape((5 * rows // 2, 256), BF)] * count
            + [shape((rows, 384), BF)] * count,
            query_bias,
            value_bias,
            *v.tokens,
            *v.attn_pieces,
            scratch=[pltpu.VMEM((all_rows, columns), BF)],
        )
        v.attn_matrix, v.vectors = made[1:3]
        v.pairs = turn_ctx(made[3 + count :])
        v.queries = turn_ctx(made[3 : 3 + count])

    def stack_pairs():
        joined = stacked(v.pairs)
        v.partners = [over_ctx(joined, j) for j in range(1, blocks)]

    def join_fc():
        v.fc_matrix = run(join_body, [shape((features, hidden), BF)], *v.fc_columns)[0]

    def stack_extra():
        v.extra = spread(stacked([cotangent[0], proj_weight]))
        v.extra_across = [v.extra[2]]

    def attend():
        kept = run(
            partial(attend_body, count, blocks, rows),
            [shape((rows + rows // 2, 128), BF)] * count
            + [
                shape((count * rows, 256), F32),
                shape((count * rows, 128), F32),
                shape((count * rows, 256), BF),
                shape((count * blocks * rows, 384), BF),
            ],
            *v.queries,
            *v.pairs,
            *v.partners,
        )
        v.att_pieces, v.state = turn_ctx(kept[:count]), kept[count:]

    def plain_front():
        kept = plain_attend(count, blocks, rows, at, v.queries, v.pairs, v.partners)
        v.att_pieces, v.state = turn_ctx(kept[:count]), kept[count:]

    def normed_stack():
        outs = [shape((count * rows, features // 2), BF)]
        own = run(partial(normed_stack_body, rows), outs, *v.queries)[0]
        v.normed_across = [over_ctx(own, j) for j in range(1, blocks)]
        v.normed_sides = [own] + v.normed_across

    def middle():
        attended_all = lax.all_gather(jnp.concatenate(v.att_pieces, 0), "fsdp")
        gn_mine, gn_other, v.mid_mine, v.normed_two, v.active, v.g_hidden, v.attended = run(
            partial(middle_body, parts, rows),
            [shape((half_rows, features), F32)] * 3
            + [shape((all_rows, features), BF), shape((all_rows, hidden), BF), shape((all_rows, hidden), BF)]
            + [shape((all_rows, 256), BF)],
            attended_all,
            v.vectors,
            v.fc_matrix,
            fc_bias,
            out_weight,
            *v.tokens,
            *v.extra,
            scratch=[pltpu.VMEM((all_rows, parts * 256), BF), pltpu.VMEM((parts * 256, features), BF)],
            mib=24,
        )
        v.chip_sum = gn_mine + over_fsdp(gn_other, 1)
        v.chip_low = v.chip_sum.astype(BF)
        v.arrived = over_fsdp(v.chip_low, 2)


    def place():
        sides = v.normed_sides + [over_fsdp(side, 1) for side in v.normed_sides]
        v.every, v.own_rows = run(
            partial(normed_place_body, count, blocks, rows),
            [shape((count * blocks * rows, features), BF), shape((count * rows, features), BF)],
            *sides,
        )

    def fc_weights():
        v.fc_kept, away, v.sums = run(
            partial(fc_weights_body, parts, chunks, FC_STEPS[0]),
            [shape((features // 2, hidden), F32), shape((features // 2, hidden), BF), shape((8, features), F32)],
            v.normed_two,
            v.g_hidden,
            v.sums,
            scratch=[pltpu.VMEM((features, hidden), F32)],
        )
        v.fc_in = over_ctx(away, FC_STEPS[0])

    def out_weights():
        v.out_kept, away, v.sums = run(
            partial(out_weights_body, rows, OUT_STEPS[0]),
            [shape((hidden // 2, features), F32), shape((hidden // 2, features), BF), shape((8, features), F32)],
            v.active,
            v.sums,
            *v.extra,
            scratch=[pltpu.VMEM((hidden, features), F32)],
        )
        v.out_in = over_ctx(away, OUT_STEPS[0])

    def both_weights():
        v.out_grad, v.fc_grad, v.sums = run(
            partial(plain_weights_body, rows),
            [shape((hidden, features), BF), shape((features, hidden), BF), shape((8, features), F32)],
            v.active,
            v.normed_two,
            v.g_hidden,
            v.sums,
            *v.extra,
        )

    def second_norm():
        v.g_branch, v.own_middle, v.sums = run(
            partial(second_norm_body, rows),
            [shape((half_rows, features), BF), shape((rows, features), F32), shape((8, features), F32)],
            v.chip_sum,
            v.arrived,
            v.mid_mine,
            v.extra[0],
            v.extra[2],
            v.vectors,
            v.sums,
        )

    def attended_grad():
        grads = run(
            partial(attended_grad_body, parts, rows),
            [shape((rows, 256), BF)] * parts + [shape((all_rows, features), BF)],
            v.g_branch,
            over_fsdp(v.g_branch, 1),
            proj_weight,
            scratch=[pltpu.VMEM((all_rows, 256), BF)],
        )
        v.g_pieces, v.g_branch_all = turn_ctx(grads[:parts]), grads[parts]

    def proj_weights():
        v.proj, v.sums = run(
            partial(proj_grad_body, rows),
            [shape((width, features), F32), shape((8, features), F32)],
            v.attended,
            v.g_branch_all,
            v.sums,
        )

    def fc_one():
        v.fc_kept, away = halve(v.fc_kept, v.fc_in, FC_STEPS[1])
        v.fc_in = over_ctx(away, FC_STEPS[1])

    def fc_two():
        v.fc_kept, away = halve(v.fc_kept, v.fc_in, FC_STEPS[2])
        v.fc_in = over_ctx(away, FC_STEPS[2])

    def fc_sum():
        v.fc_parts = turn_fsdp(last_sum(v.fc_kept, v.fc_in, [size] * parts))

    def fc_turned():
        part = stacked(v.fc_parts)
        v.fc_pieces = [part, over_ctx(part, FC_STEPS[2])]

    def fc_double():
        v.fc_pieces.append(over_ctx(stacked(v.fc_pieces), FC_STEPS[1]))

    def fc_fourfold():
        v.fc_pieces.append(over_ctx(stacked(v.fc_pieces), FC_STEPS[0]))

    def fc_final():
        outs = [shape((width, parts * hidden), F32)]
        v.fc_weight_grad = run(partial(fc_final_body, parts, FC_STEPS), outs, *v.fc_pieces)[0]

    def out_one():
        v.out_kept, away = halve(v.out_kept, v.out_in, OUT_STEPS[1])
        v.out_in = over_ctx(away, OUT_STEPS[1])

    def out_two():
        v.out_kept, away = halve(v.out_kept, v.out_in, OUT_STEPS[2])
        v.out_in = over_ctx(away, OUT_STEPS[2])

    def out_sum():
        part = last_sum(v.out_kept, v.out_in, [hidden // 8])[0]
        v.out_pieces = [part, over_ctx(part, OUT_STEPS[2])]

    def out_double():
        v.out_pieces.append(over_ctx(stacked(v.out_pieces), OUT_STEPS[1]))

    def out_fourfold():
        v.out_pieces.append(over_ctx(stacked(v.out_pieces), OUT_STEPS[0]))

    def out_final():
        outs = [shape((hidden, features), F32)]
        v.out_weight_grad = run(partial(out_final_body, OUT_STEPS), outs, *v.out_pieces)[0]

    def attend_back():
        v.own, away, v.dq, v.dkv = run(
            partial(attend_back_body, count, blocks, rows),
            [
                shape((count * rows, 384), F32),
                shape(((blocks - 1) * count * rows, 384), BF),
                shape((count * rows, 256), BF),
                shape((count * blocks * rows, 384), BF),
            ],
            *v.g_pieces,
            v.state[2],
            v.state[3],
            *v.state[:2],
            scratch=[pltpu.VMEM((count * rows, 256), BF), pltpu.VMEM((count * blocks * rows, 384), F32)],
        )
        v.from_partners = [over_ctx(away, 1)]

    def plain_back():
        v.own, away, v.dq, v.dkv = plain_attend_back(
            count, blocks, rows, at, v.g_pieces, v.state[2], v.state[3], *v.state[:2]
        )
        stack = count * rows
        v.from_partners = [over_ctx(away[(j - 1) * stack : j * stack], j) for j in range(1, blocks)]

    def attn_weights():
        outs = [shape((count * (parts * size + packed), columns), kind) for kind in (F32, BF)]
        v.attn_kept, away, v.sums_attn = run(
            partial(attn_halves_body, parts, count),
            outs + [shape((8, columns), F32)],
            v.own_rows,
            v.every,
            v.dq,
            v.dkv,
            v.proj,
            scratch=[pltpu.VMEM((features, columns), F32)],
        )
        v.attn_in = over_ctx(away, 1)

    def attn_pair():
        outs = [shape((parts * size + packed, columns), kind) for kind in (F32, BF, BF, BF)]
        v.attn_sent = turn_ctx(run(attn_pair_body, outs, v.attn_kept, v.attn_in))

    def attn_fold():
        outs = [shape((size, columns), BF)] * parts + [shape((packed, columns), BF)]
        *attn_parts, v.proj = run(partial(attn_fold_body, count), outs, *v.attn_sent)
        v.attn_parts = turn_fsdp(attn_parts)

    def attn_turned():
        v.attn_pieces = turn_ctx([stacked([*v.attn_parts, v.proj])] * count)

    def attn_fourfold():
        v.attn_pieces.append(over_ctx(stacked(v.attn_pieces), 1))

    def attn_final():
        outs = [shape((width, 3 * features), F32), shape((width, features), F32)]
        v.attn_weight_grad, v.proj_weight_grad = run(
            partial(attn_place_body, parts, count),
            outs,
            *v.attn_pieces,
            scratch=[pltpu.VMEM((parts, width, columns), F32)],
        )

    def plain_attn_weights():
        attn_grads, v.sums_attn = run(
            partial(attn_weights_body, parts, ways),
            [shape((parts * ways, width // ways, columns), BF), shape((8, columns), F32)],
            v.own_rows,
            v.every,
            v.dq,
            v.dkv,
        )
        attn_in = lax.all_to_all(attn_grads, ("ctx", "fsdp"), split_axis=0, concat_axis=0, tiled=True)
        outs = [shape((ways, parts, width // ways, columns), BF)]
        attn_sum = run(partial(attn_sum_body, parts, ways), outs, attn_in)[0]
        attn_all = lax.all_to_all(attn_sum, "ctx", split_axis=0, concat_axis=0, tiled=True)
        outs = [shape((width, 3 * features), F32)]
        v.attn_weight_grad = run(partial(attn_final_body, parts, ways), outs, attn_all)[0]

    def merge():
        outs = [shape((count * rows, columns), BF)]
        if MERGE_PERMUTES and halved:
            outs = [shape((rows, columns), BF)] * count
            pieces = run(partial(merge_pieces_body, rows), outs, v.dq, v.own, *v.from_partners)
            v.g_mixed = turn_ctx(pieces)
            return
        made = run(merge_body, outs, v.dq, v.own, *v.from_partners)[0]
        groups = [[i * blocks + j for i in range(count)] for j in range(blocks)]
        v.g_mixed = lax.all_to_all(made, "ctx", split_axis=0, concat_axis=0, tiled=True, axis_index_groups=groups)

    def out_partial():
        outs = [shape((half_rows, features), F32)] * 2
        mine, other = run(partial(out_partial_body, rows), outs, v.active, out_weight)
        core = over_fsdp(other, 1)
        across = over_fsdp((mine[rows:] + core[rows:]).astype(BF), 2)
        output = mine[:rows] + core[:rows] + across.astype(F32) + v.vectors[5:6]
        v.block_out = (v.mid_mine[:rows] + RESIDUAL * output).astype(BF)

    def first_grad():
        mine, other = run(
            partial(first_grad_body, parts, rows),
            [shape((half_rows, features), F32)] * 2,
            v.attn_matrix,
            *(v.g_mixed if MERGE_PERMUTES and halved else [v.g_mixed]),
            scratch=[pltpu.VMEM((all_rows, columns), BF)],
        )
        arrived = over_fsdp(other, 1)
        v.first_own = (mine, arrived)
        v.first_in = over_fsdp((mine[rows:] + arrived[rows:]).astype(BF), 2)

    def first_norm():
        v.input_grad, shares = run(
            partial(first_norm_body, rows),
            [shape((rows, features), BF), shape((parts * ways, 8, 512), F32)],
            *v.first_own,
            v.first_in,
            tokens[0],
            v.own_middle,
            v.vectors,
            v.sums,
            v.sums_attn,
        )
        v.shares = lax.all_to_all(shares, ("ctx", "fsdp"), split_axis=0, concat_axis=0, tiled=True)

    def vector_final():
        outs = [shape((width,), F32)] * 8 + [shape((hidden,), F32)]
        v.vector_grads = run(partial(vector_final_body, ways, parts), outs, v.shares)

    def gather_rest():
        def over_all(value):
            part = lax.psum_scatter(value, "ctx", scatter_dimension=1, tiled=True)
            return lax.all_gather(part, "ctx", axis=1, tiled=True)

        v.out_weight_grad = over_all(v.out_grad).astype(F32)
        v.proj_weight_grad = over_all(v.proj.astype(BF)).astype(F32)
        fc_grad = over_all(v.fc_grad).reshape(parts, width, hidden)
        fc_grad = lax.all_to_all(fc_grad, "fsdp", split_axis=0, concat_axis=0)
        v.fc_weight_grad = fc_grad.transpose(1, 0, 2).reshape(width, parts * hidden).astype(F32)

    v.free = {
        attn_pair, fc_final, fc_fourfold, fc_weights, out_double, out_partial, vector_final,
    }
    v.hooks = {
        attend: lambda: [v.extra_across],
        fc_columns: lambda: [v.attn_core],
        fc_weights: lambda: [v.chip_low],
        middle: lambda: [v.normed_across],
        mixed: lambda: [v.fc_core],
        out_weights: lambda: [v.chip_low],
        place: lambda: [v.chip_low],
    }
    v.costs = {merge: 1.0, out_sum: 1000000.0}
    front = (attn_columns, token_message, fc_columns, mixed, stack_pairs, join_fc, stack_extra)
    if halved:
        order = (
            attn_columns, token_message, fc_columns, mixed, stack_pairs, join_fc, stack_extra, attend, normed_stack,
            middle, place, fc_weights, out_weights, second_norm, attended_grad, fc_one, proj_weights, out_one,
            attend_back, attn_weights, fc_two, out_two, fc_sum, merge, first_grad, attn_pair, fc_turned, out_sum,
            attn_fold, out_double, first_norm, fc_double, fc_fourfold, out_partial, out_fourfold, attn_turned,
            out_final, attn_fourfold, fc_final, vector_final, attn_final,
        )
    else:
        order = (*front, plain_front, normed_stack, middle, place, both_weights, second_norm, attended_grad)
        order += (proj_weights, plain_back, plain_attn_weights, merge, first_grad, out_partial, first_norm)
        order += (vector_final, gather_rest)
    for task in order:
        v.task = task
        task()
    first_gain_grad, first_bias_grad, second_gain_grad, second_bias_grad = v.vector_grads[:4]
    proj_bias_grad, out_bias_grad, query_bias_grad, value_bias_grad, fc_bias_grad = v.vector_grads[4:]
    return (
        v.block_out[None],
        v.input_grad[None],
        first_gain_grad,
        first_bias_grad,
        v.attn_weight_grad,
        query_bias_grad,
        value_bias_grad,
        v.proj_weight_grad,
        proj_bias_grad,
        second_gain_grad,
        second_bias_grad,
        v.fc_weight_grad,
        fc_bias_grad,
        v.out_weight_grad,
        out_bias_grad,
    )


def solution(mesh):
    rows, row, matrix = P("fsdp", "ctx", None), P("fsdp"), P("fsdp", None)
    return jax.shard_map(
        partial(shards, mesh.shape["fsdp"], mesh.shape["ctx"]),
        mesh=mesh,
        in_specs=(
            rows, row, row, matrix, row, row, matrix, row, row, row, matrix, row, matrix, row, rows,
        ),
        out_specs=(
            rows, rows, row, row, matrix, row, row, matrix, row, row, row, matrix, row, matrix, row,
        ),
        check_vma=False,
    )
```

time: 279 us -> 253 us (0.907)
  waiting for transfers between devices: 128 us -> 92.7 us
  blocking collectives: 8.26 us -> 26.3 us
  starting transfers between devices: 72.3 us -> 60.9 us
  local copies, waits for them, and re-layouts: 8.46 us -> 11.4 us
  Pallas kernels: 59 us -> 56.1 us
    ppermute x42 -> x35, waiting for transfers between devices: 91.6 us -> 62.9 us  [over_ctx(): return lax.ppermute(value, 'ctx', [(i, i ^ k) for i in range(ways)])]
    all_to_all x0 -> x1, blocking collectives: none -> 17.5 us  [merge(): lax.all_to_all(made, 'ctx', split_axis=0, concat_axis=0, tiled=True, axis...]
    ppermute x42 -> x35, starting transfers between devices: 54.7 us -> 40.6 us  [over_ctx(): return lax.ppermute(value, 'ctx', [(i, i ^ k) for i in range(ways)])]
    ppermute x27, waiting for transfers between devices: 36.4 us -> 29.8 us  [over_fsdp(): return lax.ppermute(value, 'fsdp', [(i, i ^ k) for i in range(parts)])]
    all_to_all x0 -> x1, starting transfers between devices: none -> 3.56 us  [first_norm(): lax.all_to_all(shares, ('ctx', 'fsdp'), split_axis=0, concat_axis=0, tile...]
    pallas_call x38 -> x41, Pallas kernels: 59 us -> 56.1 us  [call(): pl.pallas_call(run, name=name, out_shape=outs, in_specs=[smem] + [vmem] *...]
    unnamed x50 -> x60, local copies, waits for them, and re-layouts: 8.4 us -> 10.7 us
  transfers between devices with their start and end apart: 69 -> 63, of which waited for: 35 -> 30; matrix products, arithmetic and copies ran while one was open for 0% -> 1% of each run, Pallas kernels for 13% -> 17%
where the time goes in v4:
time: 253 us; the launch traced here: 252 us
  waiting for transfers between devices  92.7 us (37%)
  starting transfers between devices  60.9 us (24%)
  Pallas kernels  56.1 us (22%)
  blocking collectives  26.3 us (10%)
  local copies, waits for them, and re-layouts  11.4 us (5%)
  other arithmetic  3.07 us (1%)
    ppermute x35, waiting for transfers between devices, over_ctx(): return lax.ppermute(value, 'ctx', [(i, i ^ k) for i in range(ways)])  62.9 us
    pallas_call x41, Pallas kernels, call(): pl.pallas_call(run, name=name, out_shape=outs, in_specs=[smem] + [vmem] *...  56.1 us
    ppermute x35, starting transfers between devices, over_ctx(): return lax.ppermute(value, 'ctx', [(i, i ^ k) for i in range(ways)])  40.6 us
    ppermute x27, waiting for transfers between devices, over_fsdp(): return lax.ppermute(value, 'fsdp', [(i, i ^ k) for i in range(parts)])  29.8 us
    all_to_all x1, blocking collectives, merge(): lax.all_to_all(made, 'ctx', split_axis=0, concat_axis=0, tiled=True, axis...  17.5 us
    ppermute x27, starting transfers between devices, over_fsdp(): return lax.ppermute(value, 'fsdp', [(i, i ^ k) for i in range(parts)])  16.8 us
    unnamed x60, local copies, waits for them, and re-layouts  10.7 us
    all_gather x1, blocking collectives, middle(): attended_all = lax.all_gather(jnp.concatenate(v.att_pieces, 0), 'fsdp')  8.8 us
  transfers between devices with their start and end apart: 63, of which 30 were waited for; matrix products, arithmetic and copies ran while one was open for 1% of the time, Pallas kernels for 17%

profile of v4, /device:TPU:0, one launch (start us, length us, event | category | flops | bytes accessed | tf_op | source)
XLA Modules:
  0.0 251.8 jit_solution(16794228348554560774)
XLA Ops:
  14.4 5.1 %collective-permute-done.1.refs_5_.refs_8_ = bf16[136,768]{1,0:T(8,128)(2,1)S(1)} collective-permute-done((bf16[136,768]{1,0:T(8,128)(2,1)S(1)}, bf16[136,768]{1,0:T(8,128)(2,1)S(1)}, u32[]{:S(2)}, u32[]{:S(2)}) %collective-permute-start.1) | collective-permute-done | bytes 208928 | tf_op jit(solution)/shard_map/ppermute | solution.py:796
  30.8 6.9 %collective-permute-done.11.refs_3_.refs_7_ = bf16[128,384]{1,0:T(8,128)(2,1)S(1)} collective-permute-done((bf16[128,384]{1,0:T(8,128)(2,1)S(1)}, bf16[128,384]{1,0:T(8,128)(2,1)S(1)}, u32[]{:S(2)}, u32[]{:S(2)}) %collective-permute-start.11) | collective-permute-done | bytes 98336 | tf_op jit(solution)/shard_map/ppermute | solution.py:799
  47.5 3.1 %collective-permute-done.7.refs_2_ = bf16[320,256]{1,0:T(8,128)(2,1)S(1)} collective-permute-done((bf16[320,256]{1,0:T(8,128)(2,1)S(1)}, bf16[320,256]{1,0:T(8,128)(2,1)S(1)}, u32[]{:S(2)}, u32[]{:S(2)}) %collective-permute-start.7) | collective-permute-done | bytes 163872 | tf_op jit(solution)/shard_map/ppermute | solution.py:799
  53.2 6.6 %collective-permute-done.8.refs_3_ = bf16[320,256]{1,0:T(8,128)(2,1)S(1)} collective-permute-done((bf16[320,256]{1,0:T(8,128)(2,1)S(1)}, bf16[320,256]{1,0:T(8,128)(2,1)S(1)}, u32[]{:S(2)}, u32[]{:S(2)}) %collective-permute-start.8) | collective-permute-done | bytes 163872 | tf_op jit(solution)/shard_map/ppermute | solution.py:799
  59.7 5.3 %attend.1 = (bf16[192,128]{1,0:T(8,128)(2,1)S(1)}, bf16[192,128]{1,0:T(8,128)(2,1)S(1)}, bf16[192,128]{1,0:T(8,128)(2,1)S(1)}, bf16[192,128]{1,0:T(8,128)(2,1)S(...) custom-call(s32[4]{0:T(128)S(1)} %pad_add_fusion.refs_0_, ...), custom_call_target="tpu_custom_call" | custom-call | flops 1000 | bytes 1000 | tf_op jit(solution)/shard_map/attend/pallas_call | solution.py:35
  74.5 8.8 %all-gather = bf16[3072,128]{1,0:T(8,128)(2,1)S(1)} all-gather(bf16[768,128]{1,0:T(8,128)(2,1)S(1)} %pad_maximum_fusion), channel_id=2, replica_groups=mesh['ctx'=8,'fsdp'=4] {'fsdp'}, dimensions={0}, use_global_device_ids=true | all-gather | bytes 983040 | tf_op jit(solution)/shard_map/all_gather | solution.py:893
  83.4 4.9 %middle.1 = (f32[256,768]{1,0:T(8,128)S(1)}, f32[256,768]{1,0:T(8,128)S(1)}, f32[256,768]{1,0:T(8,128)S(1)}, bf16[512,768]{1,0:T(8,128)(2,1)S(1)}, bf16[512,768]...) custom-call(s32[4]{0:T(128)S(1)} %pad_add_fusion.refs_0_, ...), custom_call_target="tpu_custom_call" | custom-call | flops 1000 | bytes 1000 | tf_op jit(solution)/shard_map/middle/pallas_call | solution.py:35
  96.6 5.6 %collective-permute-done.26.refs_2_ = bf16[256,768]{1,0:T(8,128)(2,1)S(1)} collective-permute-done((bf16[256,768]{1,0:T(8,128)(2,1)S(1)}, bf16[256,768]{1,0:T(8,128)(2,1)S(1)}, u32[]{:S(2)}, u32[]{:S(2)}) %collective-permute-start.26) | collective-permute-done | bytes 393248 | tf_op jit(solution)/shard_map/ppermute | solution.py:796
  114.9 5.5 %attend_back.1 = (f32[512,384]{1,0:T(8,128)S(1)}, bf16[512,384]{1,0:T(8,128)(2,1)S(1)}, bf16[512,256]{1,0:T(8,128)(2,1)S(1)}, bf16[1024,384]{1,0:T(8,128)(2,1)S(1)}) custom-call(s32[4]{0:T(128)S(1)} %pad_add_fusion.refs_0_, bf16[128,256]{1,0:T(8,128)(2,1)S(1)} %get-tuple-element.148.refs_1_, bf16[128,256]{1,0:T(8,128)(2,1)S(1)} %collective-permute-done.30.refs_2_, ...), custom_call_target="tpu_custom_call" | custom-call | flops 1000 | bytes 1000 | tf_op jit(solution)/shard_map/attend_back/pallas_call | solution.py:35
  126.1 4.3 %collective-permute-done.38.refs_2_ = bf16[192,768]{1,0:T(8,128)(2,1)S(1)} collective-permute-done((bf16[192,768]{1,0:T(8,128)(2,1)S(1)}, bf16[192,768]{1,0:T(8,128)(2,1)S(1)}, u32[]{:S(2)}, u32[]{:S(2)}) %collective-permute-start.38) | collective-permute-done | bytes 294944 | tf_op jit(solution)/shard_map/ppermute | solution.py:799
  134.9 17.5 %all_to_all.16 = bf16[4,128,640]{2,1,0:T(8,128)(2,1)S(1)} all-to-all(bf16[4,128,640]{2,1,0:T(8,128)(2,1)S(1)} %bitcast.12), channel_id=1, replica_groups={{0,8,16,24},{4,12,20,28},{1,9,17,25},{5,13,21,29},{2,10,18,26},{6,14,22..., dimensions={0} | all-to-all | bytes 1310720 | tf_op jit(solution)/shard_map/all_to_all | solution.py:1122
  160.8 4.2 %collective-permute-done.45.refs_2_ = bf16[96,768]{1,0:T(8,128)(2,1)S(1)} collective-permute-done((bf16[96,768]{1,0:T(8,128)(2,1)S(1)}, bf16[96,768]{1,0:T(8,128)(2,1)S(1)}, u32[]{:S(2)}, u32[]{:S(2)}) %collective-permute-start.45) | collective-permute-done | bytes 147488 | tf_op jit(solution)/shard_map/ppermute | solution.py:799
  165.7 5.3 %collective-permute-done.41.refs_2_ = bf16[512,640]{1,0:T(8,128)(2,1)S(1)} collective-permute-done((bf16[512,640]{1,0:T(8,128)(2,1)S(1)}, bf16[512,640]{1,0:T(8,128)(2,1)S(1)}, u32[]{:S(2)}, u32[]{:S(2)}) %collective-permute-start.41) | collective-permute-done | bytes 655392 | tf_op jit(solution)/shard_map/ppermute | solution.py:799
  179.2 2.8 %collective-permute-done.42.refs_2_ = bf16[128,640]{1,0:T(8,128)(2,1)S(1)} collective-permute-done((bf16[128,640]{1,0:T(8,128)(2,1)S(1)}, bf16[128,640]{1,0:T(8,128)(2,1)S(1)}, u32[]{:S(2)}, u32[]{:S(2)}) %collective-permute-start.42) | collective-permute-done | bytes 163872 | tf_op jit(solution)/shard_map/ppermute | solution.py:799
  183.8 8.0 %collective-permute-done.44.refs_4_ = bf16[128,640]{1,0:T(8,128)(2,1)S(1)} collective-permute-done((bf16[128,640]{1,0:T(8,128)(2,1)S(1)}, bf16[128,640]{1,0:T(8,128)(2,1)S(1)}, u32[]{:S(2)}, u32[]{:S(2)}) %collective-permute-start.44) | collective-permute-done | bytes 163872 | tf_op jit(solution)/shard_map/ppermute | solution.py:799
  194.3 2.8 %collective-permute-done.54.refs_2_ = bf16[96,768]{1,0:T(8,128)(2,1)S(1)} collective-permute-done((bf16[96,768]{1,0:T(8,128)(2,1)S(1)}, bf16[96,768]{1,0:T(8,128)(2,1)S(1)}, u32[]{:S(2)}, u32[]{:S(2)}) %collective-permute-start.54) | collective-permute-done | bytes 147488 | tf_op jit(solution)/shard_map/ppermute | solution.py:799
  200.3 3.6 %all-to-all-start.1 = ((f32[32,8,512]{2,1,0:T(8,128)}), f32[32,8,512]{2,1,0:T(8,128)S(1)}, u32[]{:S(2)}, u32[]{:S(2)}) async-start(f32[32,8,512]{2,1,0:T(8,128)} %get-tuple-element.191.refs_3_), calls=%async_computation.1 | async-start | bytes 1048576 | tf_op jit(solution)/shard_map/all_to_all | solution.py:1156
  206.7 3.1 %collective-permute-done.50.refs_3_ = bf16[24,640]{1,0:T(8,128)(2,1)S(1)} collective-permute-done((bf16[24,640]{1,0:T(8,128)(2,1)S(1)}, bf16[24,640]{1,0:T(8,128)(2,1)S(1)}, u32[]{:S(2)}, u32[]{:S(2)}) %collective-permute-start.50) | collective-permute-done | bytes 30752 | tf_op jit(solution)/shard_map/ppermute | solution.py:796
  213.9 4.2 %collective-permute-start.56 = (bf16[128,640]{1,0:T(8,128)(2,1)S(1)}, bf16[128,640]{1,0:T(8,128)(2,1)S(1)}, u32[]{:S(2)}, u32[]{:S(2)}) collective-permute-start(bf16[128,640]{1,0:T(8,128)(2,1)S(1)} %attn_turned.1.refs_5_.refs_1_), channel_id=1, source_target_pairs={{0,16},{4,20},{8,24},{12,28},{16,0},{20,4},{24,8},{28,12},{1,17},{... | collective-permute-start | bytes 491528 | tf_op jit(solution)/shard_map/ppermute | solution.py:799
  218.1 6.8 %collective-permute-done.60.refs_3_ = bf16[192,768]{1,0:T(8,128)(2,1)S(1)} collective-permute-done((bf16[192,768]{1,0:T(8,128)(2,1)S(1)}, bf16[192,768]{1,0:T(8,128)(2,1)S(1)}, u32[]{:S(2)}, u32[]{:S(2)}) %collective-permute-start.60) | collective-permute-done | bytes 294944 | tf_op jit(solution)/shard_map/ppermute | solution.py:799
  228.0 2.7 %out_final.1.refs_5_ = f32[768,768]{1,0:T(8,128)} custom-call(s32[4]{0:T(128)S(1)} %pad_add_fusion.refs_0_, bf16[96,768]{1,0:T(8,128)(2,1)S(1)} %out_sum.1.refs_5_.refs_1_, bf16[96,768]{1,0:T(8,128)(2,1)S(1)} %collective-permute-done.52.refs_2_, bf16[192,768]{1,0:T(8,128)(2,1)S(1)} %collective-permute-done.53.refs_3_, ...), custom_call_target="tpu_custom_call" | custom-call | flops 1000 | bytes 1000 | tf_op jit(solution)/shard_map/out_final/pallas_call | solution.py:35
  230.7 3.1 %collective-permute-done.57.refs_4_ = bf16[128,640]{1,0:T(8,128)(2,1)S(1)} collective-permute-done((bf16[128,640]{1,0:T(8,128)(2,1)S(1)}, bf16[128,640]{1,0:T(8,128)(2,1)S(1)}, u32[]{:S(2)}, u32[]{:S(2)}) %collective-permute-start.57) | collective-permute-done | bytes 163872 | tf_op jit(solution)/shard_map/ppermute | solution.py:799
  239.6 3.7 %collective-permute-done.24 = bf16[128,768]{1,0:T(8,128)(2,1)S(1)} collective-permute-done((bf16[128,768]{1,0:T(8,128)(2,1)S(1)}, bf16[128,768]{1,0:T(8,128)(2,1)S(1)}, u32[]{:S(2)}, u32[]{:S(2)}) %collective-permute-start.24) | collective-permute-done | bytes 196640 | tf_op jit(solution)/shard_map/ppermute | solution.py:796
  248.6 3.2 %attn_final.1 = (f32[192,2304]{1,0:T(8,128)}, f32[192,768]{1,0:T(8,128)}) custom-call(s32[4]{0:T(128)S(1)} %pad_add_fusion.refs_0_, bf16[128,640]{1,0:T(8,128)(2,1)S(1)} %attn_turned.1.refs_5_.refs_1_, bf16[128,640]{1,0:T(8,128)(2,1)S(1)} %copy-done.10, bf16[128,640]{1,0:T(8,128)(2,1)S(1)} %copy-done.12, bf16[128,640]{1,0:T(8,128)(2,1)S(1)} %copy-done.14, ...), custom_call_target="tpu_custom_call" | custom-call | flops 1000 | bytes 1000 | tf_op jit(solution)/shard_map/attn_final/pallas_call | solution.py:35
  (213 shorter events, 123.7 us)
Async XLA Ops:
  3.4 16.1 %collective-permute-start.4 = (bf16[192,640]{1,0:T(8,128)(2,1)S(1)}, bf16[192,640]{1,0:T(8,128)(2,1)S(1)}, u32[]{:S(2)}, u32[]{:S(2)}) collective-permute-start(bf16[192,640]{1,0:T(8,128)(2,1)S(1)} %get-tuple-element.114), channel_id=1, source_target_pairs={{0,2},{1,3},{2,0},{3,1},{4,6},{5,7},{6,4},{7,5},{8,10},{9,11},{10,... | collective-permute-start | bytes 737288 | tf_op jit(solution)/shard_map/ppermute | solution.py:796
  19.4 18.8 %collective-permute-start.14 = (bf16[192,768]{1,0:T(8,128)(2,1)S(1)}, bf16[192,768]{1,0:T(8,128)(2,1)S(1)}, u32[]{:S(2)}, u32[]{:S(2)}) collective-permute-start(bf16[192,768]{1,0:T(8,128)(2,1)S(1)} %get-tuple-element.126), channel_id=1, source_target_pairs={{0,2},{1,3},{2,0},{3,1},{4,6},{5,7},{6,4},{7,5},{8,10},{9,11},{10,... | collective-permute-start | bytes 884744 | tf_op jit(solution)/shard_map/ppermute | solution.py:796
  19.5 18.8 %collective-permute-start.15 = (bf16[192,768]{1,0:T(8,128)(2,1)S(1)}, bf16[192,768]{1,0:T(8,128)(2,1)S(1)}, u32[]{:S(2)}, u32[]{:S(2)}) collective-permute-start(bf16[192,768]{1,0:T(8,128)(2,1)S(1)} %get-tuple-element.115.refs_11_), channel_id=1, source_target_pairs={{0,3},{1,2},{2,1},{3,0},{4,7},{5,6},{6,5},{7,4},{8,11},{9,10},{10,... | collective-permute-start | bytes 884744 | tf_op jit(solution)/shard_map/ppermute | solution.py:796
  39.8 13.3 %collective-permute-start.16 = (bf16[320,768]{1,0:T(8,128)(2,1)S(1)}, bf16[320,768]{1,0:T(8,128)(2,1)S(1)}, u32[]{:S(2)}, u32[]{:S(2)}) collective-permute-start(bf16[320,768]{1,0:T(8,128)(2,1)S(1)} %stack_extra.1.refs_10_.refs_3_.refs_4_), channel_id=1, source_target_pairs={{0,2},{1,3},{2,0},{3,1},{4,6},{5,7},{6,4},{7,5},{8,10},{9,11},{10,... | collective-permute-start | bytes 1474568 | tf_op jit(solution)/shard_map/ppermute | solution.py:796
  41.1 18.6 %collective-permute-start.13 = (bf16[512,384]{1,0:T(8,128)(2,1)S(1)}, bf16[512,384]{1,0:T(8,128)(2,1)S(1)}, u32[]{:S(2)}, u32[]{:S(2)}) collective-permute-start(bf16[512,384]{1,0:T(8,128)(2,1)S(1)} %stack_pairs.1.refs_5_), channel_id=1, source_target_pairs={{0,4},{4,0},{8,12},{12,8},{16,20},{20,16},{24,28},{28,24},{1,5},{5... | collective-permute-start | bytes 1179656 | tf_op jit(solution)/shard_map/ppermute | solution.py:799
  45.0 14.8 %collective-permute-start.8 = (bf16[320,256]{1,0:T(8,128)(2,1)S(1)}, bf16[320,256]{1,0:T(8,128)(2,1)S(1)}, u32[]{:S(2)}, u32[]{:S(2)}) collective-permute-start(bf16[320,256]{1,0:T(8,128)(2,1)S(1)} %get-tuple-element.119), channel_id=1, source_target_pairs={{0,16},{4,20},{8,24},{12,28},{16,0},{20,4},{24,8},{28,12},{1,17},{... | collective-permute-start | bytes 491528 | tf_op jit(solution)/shard_map/ppermute | solution.py:799
  46.0 13.7 %collective-permute-start.9 = (bf16[320,256]{1,0:T(8,128)(2,1)S(1)}, bf16[320,256]{1,0:T(8,128)(2,1)S(1)}, u32[]{:S(2)}, u32[]{:S(2)}) collective-permute-start(bf16[320,256]{1,0:T(8,128)(2,1)S(1)} %get-tuple-element.120), channel_id=1, source_target_pairs={{0,24},{4,28},{8,16},{12,20},{16,8},{20,12},{24,0},{28,4},{1,25},{... | collective-permute-start | bytes 491528 | tf_op jit(solution)/shard_map/ppermute | solution.py:799
  50.5 32.8 %collective-permute-start.20 = (bf16[320,768]{1,0:T(8,128)(2,1)S(1)}, bf16[320,768]{1,0:T(8,128)(2,1)S(1)}, u32[]{:S(2)}, u32[]{:S(2)}) collective-permute-start(bf16[320,768]{1,0:T(8,128)(2,1)S(1)} %stack_extra.1.refs_10_.refs_3_.refs_4_), channel_id=1, source_target_pairs={{0,1},{1,0},{2,3},{3,2},{4,5},{5,4},{6,7},{7,6},{8,9},{9,8},{10,11... | collective-permute-start | bytes 1474568 | tf_op jit(solution)/shard_map/ppermute | solution.py:796
  53.2 30.2 %collective-permute-start.21 = (bf16[320,768]{1,0:T(8,128)(2,1)S(1)}, bf16[320,768]{1,0:T(8,128)(2,1)S(1)}, u32[]{:S(2)}, u32[]{:S(2)}) collective-permute-start(bf16[320,768]{1,0:T(8,128)(2,1)S(1)} %collective-permute-done.16.refs_11_.refs_12_.refs_5_), channel_id=1, source_target_pairs={{0,1},{1,0},{2,3},{3,2},{4,5},{5,4},{6,7},{7,6},{8,9},{9,8},{10,11... | collective-permute-start | bytes 1474568 | tf_op jit(solution)/shard_map/ppermute | solution.py:796
  92.8 17.7 %collective-permute-start.34 = (bf16[384,768]{1,0:T(8,128)(2,1)S(1)}, bf16[384,768]{1,0:T(8,128)(2,1)S(1)}, u32[]{:S(2)}, u32[]{:S(2)}) collective-permute-start(bf16[384,768]{1,0:T(8,128)(2,1)S(1)} %get-tuple-element.159), channel_id=1, source_target_pairs={{0,8},{4,12},{8,0},{12,4},{16,24},{20,28},{24,16},{28,20},{1,9},{5... | collective-permute-start | bytes 1769480 | tf_op jit(solution)/shard_map/ppermute | solution.py:799
  96.0 16.8 %collective-permute-start.33 = (bf16[384,768]{1,0:T(8,128)(2,1)S(1)}, bf16[384,768]{1,0:T(8,128)(2,1)S(1)}, u32[]{:S(2)}, u32[]{:S(2)}) collective-permute-start(bf16[384,768]{1,0:T(8,128)(2,1)S(1)} %get-tuple-element.156), channel_id=1, source_target_pairs={{0,4},{4,0},{8,12},{12,8},{16,20},{20,16},{24,28},{28,24},{1,5},{5... | collective-permute-start | bytes 1769480 | tf_op jit(solution)/shard_map/ppermute | solution.py:799
  120.5 13.7 %collective-permute-start.35 = (bf16[512,384]{1,0:T(8,128)(2,1)S(1)}, bf16[512,384]{1,0:T(8,128)(2,1)S(1)}, u32[]{:S(2)}, u32[]{:S(2)}) collective-permute-start(bf16[512,384]{1,0:T(8,128)(2,1)S(1)} %get-tuple-element.165), channel_id=1, source_target_pairs={{0,4},{4,0},{8,12},{12,8},{16,20},{20,16},{24,28},{28,24},{1,5},{5... | collective-permute-start | bytes 1179656 | tf_op jit(solution)/shard_map/ppermute | solution.py:799
  153.7 21.4 %collective-permute-start.39 = (f32[256,768]{1,0:T(8,128)S(1)}, f32[256,768]{1,0:T(8,128)S(1)}, u32[]{:S(2)}, u32[]{:S(2)}) collective-permute-start(f32[256,768]{1,0:T(8,128)S(1)} %get-tuple-element.177.refs_5_), channel_id=1, source_target_pairs={{0,1},{1,0},{2,3},{3,2},{4,5},{5,4},{6,7},{7,6},{8,9},{9,8},{10,11... | collective-permute-start | bytes 2359304 | tf_op jit(solution)/shard_map/ppermute | solution.py:796
  153.8 17.1 %collective-permute-start.41 = (bf16[512,640]{1,0:T(8,128)(2,1)S(1)}, bf16[512,640]{1,0:T(8,128)(2,1)S(1)}, u32[]{:S(2)}, u32[]{:S(2)}) collective-permute-start(bf16[512,640]{1,0:T(8,128)(2,1)S(1)} %get-tuple-element.180), channel_id=1, source_target_pairs={{0,4},{4,0},{8,12},{12,8},{16,20},{20,16},{24,28},{28,24},{1,5},{5... | collective-permute-start | bytes 1966088 | tf_op jit(solution)/shard_map/ppermute | solution.py:799
  175.0 22.6 %collective-permute-start.53 = (bf16[192,768]{1,0:T(8,128)(2,1)S(1)}, bf16[192,768]{1,0:T(8,128)(2,1)S(1)}, u32[]{:S(2)}, u32[]{:S(2)}) collective-permute-start(bf16[192,768]{1,0:T(8,128)(2,1)S(1)} %out_double.1), channel_id=1, source_target_pairs={{0,8},{4,12},{8,0},{12,4},{16,24},{20,28},{24,16},{28,20},{1,9},{5... | collective-permute-start | bytes 884744 | tf_op jit(solution)/shard_map/ppermute | solution.py:799
  175.2 17.3 %collective-permute-start.40 = (bf16[128,768]{1,0:T(8,128)(2,1)S(1)}, bf16[128,768]{1,0:T(8,128)(2,1)S(1)}, u32[]{:S(2)}, u32[]{:S(2)}) collective-permute-start(bf16[128,768]{1,0:T(8,128)(2,1)S(1)} %fusion), channel_id=1, source_target_pairs={{0,2},{1,3},{2,0},{3,1},{4,6},{5,7},{6,4},{7,5},{8,10},{9,11},{10,... | collective-permute-start | bytes 589832 | tf_op jit(solution)/shard_map/ppermute | solution.py:796
  179.2 57.3 %collective-permute-start.23 = (f32[256,768]{1,0:T(8,128)}, f32[256,768]{1,0:T(8,128)}, u32[]{:S(2)}, u32[]{:S(2)}) collective-permute-start(f32[256,768]{1,0:T(8,128)} %get-tuple-element.136), channel_id=1, source_target_pairs={{0,1},{1,0},{2,3},{3,2},{4,5},{5,4},{6,7},{7,6},{8,9},{9,8},{10,11... | collective-permute-start | bytes 2359304 | tf_op jit(solution)/shard_map/ppermute | solution.py:796
  183.8 13.3 %collective-permute-start.54 = (bf16[96,768]{1,0:T(8,128)(2,1)S(1)}, bf16[96,768]{1,0:T(8,128)(2,1)S(1)}, u32[]{:S(2)}, u32[]{:S(2)}) collective-permute-start(bf16[96,768]{1,0:T(8,128)(2,1)S(1)} %fc_turned.1.refs_3_.refs_1_), channel_id=1, source_target_pairs={{0,16},{4,20},{8,24},{12,28},{16,0},{20,4},{24,8},{28,12},{1,17},{... | collective-permute-start | bytes 442376 | tf_op jit(solution)/shard_map/ppermute | solution.py:799
  198.3 29.6 %collective-permute-start.58 = (bf16[384,768]{1,0:T(8,128)(2,1)S(1)}, bf16[384,768]{1,0:T(8,128)(2,1)}, u32[]{:S(2)}, u32[]{:S(2)}) collective-permute-start(bf16[384,768]{1,0:T(8,128)(2,1)S(1)} %out_fourfold.1.refs_6_), channel_id=1, source_target_pairs={{0,4},{4,0},{8,12},{12,8},{16,20},{20,16},{24,28},{28,24},{1,5},{5... | collective-permute-start | bytes 1769480 | tf_op jit(solution)/shard_map/ppermute | solution.py:799
  199.1 25.7 %collective-permute-start.60 = (bf16[192,768]{1,0:T(8,128)(2,1)S(1)}, bf16[192,768]{1,0:T(8,128)(2,1)S(1)}, u32[]{:S(2)}, u32[]{:S(2)}) collective-permute-start(bf16[192,768]{1,0:T(8,128)(2,1)S(1)} %fc_double.1.refs_4_), channel_id=1, source_target_pairs={{0,4},{4,0},{8,12},{12,8},{16,20},{20,16},{24,28},{28,24},{1,5},{5... | collective-permute-start | bytes 884744 | tf_op jit(solution)/shard_map/ppermute | solution.py:799
  200.3 46.8 %all-to-all-start.1 = ((f32[32,8,512]{2,1,0:T(8,128)}), f32[32,8,512]{2,1,0:T(8,128)S(1)}, u32[]{:S(2)}, u32[]{:S(2)}) async-start(f32[32,8,512]{2,1,0:T(8,128)} %get-tuple-element.191.refs_3_), calls=%async_computation.1 | async-start | bytes 1048576 | tf_op jit(solution)/shard_map/all_to_all | solution.py:1156
  213.6 17.1 %collective-permute-start.55 = (bf16[128,640]{1,0:T(8,128)(2,1)S(1)}, bf16[128,640]{1,0:T(8,128)(2,1)S(1)}, u32[]{:S(2)}, u32[]{:S(2)}) collective-permute-start(bf16[128,640]{1,0:T(8,128)(2,1)S(1)} %attn_turned.1.refs_5_.refs_1_), channel_id=1, source_target_pairs={{0,8},{4,12},{8,0},{12,4},{16,24},{20,28},{24,16},{28,20},{1,9},{5... | collective-permute-start | bytes 491528 | tf_op jit(solution)/shard_map/ppermute | solution.py:799
  213.9 16.9 %collective-permute-start.56 = (bf16[128,640]{1,0:T(8,128)(2,1)S(1)}, bf16[128,640]{1,0:T(8,128)(2,1)S(1)}, u32[]{:S(2)}, u32[]{:S(2)}) collective-permute-start(bf16[128,640]{1,0:T(8,128)(2,1)S(1)} %attn_turned.1.refs_5_.refs_1_), channel_id=1, source_target_pairs={{0,16},{4,20},{8,24},{12,28},{16,0},{20,4},{24,8},{28,12},{1,17},{... | collective-permute-start | bytes 491528 | tf_op jit(solution)/shard_map/ppermute | solution.py:799
  227.9 17.1 %collective-permute-start.61 = (bf16[384,768]{1,0:T(8,128)(2,1)S(1)}, bf16[384,768]{1,0:T(8,128)(2,1)S(1)}, u32[]{:S(2)}, u32[]{:S(2)}) collective-permute-start(bf16[384,768]{1,0:T(8,128)(2,1)S(1)} %fc_fourfold.1), channel_id=1, source_target_pairs={{0,8},{4,12},{8,0},{12,4},{16,24},{20,28},{24,16},{28,20},{1,9},{5... | collective-permute-start | bytes 1769480 | tf_op jit(solution)/shard_map/ppermute | solution.py:799
  (69 other events, 589.9 us)

commit v5 on v4

--- a/solution.py
+++ b/solution.py
@@ -16,7 +16,7 @@
 SCORE = HD ** (-0.5)
 NEVER = -1e30
 OUT_STEPS, FC_STEPS = (1, 2, 4), (2, 1, 4)
-MERGE_PERMUTES = False
+MERGE_PERMUTES = True
 
 
 def shape(dims, kind):
@@ -1171,14 +1171,18 @@
         v.fc_weight_grad = fc_grad.transpose(1, 0, 2).reshape(width, parts * hidden).astype(F32)
 
     v.free = {
-        attn_pair, fc_final, fc_fourfold, fc_weights, out_double, out_partial, vector_final,
+        attn_pair, fc_final, fc_fourfold, fc_one, fc_two, out_double, out_final, out_partial, out_sum, place,
+        vector_final,
     }
     v.hooks = {
         attend: lambda: [v.extra_across],
+        attn_fourfold: lambda: [v.out_pieces],
+        attn_pair: lambda: [v.from_partners],
         fc_columns: lambda: [v.attn_core],
         fc_weights: lambda: [v.chip_low],
         middle: lambda: [v.normed_across],
         mixed: lambda: [v.fc_core],
+        out_partial: lambda: [v.queries],
         out_weights: lambda: [v.chip_low],
         place: lambda: [v.chip_low],
     }
@@ -1187,10 +1191,10 @@
     if halved:
         order = (
             attn_columns, token_message, fc_columns, mixed, stack_pairs, join_fc, stack_extra, attend, normed_stack,
-            middle, place, fc_weights, out_weights, second_norm, attended_grad, fc_one, proj_weights, out_one,
-            attend_back, attn_weights, fc_two, out_two, fc_sum, merge, first_grad, attn_pair, fc_turned, out_sum,
-            attn_fold, out_double, first_norm, fc_double, fc_fourfold, out_partial, out_fourfold, attn_turned,
-            out_final, attn_fourfold, fc_final, vector_final, attn_final,
+            middle, fc_weights, out_weights, second_norm, attended_grad, fc_one, place, proj_weights, out_one,
+            attend_back, attn_weights, fc_two, out_two, fc_sum, merge, fc_turned, first_grad, attn_pair, out_sum,
+            first_norm, out_double, fc_double, attn_fold, out_partial, out_fourfold, attn_turned, attn_fourfold,
+            out_final, fc_fourfold, vector_final, fc_final, attn_final,
         )
     else:
         order = (*front, plain_front, normed_stack, middle, place, both_weights, second_norm, attended_grad)

time: 253 us -> 249 us (0.984)
  blocking collectives: 26.3 us -> 8.8 us
  starting transfers between devices: 60.9 us -> 73.8 us
  waiting for transfers between devices: 92.7 us -> 97 us
  local copies, waits for them, and re-layouts: 11.4 us -> 7.5 us
    all_to_all x1 -> x0, blocking collectives: 17.5 us -> none  [merge(): lax.all_to_all(made, 'ctx', split_axis=0, concat_axis=0, tiled=True, axis...]
    ppermute x35 -> x38, starting transfers between devices: 40.6 us -> 52.9 us  [over_ctx(): return lax.ppermute(value, 'ctx', [(i, i ^ k) for i in range(ways)])]
    unnamed x60 -> x52, local copies, waits for them, and re-layouts: 10.7 us -> 7.48 us
    ppermute x35 -> x38, waiting for transfers between devices: 62.9 us -> 65.4 us  [over_ctx(): return lax.ppermute(value, 'ctx', [(i, i ^ k) for i in range(ways)])]
  transfers between devices with their start and end apart: 63 -> 66, of which waited for: 30 -> 29; matrix products, arithmetic and copies ran while one was open for 1% -> 1% of each run, Pallas kernels for 17% -> 18%
where the time goes in v5:
time: 249 us; the launch traced here: 248 us
  waiting for transfers between devices  97 us (39%)
  starting transfers between devices  73.8 us (30%)
  Pallas kernels  57.1 us (23%)
  blocking collectives  8.8 us (4%)
  local copies, waits for them, and re-layouts  7.5 us (3%)
  other arithmetic  3.06 us (1%)
    ppermute x38, waiting for transfers between devices, over_ctx(): return lax.ppermute(value, 'ctx', [(i, i ^ k) for i in range(ways)])  65.4 us
    pallas_call x41, Pallas kernels, call(): pl.pallas_call(run, name=name, out_shape=outs, in_specs=[smem] + [vmem] *...  57.1 us
    ppermute x38, starting transfers between devices, over_ctx(): return lax.ppermute(value, 'ctx', [(i, i ^ k) for i in range(ways)])  52.9 us
    ppermute x27, waiting for transfers between devices, over_fsdp(): return lax.ppermute(value, 'fsdp', [(i, i ^ k) for i in range(parts)])  31.5 us
    ppermute x27, starting transfers between devices, over_fsdp(): return lax.ppermute(value, 'fsdp', [(i, i ^ k) for i in range(parts)])  16.3 us
    all_gather x1, blocking collectives, middle(): attended_all = lax.all_gather(jnp.concatenate(v.att_pieces, 0), 'fsdp')  8.8 us
    unnamed x52, local copies, waits for them, and re-layouts  7.48 us
  transfers between devices with their start and end apart: 66, of which 29 were waited for; matrix products, arithmetic and copies ran while one was open for 1% of the time, Pallas kernels for 18%

profile of v5, /device:TPU:0, one launch (start us, length us, event | category | flops | bytes accessed | tf_op | source)
XLA Modules:
  0.0 248.4 jit_solution(14987700659750512109)
XLA Ops:
  14.4 5.1 %collective-permute-done.1.refs_5_.refs_8_ = bf16[136,768]{1,0:T(8,128)(2,1)S(1)} collective-permute-done((bf16[136,768]{1,0:T(8,128)(2,1)S(1)}, bf16[136,768]{1,0:T(8,128)(2,1)S(1)}, u32[]{:S(2)}, u32[]{:S(2)}) %collective-permute-start.1) | collective-permute-done | bytes 208928 | tf_op jit(solution)/shard_map/ppermute | solution.py:796
  30.8 6.9 %collective-permute-done.11.refs_3_.refs_7_ = bf16[128,384]{1,0:T(8,128)(2,1)S(1)} collective-permute-done((bf16[128,384]{1,0:T(8,128)(2,1)S(1)}, bf16[128,384]{1,0:T(8,128)(2,1)S(1)}, u32[]{:S(2)}, u32[]{:S(2)}) %collective-permute-start.11) | collective-permute-done | bytes 98336 | tf_op jit(solution)/shard_map/ppermute | solution.py:799
  47.5 3.1 %collective-permute-done.7.refs_2_.refs_4_ = bf16[320,256]{1,0:T(8,128)(2,1)S(1)} collective-permute-done((bf16[320,256]{1,0:T(8,128)(2,1)S(1)}, bf16[320,256]{1,0:T(8,128)(2,1)S(1)}, u32[]{:S(2)}, u32[]{:S(2)}) %collective-permute-start.7) | collective-permute-done | bytes 163872 | tf_op jit(solution)/shard_map/ppermute | solution.py:799
  53.2 6.6 %collective-permute-done.8.refs_3_.refs_5_ = bf16[320,256]{1,0:T(8,128)(2,1)S(1)} collective-permute-done((bf16[320,256]{1,0:T(8,128)(2,1)S(1)}, bf16[320,256]{1,0:T(8,128)(2,1)S(1)}, u32[]{:S(2)}, u32[]{:S(2)}) %collective-permute-start.8) | collective-permute-done | bytes 163872 | tf_op jit(solution)/shard_map/ppermute | solution.py:799
  59.7 5.3 %attend.1 = (bf16[192,128]{1,0:T(8,128)(2,1)S(1)}, bf16[192,128]{1,0:T(8,128)(2,1)S(1)}, bf16[192,128]{1,0:T(8,128)(2,1)S(1)}, bf16[192,128]{1,0:T(8,128)(2,1)S(...) custom-call(s32[4]{0:T(128)S(1)} %pad_add_fusion.refs_0_, ...), custom_call_target="tpu_custom_call" | custom-call | flops 1000 | bytes 1000 | tf_op jit(solution)/shard_map/attend/pallas_call | solution.py:35
  73.1 8.8 %all-gather = bf16[3072,128]{1,0:T(8,128)(2,1)S(1)} all-gather(bf16[768,128]{1,0:T(8,128)(2,1)S(1)} %pad_maximum_fusion), channel_id=2, replica_groups=mesh['ctx'=8,'fsdp'=4] {'fsdp'}, dimensions={0}, use_global_device_ids=true | all-gather | bytes 983040 | tf_op jit(solution)/shard_map/all_gather | solution.py:893
  81.9 4.9 %middle.1 = (f32[256,768]{1,0:T(8,128)S(1)}, f32[256,768]{1,0:T(8,128)S(1)}, f32[256,768]{1,0:T(8,128)S(1)}, bf16[512,768]{1,0:T(8,128)(2,1)S(1)}, bf16[512,768]...) custom-call(s32[4]{0:T(128)S(1)} %pad_add_fusion.refs_0_, ...), custom_call_target="tpu_custom_call" | custom-call | flops 1000 | bytes 1000 | tf_op jit(solution)/shard_map/middle/pallas_call | solution.py:35
  94.8 5.9 %collective-permute-done.26.refs_2_ = bf16[256,768]{1,0:T(8,128)(2,1)S(1)} collective-permute-done((bf16[256,768]{1,0:T(8,128)(2,1)S(1)}, bf16[256,768]{1,0:T(8,128)(2,1)S(1)}, u32[]{:S(2)}, u32[]{:S(2)}) %collective-permute-start.26) | collective-permute-done | bytes 393248 | tf_op jit(solution)/shard_map/ppermute | solution.py:796
  113.9 5.5 %attend_back.1 = (f32[512,384]{1,0:T(8,128)S(1)}, bf16[512,384]{1,0:T(8,128)(2,1)S(1)}, bf16[512,256]{1,0:T(8,128)(2,1)S(1)}, bf16[1024,384]{1,0:T(8,128)(2,1)S(1)}) custom-call(s32[4]{0:T(128)S(1)} %pad_add_fusion.refs_0_, bf16[128,256]{1,0:T(8,128)(2,1)S(1)} %get-tuple-element.151.refs_1_, bf16[128,256]{1,0:T(8,128)(2,1)S(1)} %collective-permute-done.28.refs_2_, ...), custom_call_target="tpu_custom_call" | custom-call | flops 1000 | bytes 1000 | tf_op jit(solution)/shard_map/attend_back/pallas_call | solution.py:35
  126.4 5.3 %collective-permute-done.36.refs_2_ = bf16[192,768]{1,0:T(8,128)(2,1)S(1)} collective-permute-done((bf16[192,768]{1,0:T(8,128)(2,1)S(1)}, bf16[192,768]{1,0:T(8,128)(2,1)S(1)}, u32[]{:S(2)}, u32[]{:S(2)}) %collective-permute-start.36) | collective-permute-done | bytes 294944 | tf_op jit(solution)/shard_map/ppermute | solution.py:799
  143.3 5.2 %collective-permute-done.40.refs_4_ = bf16[128,640]{1,0:T(8,128)(2,1)S(1)} collective-permute-done((bf16[128,640]{1,0:T(8,128)(2,1)S(1)}, bf16[128,640]{1,0:T(8,128)(2,1)S(1)}, u32[]{:S(2)}, u32[]{:S(2)}) %collective-permute-start.40) | collective-permute-done | bytes 163872 | tf_op jit(solution)/shard_map/ppermute | solution.py:799
  149.9 3.4 %collective-permute-start.55 = (bf16[96,768]{1,0:T(8,128)(2,1)S(1)}, bf16[96,768]{1,0:T(8,128)(2,1)S(1)}, u32[]{:S(2)}, u32[]{:S(2)}) collective-permute-start(bf16[96,768]{1,0:T(8,128)(2,1)S(1)} %get-tuple-element.178.refs_3_), channel_id=1, source_target_pairs={{0,16},{4,20},{8,24},{12,28},{16,0},{20,4},{24,8},{28,12},{1,17},{... | collective-permute-start | bytes 442376 | tf_op jit(solution)/shard_map/ppermute | solution.py:799
  153.3 7.6 %collective-permute-done.55.refs_2_ = bf16[96,768]{1,0:T(8,128)(2,1)S(1)} collective-permute-done((bf16[96,768]{1,0:T(8,128)(2,1)S(1)}, bf16[96,768]{1,0:T(8,128)(2,1)S(1)}, u32[]{:S(2)}, u32[]{:S(2)}) %collective-permute-start.55) | collective-permute-done | bytes 147488 | tf_op jit(solution)/shard_map/ppermute | solution.py:799
  162.2 2.9 %collective-permute-start.51 = (bf16[96,768]{1,0:T(8,128)(2,1)S(1)}, bf16[96,768]{1,0:T(8,128)(2,1)S(1)}, u32[]{:S(2)}, u32[]{:S(2)}) collective-permute-start(bf16[96,768]{1,0:T(8,128)(2,1)S(1)} %fc_turned.1.refs_6_.refs_1_), channel_id=1, source_target_pairs={{0,16},{4,20},{8,24},{12,28},{16,0},{20,4},{24,8},{28,12},{1,17},{... | collective-permute-start | bytes 442376 | tf_op jit(solution)/shard_map/ppermute | solution.py:799
  165.1 8.2 %collective-permute-done.56.refs_2_.refs_7_ = bf16[96,768]{1,0:T(8,128)(2,1)S(1)} collective-permute-done((bf16[96,768]{1,0:T(8,128)(2,1)S(1)}, bf16[96,768]{1,0:T(8,128)(2,1)S(1)}, u32[]{:S(2)}, u32[]{:S(2)}) %collective-permute-start.56) | collective-permute-done | bytes 147488 | tf_op jit(solution)/shard_map/ppermute | solution.py:799
  184.4 5.4 %collective-permute-done.48.refs_2_ = bf16[128,640]{1,0:T(8,128)(2,1)S(1)} collective-permute-done((bf16[128,640]{1,0:T(8,128)(2,1)S(1)}, bf16[128,640]{1,0:T(8,128)(2,1)S(1)}, u32[]{:S(2)}, u32[]{:S(2)}) %collective-permute-start.48) | collective-permute-done | bytes 163872 | tf_op jit(solution)/shard_map/ppermute | solution.py:799
  189.8 4.2 %collective-permute-done.50.refs_4_ = bf16[128,640]{1,0:T(8,128)(2,1)S(1)} collective-permute-done((bf16[128,640]{1,0:T(8,128)(2,1)S(1)}, bf16[128,640]{1,0:T(8,128)(2,1)S(1)}, u32[]{:S(2)}, u32[]{:S(2)}) %collective-permute-start.50) | collective-permute-done | bytes 163872 | tf_op jit(solution)/shard_map/ppermute | solution.py:799
  197.3 4.5 %all-to-all-start = ((f32[32,8,512]{2,1,0:T(8,128)}), f32[32,8,512]{2,1,0:T(8,128)S(1)}, u32[]{:S(2)}, u32[]{:S(2)}) async-start(f32[32,8,512]{2,1,0:T(8,128)} %get-tuple-element.191.refs_3_), calls=%async_computation | async-start | bytes 1048576 | tf_op jit(solution)/shard_map/all_to_all | solution.py:1156
  204.6 3.1 %collective-permute-done.53.refs_3_ = bf16[24,640]{1,0:T(8,128)(2,1)S(1)} collective-permute-done((bf16[24,640]{1,0:T(8,128)(2,1)S(1)}, bf16[24,640]{1,0:T(8,128)(2,1)S(1)}, u32[]{:S(2)}, u32[]{:S(2)}) %collective-permute-start.53) | collective-permute-done | bytes 30752 | tf_op jit(solution)/shard_map/ppermute | solution.py:796
  210.2 4.2 %collective-permute-start.59 = (bf16[128,640]{1,0:T(8,128)(2,1)S(1)}, bf16[128,640]{1,0:T(8,128)(2,1)S(1)}, u32[]{:S(2)}, u32[]{:S(2)}) collective-permute-start(bf16[128,640]{1,0:T(8,128)(2,1)S(1)} %attn_turned.1.refs_1_.refs_5_), channel_id=1, source_target_pairs={{0,16},{4,20},{8,24},{12,28},{16,0},{20,4},{24,8},{28,12},{1,17},{... | collective-permute-start | bytes 491528 | tf_op jit(solution)/shard_map/ppermute | solution.py:799
  214.5 7.1 %collective-permute-done.63.refs_3_ = bf16[192,768]{1,0:T(8,128)(2,1)} collective-permute-done((bf16[192,768]{1,0:T(8,128)(2,1)}, bf16[192,768]{1,0:T(8,128)(2,1)}, u32[]{:S(2)}, u32[]{:S(2)}) %collective-permute-start.63) | collective-permute-done | bytes 294944 | tf_op jit(solution)/shard_map/ppermute | solution.py:799
  225.0 3.4 %collective-permute-start.64 = (bf16[384,768]{1,0:T(8,128)(2,1)S(1)}, bf16[384,768]{1,0:T(8,128)(2,1)S(1)}, u32[]{:S(2)}, u32[]{:S(2)}) collective-permute-start(bf16[384,768]{1,0:T(8,128)(2,1)S(1)} %fc_fourfold.1), channel_id=1, source_target_pairs={{0,8},{4,12},{8,0},{12,4},{16,24},{20,28},{24,16},{28,20},{1,9},{5... | collective-permute-start | bytes 1769480 | tf_op jit(solution)/shard_map/ppermute | solution.py:799
  232.7 4.2 %collective-permute-done.24 = bf16[128,768]{1,0:T(8,128)(2,1)S(1)} collective-permute-done((bf16[128,768]{1,0:T(8,128)(2,1)S(1)}, bf16[128,768]{1,0:T(8,128)(2,1)S(1)}, u32[]{:S(2)}, u32[]{:S(2)}) %collective-permute-start.24) | collective-permute-done | bytes 196640 | tf_op jit(solution)/shard_map/ppermute | solution.py:796
  245.2 3.2 %attn_final.1 = (f32[192,2304]{1,0:T(8,128)}, f32[192,768]{1,0:T(8,128)}) custom-call(s32[4]{0:T(128)S(1)} %pad_add_fusion.refs_0_, bf16[128,640]{1,0:T(8,128)(2,1)S(1)} %attn_turned.1.refs_1_.refs_5_, bf16[128,640]{1,0:T(8,128)(2,1)S(1)} %copy-done.11, bf16[128,640]{1,0:T(8,128)(2,1)S(1)} %copy-done.13, bf16[128,640]{1,0:T(8,128)(2,1)S(1)} %copy-done.15, ...), custom_call_target="tpu_custom_call" | custom-call | flops 1000 | bytes 1000 | tf_op jit(solution)/shard_map/attn_final/pallas_call | solution.py:35
  (210 shorter events, 123.5 us)
Async XLA Ops:
  3.4 16.1 %collective-permute-start.4 = (bf16[192,640]{1,0:T(8,128)(2,1)S(1)}, bf16[192,640]{1,0:T(8,128)(2,1)S(1)}, u32[]{:S(2)}, u32[]{:S(2)}) collective-permute-start(bf16[192,640]{1,0:T(8,128)(2,1)S(1)} %get-tuple-element.118), channel_id=1, source_target_pairs={{0,2},{1,3},{2,0},{3,1},{4,6},{5,7},{6,4},{7,5},{8,10},{9,11},{10,... | collective-permute-start | bytes 737288 | tf_op jit(solution)/shard_map/ppermute | solution.py:796
  19.4 18.8 %collective-permute-start.14 = (bf16[192,768]{1,0:T(8,128)(2,1)S(1)}, bf16[192,768]{1,0:T(8,128)(2,1)S(1)}, u32[]{:S(2)}, u32[]{:S(2)}) collective-permute-start(bf16[192,768]{1,0:T(8,128)(2,1)S(1)} %get-tuple-element.130), channel_id=1, source_target_pairs={{0,2},{1,3},{2,0},{3,1},{4,6},{5,7},{6,4},{7,5},{8,10},{9,11},{10,... | collective-permute-start | bytes 884744 | tf_op jit(solution)/shard_map/ppermute | solution.py:796
  19.5 18.8 %collective-permute-start.15 = (bf16[192,768]{1,0:T(8,128)(2,1)S(1)}, bf16[192,768]{1,0:T(8,128)(2,1)S(1)}, u32[]{:S(2)}, u32[]{:S(2)}) collective-permute-start(bf16[192,768]{1,0:T(8,128)(2,1)S(1)} %get-tuple-element.119.refs_11_), channel_id=1, source_target_pairs={{0,3},{1,2},{2,1},{3,0},{4,7},{5,6},{6,5},{7,4},{8,11},{9,10},{10,... | collective-permute-start | bytes 884744 | tf_op jit(solution)/shard_map/ppermute | solution.py:796
  41.1 18.6 %collective-permute-start.13 = (bf16[512,384]{1,0:T(8,128)(2,1)S(1)}, bf16[512,384]{1,0:T(8,128)(2,1)S(1)}, u32[]{:S(2)}, u32[]{:S(2)}) collective-permute-start(bf16[512,384]{1,0:T(8,128)(2,1)S(1)} %stack_pairs.1.refs_5_), channel_id=1, source_target_pairs={{0,4},{4,0},{8,12},{12,8},{16,20},{20,16},{24,28},{28,24},{1,5},{5... | collective-permute-start | bytes 1179656 | tf_op jit(solution)/shard_map/ppermute | solution.py:799
  45.0 14.8 %collective-permute-start.8 = (bf16[320,256]{1,0:T(8,128)(2,1)S(1)}, bf16[320,256]{1,0:T(8,128)(2,1)S(1)}, u32[]{:S(2)}, u32[]{:S(2)}) collective-permute-start(bf16[320,256]{1,0:T(8,128)(2,1)S(1)} %get-tuple-element.123), channel_id=1, source_target_pairs={{0,16},{4,20},{8,24},{12,28},{16,0},{20,4},{24,8},{28,12},{1,17},{... | collective-permute-start | bytes 491528 | tf_op jit(solution)/shard_map/ppermute | solution.py:799
  46.0 13.7 %collective-permute-start.9 = (bf16[320,256]{1,0:T(8,128)(2,1)S(1)}, bf16[320,256]{1,0:T(8,128)(2,1)S(1)}, u32[]{:S(2)}, u32[]{:S(2)}) collective-permute-start(bf16[320,256]{1,0:T(8,128)(2,1)S(1)} %get-tuple-element.124), channel_id=1, source_target_pairs={{0,24},{4,28},{8,16},{12,20},{16,8},{20,12},{24,0},{28,4},{1,25},{... | collective-permute-start | bytes 491528 | tf_op jit(solution)/shard_map/ppermute | solution.py:799
  50.5 31.3 %collective-permute-start.20 = (bf16[320,768]{1,0:T(8,128)(2,1)S(1)}, bf16[320,768]{1,0:T(8,128)(2,1)S(1)}, u32[]{:S(2)}, u32[]{:S(2)}) collective-permute-start(bf16[320,768]{1,0:T(8,128)(2,1)S(1)} %stack_extra.1.refs_10_.refs_3_.refs_4_), channel_id=1, source_target_pairs={{0,1},{1,0},{2,3},{3,2},{4,5},{5,4},{6,7},{7,6},{8,9},{9,8},{10,11... | collective-permute-start | bytes 1474568 | tf_op jit(solution)/shard_map/ppermute | solution.py:796
  53.2 28.7 %collective-permute-start.21 = (bf16[320,768]{1,0:T(8,128)(2,1)S(1)}, bf16[320,768]{1,0:T(8,128)(2,1)S(1)}, u32[]{:S(2)}, u32[]{:S(2)}) collective-permute-start(bf16[320,768]{1,0:T(8,128)(2,1)S(1)} %collective-permute-done.16.refs_11_.refs_12_.refs_5_), channel_id=1, source_target_pairs={{0,1},{1,0},{2,3},{3,2},{4,5},{5,4},{6,7},{7,6},{8,9},{9,8},{10,11... | collective-permute-start | bytes 1474568 | tf_op jit(solution)/shard_map/ppermute | solution.py:796
  91.4 17.7 %collective-permute-start.33 = (bf16[384,768]{1,0:T(8,128)(2,1)S(1)}, bf16[384,768]{1,0:T(8,128)(2,1)S(1)}, u32[]{:S(2)}, u32[]{:S(2)}) collective-permute-start(bf16[384,768]{1,0:T(8,128)(2,1)S(1)} %get-tuple-element.167), channel_id=1, source_target_pairs={{0,8},{4,12},{8,0},{12,4},{16,24},{20,28},{24,16},{28,20},{1,9},{5... | collective-permute-start | bytes 1769480 | tf_op jit(solution)/shard_map/ppermute | solution.py:799
  94.1 16.3 %collective-permute-start.31 = (bf16[384,768]{1,0:T(8,128)(2,1)S(1)}, bf16[384,768]{1,0:T(8,128)(2,1)S(1)}, u32[]{:S(2)}, u32[]{:S(2)}) collective-permute-start(bf16[384,768]{1,0:T(8,128)(2,1)S(1)} %get-tuple-element.159), channel_id=1, source_target_pairs={{0,4},{4,0},{8,12},{12,8},{16,20},{20,16},{24,28},{28,24},{1,5},{5... | collective-permute-start | bytes 1769480 | tf_op jit(solution)/shard_map/ppermute | solution.py:799
  134.2 14.2 %collective-permute-start.40 = (bf16[128,640]{1,0:T(8,128)(2,1)S(1)}, bf16[128,640]{1,0:T(8,128)(2,1)S(1)}, u32[]{:S(2)}, u32[]{:S(2)}) collective-permute-start(bf16[128,640]{1,0:T(8,128)(2,1)S(1)} %get-tuple-element.182), channel_id=1, source_target_pairs={{0,16},{4,20},{8,24},{12,28},{16,0},{20,4},{24,8},{28,12},{1,17},{... | collective-permute-start | bytes 491528 | tf_op jit(solution)/shard_map/ppermute | solution.py:799
  153.3 22.8 %collective-permute-start.47 = (bf16[512,640]{1,0:T(8,128)(2,1)S(1)}, bf16[512,640]{1,0:T(8,128)(2,1)S(1)}, u32[]{:S(2)}, u32[]{:S(2)}) collective-permute-start(bf16[512,640]{1,0:T(8,128)(2,1)S(1)} %get-tuple-element.195), channel_id=1, source_target_pairs={{0,4},{4,0},{8,12},{12,8},{16,20},{20,16},{24,28},{28,24},{1,5},{5... | collective-permute-start | bytes 1966088 | tf_op jit(solution)/shard_map/ppermute | solution.py:799
  161.6 18.3 %collective-permute-start.46 = (bf16[128,768]{1,0:T(8,128)(2,1)S(1)}, bf16[128,768]{1,0:T(8,128)(2,1)S(1)}, u32[]{:S(2)}, u32[]{:S(2)}) collective-permute-start(bf16[128,768]{1,0:T(8,128)(2,1)S(1)} %fusion), channel_id=1, source_target_pairs={{0,2},{1,3},{2,0},{3,1},{4,6},{5,7},{6,4},{7,5},{8,10},{9,11},{10,... | collective-permute-start | bytes 589832 | tf_op jit(solution)/shard_map/ppermute | solution.py:796
  162.2 16.7 %collective-permute-start.51 = (bf16[96,768]{1,0:T(8,128)(2,1)S(1)}, bf16[96,768]{1,0:T(8,128)(2,1)S(1)}, u32[]{:S(2)}, u32[]{:S(2)}) collective-permute-start(bf16[96,768]{1,0:T(8,128)(2,1)S(1)} %fc_turned.1.refs_6_.refs_1_), channel_id=1, source_target_pairs={{0,16},{4,20},{8,24},{12,28},{16,0},{20,4},{24,8},{28,12},{1,17},{... | collective-permute-start | bytes 442376 | tf_op jit(solution)/shard_map/ppermute | solution.py:799
  173.8 20.8 %collective-permute-start.57 = (bf16[192,768]{1,0:T(8,128)(2,1)S(1)}, bf16[192,768]{1,0:T(8,128)(2,1)S(1)}, u32[]{:S(2)}, u32[]{:S(2)}) collective-permute-start(bf16[192,768]{1,0:T(8,128)(2,1)S(1)} %out_double.1), channel_id=1, source_target_pairs={{0,8},{4,12},{8,0},{12,4},{16,24},{20,28},{24,16},{28,20},{1,9},{5... | collective-permute-start | bytes 884744 | tf_op jit(solution)/shard_map/ppermute | solution.py:799
  176.1 53.9 %collective-permute-start.23 = (f32[256,768]{1,0:T(8,128)}, f32[256,768]{1,0:T(8,128)}, u32[]{:S(2)}, u32[]{:S(2)}) collective-permute-start(f32[256,768]{1,0:T(8,128)} %get-tuple-element.140), channel_id=1, source_target_pairs={{0,1},{1,0},{2,3},{3,2},{4,5},{5,4},{6,7},{7,6},{8,9},{9,8},{10,11... | collective-permute-start | bytes 2359304 | tf_op jit(solution)/shard_map/ppermute | solution.py:796
  179.9 14.1 %collective-permute-start.50 = (bf16[128,640]{1,0:T(8,128)(2,1)S(1)}, bf16[128,640]{1,0:T(8,128)(2,1)S(1)}, u32[]{:S(2)}, u32[]{:S(2)}) collective-permute-start(bf16[128,640]{1,0:T(8,128)(2,1)S(1)} %get-tuple-element.199), channel_id=1, source_target_pairs={{0,24},{4,28},{8,16},{12,20},{16,8},{20,12},{24,0},{28,4},{1,25},{... | collective-permute-start | bytes 491528 | tf_op jit(solution)/shard_map/ppermute | solution.py:799
  195.2 33.9 %collective-permute-start.61 = (bf16[384,768]{1,0:T(8,128)(2,1)S(1)}, bf16[384,768]{1,0:T(8,128)(2,1)S(1)}, u32[]{:S(2)}, u32[]{:S(2)}) collective-permute-start(bf16[384,768]{1,0:T(8,128)(2,1)S(1)} %out_fourfold.1.refs_6_), channel_id=1, source_target_pairs={{0,4},{4,0},{8,12},{12,8},{16,20},{20,16},{24,28},{28,24},{1,5},{5... | collective-permute-start | bytes 1769480 | tf_op jit(solution)/shard_map/ppermute | solution.py:799
  195.3 26.2 %collective-permute-start.63 = (bf16[192,768]{1,0:T(8,128)(2,1)}, bf16[192,768]{1,0:T(8,128)(2,1)}, u32[]{:S(2)}, u32[]{:S(2)}) collective-permute-start(bf16[192,768]{1,0:T(8,128)(2,1)} %fc_double.1.refs_5_), channel_id=1, source_target_pairs={{0,4},{4,0},{8,12},{12,8},{16,20},{20,16},{24,28},{28,24},{1,5},{5... | collective-permute-start | bytes 884744 | tf_op jit(solution)/shard_map/ppermute | solution.py:799
  197.3 46.7 %all-to-all-start = ((f32[32,8,512]{2,1,0:T(8,128)}), f32[32,8,512]{2,1,0:T(8,128)S(1)}, u32[]{:S(2)}, u32[]{:S(2)}) async-start(f32[32,8,512]{2,1,0:T(8,128)} %get-tuple-element.191.refs_3_), calls=%async_computation | async-start | bytes 1048576 | tf_op jit(solution)/shard_map/all_to_all | solution.py:1156
  210.0 15.0 %collective-permute-start.58 = (bf16[128,640]{1,0:T(8,128)(2,1)S(1)}, bf16[128,640]{1,0:T(8,128)(2,1)S(1)}, u32[]{:S(2)}, u32[]{:S(2)}) collective-permute-start(bf16[128,640]{1,0:T(8,128)(2,1)S(1)} %attn_turned.1.refs_1_.refs_5_), channel_id=1, source_target_pairs={{0,8},{4,12},{8,0},{12,4},{16,24},{20,28},{24,16},{28,20},{1,9},{5... | collective-permute-start | bytes 491528 | tf_op jit(solution)/shard_map/ppermute | solution.py:799
  210.2 18.1 %collective-permute-start.59 = (bf16[128,640]{1,0:T(8,128)(2,1)S(1)}, bf16[128,640]{1,0:T(8,128)(2,1)S(1)}, u32[]{:S(2)}, u32[]{:S(2)}) collective-permute-start(bf16[128,640]{1,0:T(8,128)(2,1)S(1)} %attn_turned.1.refs_1_.refs_5_), channel_id=1, source_target_pairs={{0,16},{4,20},{8,24},{12,28},{16,0},{20,4},{24,8},{28,12},{1,17},{... | collective-permute-start | bytes 491528 | tf_op jit(solution)/shard_map/ppermute | solution.py:799
  225.0 16.4 %collective-permute-start.64 = (bf16[384,768]{1,0:T(8,128)(2,1)S(1)}, bf16[384,768]{1,0:T(8,128)(2,1)S(1)}, u32[]{:S(2)}, u32[]{:S(2)}) collective-permute-start(bf16[384,768]{1,0:T(8,128)(2,1)S(1)} %fc_fourfold.1), channel_id=1, source_target_pairs={{0,8},{4,12},{8,0},{12,4},{16,24},{20,28},{24,16},{28,20},{1,9},{5... | collective-permute-start | bytes 1769480 | tf_op jit(solution)/shard_map/ppermute | solution.py:799
  229.8 15.4 %collective-permute-start.62 = (bf16[512,640]{1,0:T(8,128)(2,1)S(1)}, bf16[512,640]{1,0:T(8,128)(2,1)}, u32[]{:S(2)}, u32[]{:S(2)}) collective-permute-start(bf16[512,640]{1,0:T(8,128)(2,1)S(1)} %attn_fourfold.1.refs_6_), channel_id=1, source_target_pairs={{0,4},{4,0},{8,12},{12,8},{16,20},{20,16},{24,28},{28,24},{1,5},{5... | collective-permute-start | bytes 1966088 | tf_op jit(solution)/shard_map/ppermute | solution.py:799
  (68 other events, 457.0 us)

commit v6 on v5

--- a/solution.py
+++ b/solution.py
@@ -1171,17 +1171,16 @@
         v.fc_weight_grad = fc_grad.transpose(1, 0, 2).reshape(width, parts * hidden).astype(F32)
 
     v.free = {
-        attn_pair, fc_final, fc_fourfold, fc_one, fc_two, out_double, out_final, out_partial, out_sum, place,
-        vector_final,
+        attn_pair, fc_final, fc_fourfold, fc_one, fc_two, out_double, out_final, out_partial, out_sum, vector_final,
     }
     v.hooks = {
         attend: lambda: [v.extra_across],
-        attn_fourfold: lambda: [v.out_pieces],
         attn_pair: lambda: [v.from_partners],
         fc_columns: lambda: [v.attn_core],
         fc_weights: lambda: [v.chip_low],
         middle: lambda: [v.normed_across],
         mixed: lambda: [v.fc_core],
+        normed_stack: lambda: [v.attn_core],
         out_partial: lambda: [v.queries],
         out_weights: lambda: [v.chip_low],
         place: lambda: [v.chip_low],
@@ -1191,7 +1190,7 @@
     if halved:
         order = (
             attn_columns, token_message, fc_columns, mixed, stack_pairs, join_fc, stack_extra, attend, normed_stack,
-            middle, fc_weights, out_weights, second_norm, attended_grad, fc_one, place, proj_weights, out_one,
+            middle, fc_weights, out_weights, second_norm, attended_grad, fc_one, proj_weights, place, out_one,
             attend_back, attn_weights, fc_two, out_two, fc_sum, merge, fc_turned, first_grad, attn_pair, out_sum,
             first_norm, out_double, fc_double, attn_fold, out_partial, out_fourfold, attn_turned, attn_fourfold,
             out_final, fc_fourfold, vector_final, fc_final, attn_final,

time: 249 us -> 249 us (level)
    ppermute x27, waiting for transfers between devices: 31.5 us -> 28.1 us  [over_fsdp(): return lax.ppermute(value, 'fsdp', [(i, i ^ k) for i in range(parts)])]
    ppermute x38, starting transfers between devices: 52.9 us -> 56.3 us  [over_ctx(): return lax.ppermute(value, 'ctx', [(i, i ^ k) for i in range(ways)])]
    ppermute x38, waiting for transfers between devices: 65.4 us -> 68.4 us  [over_ctx(): return lax.ppermute(value, 'ctx', [(i, i ^ k) for i in range(ways)])]
    unnamed x52 -> x32, local copies, waits for them, and re-layouts: 7.48 us -> 6.49 us
  transfers between devices with their start and end apart: 66 -> 66, of which waited for: 29 -> 27; matrix products, arithmetic and copies ran while one was open for 1% -> 1% of each run, Pallas kernels for 18% -> 19%
where the time goes in v6:
time: 249 us
  waiting for transfers between devices  96.5 us (39%)
  starting transfers between devices  75.8 us (30%)
  Pallas kernels  56.8 us (23%)
  blocking collectives  8.8 us (4%)
  local copies, waits for them, and re-layouts  6.51 us (3%)
  other arithmetic  3.07 us (1%)
    ppermute x38, waiting for transfers between devices, over_ctx(): return lax.ppermute(value, 'ctx', [(i, i ^ k) for i in range(ways)])  68.4 us
    pallas_call x41, Pallas kernels, call(): pl.pallas_call(run, name=name, out_shape=outs, in_specs=[smem] + [vmem] *...  56.8 us
    ppermute x38, starting transfers between devices, over_ctx(): return lax.ppermute(value, 'ctx', [(i, i ^ k) for i in range(ways)])  56.3 us
    ppermute x27, waiting for transfers between devices, over_fsdp(): return lax.ppermute(value, 'fsdp', [(i, i ^ k) for i in range(parts)])  28.1 us
    ppermute x27, starting transfers between devices, over_fsdp(): return lax.ppermute(value, 'fsdp', [(i, i ^ k) for i in range(parts)])  16.6 us
    all_gather x1, blocking collectives, middle(): attended_all = lax.all_gather(jnp.concatenate(v.att_pieces, 0), 'fsdp')  8.8 us
    unnamed x32, local copies, waits for them, and re-layouts  6.49 us
  transfers between devices with their start and end apart: 66, of which 27 were waited for; matrix products, arithmetic and copies ran while one was open for 1% of the time, Pallas kernels for 19%

profile of v6, /device:TPU:0, one launch (start us, length us, event | category | flops | bytes accessed | tf_op | source)
XLA Modules:
  0.0 248.7 jit_solution(2657691337177636530)
XLA Ops:
  14.4 5.1 %collective-permute-done.1.refs_5_.refs_8_ = bf16[136,768]{1,0:T(8,128)(2,1)S(1)} collective-permute-done((bf16[136,768]{1,0:T(8,128)(2,1)S(1)}, bf16[136,768]{1,0:T(8,128)(2,1)S(1)}, u32[]{:S(2)}, u32[]{:S(2)}) %collective-permute-start.1) | collective-permute-done | bytes 208928 | tf_op jit(solution)/shard_map/ppermute | solution.py:796
  30.8 6.9 %collective-permute-done.11.refs_3_.refs_7_ = bf16[128,384]{1,0:T(8,128)(2,1)S(1)} collective-permute-done((bf16[128,384]{1,0:T(8,128)(2,1)S(1)}, bf16[128,384]{1,0:T(8,128)(2,1)S(1)}, u32[]{:S(2)}, u32[]{:S(2)}) %collective-permute-start.11) | collective-permute-done | bytes 98336 | tf_op jit(solution)/shard_map/ppermute | solution.py:799
  47.5 3.1 %collective-permute-done.7.refs_2_.refs_4_ = bf16[320,256]{1,0:T(8,128)(2,1)S(1)} collective-permute-done((bf16[320,256]{1,0:T(8,128)(2,1)S(1)}, bf16[320,256]{1,0:T(8,128)(2,1)S(1)}, u32[]{:S(2)}, u32[]{:S(2)}) %collective-permute-start.7) | collective-permute-done | bytes 163872 | tf_op jit(solution)/shard_map/ppermute | solution.py:799
  53.2 6.5 %collective-permute-done.8.refs_3_.refs_5_ = bf16[320,256]{1,0:T(8,128)(2,1)S(1)} collective-permute-done((bf16[320,256]{1,0:T(8,128)(2,1)S(1)}, bf16[320,256]{1,0:T(8,128)(2,1)S(1)}, u32[]{:S(2)}, u32[]{:S(2)}) %collective-permute-start.8) | collective-permute-done | bytes 163872 | tf_op jit(solution)/shard_map/ppermute | solution.py:799
  59.7 5.3 %attend.1 = (bf16[192,128]{1,0:T(8,128)(2,1)S(1)}, bf16[192,128]{1,0:T(8,128)(2,1)S(1)}, bf16[192,128]{1,0:T(8,128)(2,1)S(1)}, bf16[192,128]{1,0:T(8,128)(2,1)S(...) custom-call(s32[4]{0:T(128)S(1)} %pad_add_fusion.refs_0_, ...), custom_call_target="tpu_custom_call" | custom-call | flops 1000 | bytes 1000 | tf_op jit(solution)/shard_map/attend/pallas_call | solution.py:35
  73.1 8.8 %all-gather = bf16[3072,128]{1,0:T(8,128)(2,1)S(1)} all-gather(bf16[768,128]{1,0:T(8,128)(2,1)S(1)} %pad_maximum_fusion), channel_id=2, replica_groups=mesh['ctx'=8,'fsdp'=4] {'fsdp'}, dimensions={0}, use_global_device_ids=true | all-gather | bytes 983040 | tf_op jit(solution)/shard_map/all_gather | solution.py:893
  81.9 4.9 %middle.1 = (f32[256,768]{1,0:T(8,128)S(1)}, f32[256,768]{1,0:T(8,128)S(1)}, f32[256,768]{1,0:T(8,128)S(1)}, bf16[512,768]{1,0:T(8,128)(2,1)S(1)}, bf16[512,768]...) custom-call(s32[4]{0:T(128)S(1)} %pad_add_fusion.refs_0_, ...), custom_call_target="tpu_custom_call" | custom-call | flops 1000 | bytes 1000 | tf_op jit(solution)/shard_map/middle/pallas_call | solution.py:35
  94.8 5.9 %collective-permute-done.26.refs_2_ = bf16[256,768]{1,0:T(8,128)(2,1)S(1)} collective-permute-done((bf16[256,768]{1,0:T(8,128)(2,1)S(1)}, bf16[256,768]{1,0:T(8,128)(2,1)S(1)}, u32[]{:S(2)}, u32[]{:S(2)}) %collective-permute-start.26) | collective-permute-done | bytes 393248 | tf_op jit(solution)/shard_map/ppermute | solution.py:796
  113.9 5.5 %attend_back.1 = (f32[512,384]{1,0:T(8,128)S(1)}, bf16[512,384]{1,0:T(8,128)(2,1)S(1)}, bf16[512,256]{1,0:T(8,128)(2,1)S(1)}, bf16[1024,384]{1,0:T(8,128)(2,1)S(1)}) custom-call(s32[4]{0:T(128)S(1)} %pad_add_fusion.refs_0_, bf16[128,256]{1,0:T(8,128)(2,1)S(1)} %get-tuple-element.151.refs_1_, bf16[128,256]{1,0:T(8,128)(2,1)S(1)} %collective-permute-done.28.refs_2_, ...), custom_call_target="tpu_custom_call" | custom-call | flops 1000 | bytes 1000 | tf_op jit(solution)/shard_map/attend_back/pallas_call | solution.py:35
  125.9 5.1 %collective-permute-done.38.refs_2_ = bf16[192,768]{1,0:T(8,128)(2,1)S(1)} collective-permute-done((bf16[192,768]{1,0:T(8,128)(2,1)S(1)}, bf16[192,768]{1,0:T(8,128)(2,1)S(1)}, u32[]{:S(2)}, u32[]{:S(2)}) %collective-permute-start.38) | collective-permute-done | bytes 294944 | tf_op jit(solution)/shard_map/ppermute | solution.py:799
  142.5 4.7 %collective-permute-done.40.refs_4_ = bf16[128,640]{1,0:T(8,128)(2,1)S(1)} collective-permute-done((bf16[128,640]{1,0:T(8,128)(2,1)S(1)}, bf16[128,640]{1,0:T(8,128)(2,1)S(1)}, u32[]{:S(2)}, u32[]{:S(2)}) %collective-permute-start.40) | collective-permute-done | bytes 163872 | tf_op jit(solution)/shard_map/ppermute | solution.py:799
  149.2 2.9 %collective-permute-start.55 = (bf16[96,768]{1,0:T(8,128)(2,1)S(1)}, bf16[96,768]{1,0:T(8,128)(2,1)S(1)}, u32[]{:S(2)}, u32[]{:S(2)}) collective-permute-start(bf16[96,768]{1,0:T(8,128)(2,1)S(1)} %get-tuple-element.178.refs_3_), channel_id=1, source_target_pairs={{0,16},{4,20},{8,24},{12,28},{16,0},{20,4},{24,8},{28,12},{1,17},{... | collective-permute-start | bytes 442376 | tf_op jit(solution)/shard_map/ppermute | solution.py:799
  154.3 5.3 %collective-permute-done.55.refs_2_ = bf16[96,768]{1,0:T(8,128)(2,1)S(1)} collective-permute-done((bf16[96,768]{1,0:T(8,128)(2,1)S(1)}, bf16[96,768]{1,0:T(8,128)(2,1)S(1)}, u32[]{:S(2)}, u32[]{:S(2)}) %collective-permute-start.55) | collective-permute-done | bytes 147488 | tf_op jit(solution)/shard_map/ppermute | solution.py:799
  160.9 2.9 %collective-permute-start.51 = (bf16[96,768]{1,0:T(8,128)(2,1)S(1)}, bf16[96,768]{1,0:T(8,128)(2,1)S(1)}, u32[]{:S(2)}, u32[]{:S(2)}) collective-permute-start(bf16[96,768]{1,0:T(8,128)(2,1)S(1)} %fc_turned.1.refs_6_.refs_1_), channel_id=1, source_target_pairs={{0,16},{4,20},{8,24},{12,28},{16,0},{20,4},{24,8},{28,12},{1,17},{... | collective-permute-start | bytes 442376 | tf_op jit(solution)/shard_map/ppermute | solution.py:799
  163.8 9.0 %collective-permute-done.56.refs_2_ = bf16[96,768]{1,0:T(8,128)(2,1)S(1)} collective-permute-done((bf16[96,768]{1,0:T(8,128)(2,1)S(1)}, bf16[96,768]{1,0:T(8,128)(2,1)S(1)}, u32[]{:S(2)}, u32[]{:S(2)}) %collective-permute-start.56) | collective-permute-done | bytes 147488 | tf_op jit(solution)/shard_map/ppermute | solution.py:799
  181.7 2.9 %all-to-all-start = ((f32[32,8,512]{2,1,0:T(8,128)}), f32[32,8,512]{2,1,0:T(8,128)S(1)}, u32[]{:S(2)}, u32[]{:S(2)}) async-start(f32[32,8,512]{2,1,0:T(8,128)} %get-tuple-element.191.refs_3_), calls=%async_computation | async-start | bytes 1048576 | tf_op jit(solution)/shard_map/all_to_all | solution.py:1156
  185.2 10.3 %collective-permute-done.48.refs_2_ = bf16[128,640]{1,0:T(8,128)(2,1)S(1)} collective-permute-done((bf16[128,640]{1,0:T(8,128)(2,1)}, bf16[128,640]{1,0:T(8,128)(2,1)S(1)}, u32[]{:S(2)}, u32[]{:S(2)}) %collective-permute-start.48) | collective-permute-done | bytes 163872 | tf_op jit(solution)/shard_map/ppermute | solution.py:799
  202.6 4.2 %collective-permute-start.58 = (bf16[128,640]{1,0:T(8,128)(2,1)S(1)}, bf16[128,640]{1,0:T(8,128)(2,1)S(1)}, u32[]{:S(2)}, u32[]{:S(2)}) collective-permute-start(bf16[128,640]{1,0:T(8,128)(2,1)S(1)} %attn_turned.1.refs_1_.refs_5_), channel_id=1, source_target_pairs={{0,8},{4,12},{8,0},{12,4},{16,24},{20,28},{24,16},{28,20},{1,9},{5... | collective-permute-start | bytes 491528 | tf_op jit(solution)/shard_map/ppermute | solution.py:799
  209.2 3.1 %collective-permute-done.58.refs_2_ = bf16[128,640]{1,0:T(8,128)(2,1)S(1)} collective-permute-done((bf16[128,640]{1,0:T(8,128)(2,1)S(1)}, bf16[128,640]{1,0:T(8,128)(2,1)S(1)}, u32[]{:S(2)}, u32[]{:S(2)}) %collective-permute-start.58) | collective-permute-done | bytes 163872 | tf_op jit(solution)/shard_map/ppermute | solution.py:799
  212.3 3.4 %collective-permute-start.64 = (bf16[384,768]{1,0:T(8,128)(2,1)S(1)}, bf16[384,768]{1,0:T(8,128)(2,1)S(1)}, u32[]{:S(2)}, u32[]{:S(2)}) collective-permute-start(bf16[384,768]{1,0:T(8,128)(2,1)S(1)} %out_fourfold.1.refs_6_), channel_id=1, source_target_pairs={{0,4},{4,0},{8,12},{12,8},{16,20},{20,16},{24,28},{28,24},{1,5},{5... | collective-permute-start | bytes 1769480 | tf_op jit(solution)/shard_map/ppermute | solution.py:799
  215.7 6.0 %collective-permute-done.59.refs_3_ = bf16[128,640]{1,0:T(8,128)(2,1)S(1)} collective-permute-done((bf16[128,640]{1,0:T(8,128)(2,1)S(1)}, bf16[128,640]{1,0:T(8,128)(2,1)S(1)}, u32[]{:S(2)}, u32[]{:S(2)}) %collective-permute-start.59) | collective-permute-done | bytes 163872 | tf_op jit(solution)/shard_map/ppermute | solution.py:799
  224.5 3.1 %collective-permute-start.63 = (bf16[384,768]{1,0:T(8,128)(2,1)S(1)}, bf16[384,768]{1,0:T(8,128)(2,1)S(1)}, u32[]{:S(2)}, u32[]{:S(2)}) collective-permute-start(bf16[384,768]{1,0:T(8,128)(2,1)S(1)} %fc_fourfold.1), channel_id=1, source_target_pairs={{0,8},{4,12},{8,0},{12,4},{16,24},{20,28},{24,16},{28,20},{1,9},{5... | collective-permute-start | bytes 1769480 | tf_op jit(solution)/shard_map/ppermute | solution.py:799
  230.1 4.3 %collective-permute-done.24 = bf16[128,768]{1,0:T(8,128)(2,1)S(1)} collective-permute-done((bf16[128,768]{1,0:T(8,128)(2,1)S(1)}, bf16[128,768]{1,0:T(8,128)(2,1)S(1)}, u32[]{:S(2)}, u32[]{:S(2)}) %collective-permute-start.24) | collective-permute-done | bytes 196640 | tf_op jit(solution)/shard_map/ppermute | solution.py:796
  238.3 4.4 %collective-permute-done.61.refs_5_ = bf16[512,640]{1,0:T(8,128)(2,1)S(1)} collective-permute-done((bf16[512,640]{1,0:T(8,128)(2,1)S(1)}, bf16[512,640]{1,0:T(8,128)(2,1)S(1)}, u32[]{:S(2)}, u32[]{:S(2)}) %collective-permute-start.61) | collective-permute-done | bytes 655392 | tf_op jit(solution)/shard_map/ppermute | solution.py:799
  (190 shorter events, 124.2 us)
Async XLA Ops:
  3.4 16.1 %collective-permute-start.4 = (bf16[192,640]{1,0:T(8,128)(2,1)S(1)}, bf16[192,640]{1,0:T(8,128)(2,1)S(1)}, u32[]{:S(2)}, u32[]{:S(2)}) collective-permute-start(bf16[192,640]{1,0:T(8,128)(2,1)S(1)} %get-tuple-element.118), channel_id=1, source_target_pairs={{0,2},{1,3},{2,0},{3,1},{4,6},{5,7},{6,4},{7,5},{8,10},{9,11},{10,... | collective-permute-start | bytes 737288 | tf_op jit(solution)/shard_map/ppermute | solution.py:796
  19.5 18.8 %collective-permute-start.14 = (bf16[192,768]{1,0:T(8,128)(2,1)S(1)}, bf16[192,768]{1,0:T(8,128)(2,1)S(1)}, u32[]{:S(2)}, u32[]{:S(2)}) collective-permute-start(bf16[192,768]{1,0:T(8,128)(2,1)S(1)} %get-tuple-element.130), channel_id=1, source_target_pairs={{0,2},{1,3},{2,0},{3,1},{4,6},{5,7},{6,4},{7,5},{8,10},{9,11},{10,... | collective-permute-start | bytes 884744 | tf_op jit(solution)/shard_map/ppermute | solution.py:796
  19.5 18.8 %collective-permute-start.15 = (bf16[192,768]{1,0:T(8,128)(2,1)S(1)}, bf16[192,768]{1,0:T(8,128)(2,1)S(1)}, u32[]{:S(2)}, u32[]{:S(2)}) collective-permute-start(bf16[192,768]{1,0:T(8,128)(2,1)S(1)} %get-tuple-element.119.refs_11_), channel_id=1, source_target_pairs={{0,3},{1,2},{2,1},{3,0},{4,7},{5,6},{6,5},{7,4},{8,11},{9,10},{10,... | collective-permute-start | bytes 884744 | tf_op jit(solution)/shard_map/ppermute | solution.py:796
  41.1 18.6 %collective-permute-start.13 = (bf16[512,384]{1,0:T(8,128)(2,1)S(1)}, bf16[512,384]{1,0:T(8,128)(2,1)S(1)}, u32[]{:S(2)}, u32[]{:S(2)}) collective-permute-start(bf16[512,384]{1,0:T(8,128)(2,1)S(1)} %stack_pairs.1.refs_5_), channel_id=1, source_target_pairs={{0,4},{4,0},{8,12},{12,8},{16,20},{20,16},{24,28},{28,24},{1,5},{5... | collective-permute-start | bytes 1179656 | tf_op jit(solution)/shard_map/ppermute | solution.py:799
  45.0 14.8 %collective-permute-start.8 = (bf16[320,256]{1,0:T(8,128)(2,1)S(1)}, bf16[320,256]{1,0:T(8,128)(2,1)S(1)}, u32[]{:S(2)}, u32[]{:S(2)}) collective-permute-start(bf16[320,256]{1,0:T(8,128)(2,1)S(1)} %get-tuple-element.123), channel_id=1, source_target_pairs={{0,16},{4,20},{8,24},{12,28},{16,0},{20,4},{24,8},{28,12},{1,17},{... | collective-permute-start | bytes 491528 | tf_op jit(solution)/shard_map/ppermute | solution.py:799
  50.5 31.3 %collective-permute-start.20 = (bf16[320,768]{1,0:T(8,128)(2,1)S(1)}, bf16[320,768]{1,0:T(8,128)(2,1)S(1)}, u32[]{:S(2)}, u32[]{:S(2)}) collective-permute-start(bf16[320,768]{1,0:T(8,128)(2,1)S(1)} %stack_extra.1.refs_10_.refs_3_.refs_4_), channel_id=1, source_target_pairs={{0,1},{1,0},{2,3},{3,2},{4,5},{5,4},{6,7},{7,6},{8,9},{9,8},{10,11... | collective-permute-start | bytes 1474568 | tf_op jit(solution)/shard_map/ppermute | solution.py:796
  53.2 28.7 %collective-permute-start.21 = (bf16[320,768]{1,0:T(8,128)(2,1)S(1)}, bf16[320,768]{1,0:T(8,128)(2,1)S(1)}, u32[]{:S(2)}, u32[]{:S(2)}) collective-permute-start(bf16[320,768]{1,0:T(8,128)(2,1)S(1)} %collective-permute-done.16.refs_11_.refs_12_.refs_5_), channel_id=1, source_target_pairs={{0,1},{1,0},{2,3},{3,2},{4,5},{5,4},{6,7},{7,6},{8,9},{9,8},{10,11... | collective-permute-start | bytes 1474568 | tf_op jit(solution)/shard_map/ppermute | solution.py:796
  91.4 16.2 %collective-permute-start.35 = (bf16[384,768]{1,0:T(8,128)(2,1)S(1)}, bf16[384,768]{1,0:T(8,128)(2,1)S(1)}, u32[]{:S(2)}, u32[]{:S(2)}) collective-permute-start(bf16[384,768]{1,0:T(8,128)(2,1)S(1)} %get-tuple-element.168), channel_id=1, source_target_pairs={{0,8},{4,12},{8,0},{12,4},{16,24},{20,28},{24,16},{28,20},{1,9},{5... | collective-permute-start | bytes 1769480 | tf_op jit(solution)/shard_map/ppermute | solution.py:799
  94.1 18.2 %collective-permute-start.31 = (bf16[384,768]{1,0:T(8,128)(2,1)S(1)}, bf16[384,768]{1,0:T(8,128)(2,1)S(1)}, u32[]{:S(2)}, u32[]{:S(2)}) collective-permute-start(bf16[384,768]{1,0:T(8,128)(2,1)S(1)} %get-tuple-element.159), channel_id=1, source_target_pairs={{0,4},{4,0},{8,12},{12,8},{16,20},{20,16},{24,28},{28,24},{1,5},{5... | collective-permute-start | bytes 1769480 | tf_op jit(solution)/shard_map/ppermute | solution.py:799
  148.7 25.4 %collective-permute-start.47 = (bf16[512,640]{1,0:T(8,128)(2,1)S(1)}, bf16[512,640]{1,0:T(8,128)(2,1)S(1)}, u32[]{:S(2)}, u32[]{:S(2)}) collective-permute-start(bf16[512,640]{1,0:T(8,128)(2,1)S(1)} %get-tuple-element.195), channel_id=1, source_target_pairs={{0,4},{4,0},{8,12},{12,8},{16,20},{20,16},{24,28},{28,24},{1,5},{5... | collective-permute-start | bytes 1966088 | tf_op jit(solution)/shard_map/ppermute | solution.py:799
  154.2 73.3 %collective-permute-start.23 = (f32[256,768]{1,0:T(8,128)}, f32[256,768]{1,0:T(8,128)}, u32[]{:S(2)}, u32[]{:S(2)}) collective-permute-start(f32[256,768]{1,0:T(8,128)} %get-tuple-element.140), channel_id=1, source_target_pairs={{0,1},{1,0},{2,3},{3,2},{4,5},{5,4},{6,7},{7,6},{8,9},{9,8},{10,11... | collective-permute-start | bytes 2359304 | tf_op jit(solution)/shard_map/ppermute | solution.py:796
  160.3 17.3 %collective-permute-start.46 = (bf16[128,768]{1,0:T(8,128)(2,1)S(1)}, bf16[128,768]{1,0:T(8,128)(2,1)S(1)}, u32[]{:S(2)}, u32[]{:S(2)}) collective-permute-start(bf16[128,768]{1,0:T(8,128)(2,1)S(1)} %fusion), channel_id=1, source_target_pairs={{0,2},{1,3},{2,0},{3,1},{4,6},{5,7},{6,4},{7,5},{8,10},{9,11},{10,... | collective-permute-start | bytes 589832 | tf_op jit(solution)/shard_map/ppermute | solution.py:796
  160.9 16.6 %collective-permute-start.51 = (bf16[96,768]{1,0:T(8,128)(2,1)S(1)}, bf16[96,768]{1,0:T(8,128)(2,1)S(1)}, u32[]{:S(2)}, u32[]{:S(2)}) collective-permute-start(bf16[96,768]{1,0:T(8,128)(2,1)S(1)} %fc_turned.1.refs_6_.refs_1_), channel_id=1, source_target_pairs={{0,16},{4,20},{8,24},{12,28},{16,0},{20,4},{24,8},{28,12},{1,17},{... | collective-permute-start | bytes 442376 | tf_op jit(solution)/shard_map/ppermute | solution.py:799
  174.1 24.5 %collective-permute-start.57 = (bf16[192,768]{1,0:T(8,128)(2,1)}, bf16[192,768]{1,0:T(8,128)(2,1)S(1)}, u32[]{:S(2)}, u32[]{:S(2)}) collective-permute-start(bf16[192,768]{1,0:T(8,128)(2,1)} %out_double.1), channel_id=1, source_target_pairs={{0,8},{4,12},{8,0},{12,4},{16,24},{20,28},{24,16},{28,20},{1,9},{5... | collective-permute-start | bytes 884744 | tf_op jit(solution)/shard_map/ppermute | solution.py:799
  175.5 20.0 %collective-permute-start.48 = (bf16[128,640]{1,0:T(8,128)(2,1)}, bf16[128,640]{1,0:T(8,128)(2,1)S(1)}, u32[]{:S(2)}, u32[]{:S(2)}) collective-permute-start(bf16[128,640]{1,0:T(8,128)(2,1)} %get-tuple-element.197), channel_id=1, source_target_pairs={{0,8},{4,12},{8,0},{12,4},{16,24},{20,28},{24,16},{28,20},{1,9},{5... | collective-permute-start | bytes 491528 | tf_op jit(solution)/shard_map/ppermute | solution.py:799
  177.5 18.0 %collective-permute-start.49 = (bf16[128,640]{1,0:T(8,128)(2,1)}, bf16[128,640]{1,0:T(8,128)(2,1)}, u32[]{:S(2)}, u32[]{:S(2)}) collective-permute-start(bf16[128,640]{1,0:T(8,128)(2,1)} %get-tuple-element.198), channel_id=1, source_target_pairs={{0,16},{4,20},{8,24},{12,28},{16,0},{20,4},{24,8},{28,12},{1,17},{... | collective-permute-start | bytes 491528 | tf_op jit(solution)/shard_map/ppermute | solution.py:799
  177.6 17.9 %collective-permute-start.50 = (bf16[128,640]{1,0:T(8,128)(2,1)}, bf16[128,640]{1,0:T(8,128)(2,1)}, u32[]{:S(2)}, u32[]{:S(2)}) collective-permute-start(bf16[128,640]{1,0:T(8,128)(2,1)} %get-tuple-element.199), channel_id=1, source_target_pairs={{0,24},{4,28},{8,16},{12,20},{16,8},{20,12},{24,0},{28,4},{1,25},{... | collective-permute-start | bytes 491528 | tf_op jit(solution)/shard_map/ppermute | solution.py:799
  181.7 65.8 %all-to-all-start = ((f32[32,8,512]{2,1,0:T(8,128)}), f32[32,8,512]{2,1,0:T(8,128)S(1)}, u32[]{:S(2)}, u32[]{:S(2)}) async-start(f32[32,8,512]{2,1,0:T(8,128)} %get-tuple-element.191.refs_3_), calls=%async_computation | async-start | bytes 1048576 | tf_op jit(solution)/shard_map/all_to_all | solution.py:1156
  195.5 28.4 %collective-permute-start.62 = (bf16[192,768]{1,0:T(8,128)(2,1)S(1)}, bf16[192,768]{1,0:T(8,128)(2,1)S(1)}, u32[]{:S(2)}, u32[]{:S(2)}) collective-permute-start(bf16[192,768]{1,0:T(8,128)(2,1)S(1)} %fc_double.1.refs_5_), channel_id=1, source_target_pairs={{0,4},{4,0},{8,12},{12,8},{16,20},{20,16},{24,28},{28,24},{1,5},{5... | collective-permute-start | bytes 884744 | tf_op jit(solution)/shard_map/ppermute | solution.py:799
  206.8 14.9 %collective-permute-start.59 = (bf16[128,640]{1,0:T(8,128)(2,1)S(1)}, bf16[128,640]{1,0:T(8,128)(2,1)S(1)}, u32[]{:S(2)}, u32[]{:S(2)}) collective-permute-start(bf16[128,640]{1,0:T(8,128)(2,1)S(1)} %attn_turned.1.refs_1_.refs_5_), channel_id=1, source_target_pairs={{0,16},{4,20},{8,24},{12,28},{16,0},{20,4},{24,8},{28,12},{1,17},{... | collective-permute-start | bytes 491528 | tf_op jit(solution)/shard_map/ppermute | solution.py:799
  206.8 14.9 %collective-permute-start.60 = (bf16[128,640]{1,0:T(8,128)(2,1)S(1)}, bf16[128,640]{1,0:T(8,128)(2,1)S(1)}, u32[]{:S(2)}, u32[]{:S(2)}) collective-permute-start(bf16[128,640]{1,0:T(8,128)(2,1)S(1)} %attn_turned.1.refs_1_.refs_5_), channel_id=1, source_target_pairs={{0,24},{4,28},{8,16},{12,20},{16,8},{20,12},{24,0},{28,4},{1,25},{... | collective-permute-start | bytes 491528 | tf_op jit(solution)/shard_map/ppermute | solution.py:799
  212.3 23.9 %collective-permute-start.64 = (bf16[384,768]{1,0:T(8,128)(2,1)S(1)}, bf16[384,768]{1,0:T(8,128)(2,1)S(1)}, u32[]{:S(2)}, u32[]{:S(2)}) collective-permute-start(bf16[384,768]{1,0:T(8,128)(2,1)S(1)} %out_fourfold.1.refs_6_), channel_id=1, source_target_pairs={{0,4},{4,0},{8,12},{12,8},{16,20},{20,16},{24,28},{28,24},{1,5},{5... | collective-permute-start | bytes 1769480 | tf_op jit(solution)/shard_map/ppermute | solution.py:799
  222.2 20.5 %collective-permute-start.61 = (bf16[512,640]{1,0:T(8,128)(2,1)S(1)}, bf16[512,640]{1,0:T(8,128)(2,1)S(1)}, u32[]{:S(2)}, u32[]{:S(2)}) collective-permute-start(bf16[512,640]{1,0:T(8,128)(2,1)S(1)} %attn_fourfold.1.refs_6_), channel_id=1, source_target_pairs={{0,4},{4,0},{8,12},{12,8},{16,20},{20,16},{24,28},{28,24},{1,5},{5... | collective-permute-start | bytes 1966088 | tf_op jit(solution)/shard_map/ppermute | solution.py:799
  224.5 20.8 %collective-permute-start.63 = (bf16[384,768]{1,0:T(8,128)(2,1)S(1)}, bf16[384,768]{1,0:T(8,128)(2,1)S(1)}, u32[]{:S(2)}, u32[]{:S(2)}) collective-permute-start(bf16[384,768]{1,0:T(8,128)(2,1)S(1)} %fc_fourfold.1), channel_id=1, source_target_pairs={{0,8},{4,12},{8,0},{12,4},{16,24},{20,28},{24,16},{28,20},{1,9},{5... | collective-permute-start | bytes 1769480 | tf_op jit(solution)/shard_map/ppermute | solution.py:799
  (58 other events, 407.1 us)
